TPU v7x, 256 devices: a whole 4x4x8 slice. The times are simulated.
256 devices in a mesh: wide: 32 (over z_hi, y, core), narrow: 8 (over z_lo, x).
Axes of the slice: x: 4, y: 4, z: 8 (z_hi: 4, z_lo: 2; z = z_hi * 2 + z_lo), core: 2. Of those that a mesh axis runs over, the one named last changes fastest.
Arguments:
- valence: float32 [8, 32768], P(None, ('wide', 'narrow')), may hold values from -6 to 6
- conduction: float32 [256, 32768], P(('wide', 'narrow')), may hold values from -6 to 6
- eps_val: float32 [8], replicated, may hold values from -12 to -2
- eps_cond: float32 [256], replicated, may hold values from 0.5 to 20
- omega: float32 [6], replicated, may hold values from 0.3 to 30
- gmap: int32 [8192], replicated, may hold values from 0 to 32767, as said below
Outputs:
- chi: float32 [6, 8192, 8192], P(None, 'wide', 'narrow')
Inputs may be any that keep to these rules, and one draw needn't show every extreme that they name: `gmap`: distinct grid indices: the 8192 grid points of smallest squared wave vector (frequencies folded to -16 .. 15), equal lengths in random order, listed by rising length.
All inputs are finite; a program needn't handle non-finite values.
Results may differ from a plain program's by a relative error of at most 0.0042.
Values may be sent and summed in bfloat16 or wider, within the bound.
No kernel may reach another device: no remote copies, remote signals or barrier semaphores. Data moves between devices by JAX's collectives and lax.ppermute only.
A program may use at most 128 MiB of HBM per device.

v0:
```python
import math

import jax
import jax.numpy as jnp
from jax import lax
from jax.sharding import Mesh
from jax.sharding import PartitionSpec as P

GRID = 32
WIDE_NARROW = ("wide_0", "wide_1", "wide_2", "narrow")
WIDE = ("wide_0", "wide_1", "wide_2")


def in_blocks(value, dim, peers):
    before, after = (value.shape[:dim], value.shape[dim + 1 :])
    return jnp.moveaxis(value.reshape(*before, peers, -1, *after), dim, 0)


def laid_out(blocks, dim):
    lengths = list(blocks.shape[1:])
    lengths[dim] *= blocks.shape[0]
    return jnp.moveaxis(blocks, 0, dim).reshape(lengths)


def exchange_in_order(blocks, axes, sequence):
    inside = blocks.shape[1:]
    whole = blocks.reshape(*(lax.axis_size(a) for a in axes), *inside)
    for k in sequence:
        whole = lax.all_to_all(whole, axes[k], k, k, tiled=True)
    return whole.reshape(-1, *inside)


def exchange_by_chip(value, groups, sequence, split_dim, concat_dim):
    peers = lax.axis_size(groups[0]) * lax.axis_size(groups[1])
    blocks = in_blocks(value, split_dim, peers)
    return laid_out(exchange_in_order(blocks, groups, sequence), concat_dim)


def sent_to_all(value, axis):
    copies = jnp.broadcast_to(value, (lax.axis_size(axis), *value.shape))
    return lax.all_to_all(copies, axis, split_axis=0, concat_axis=0, tiled=True)


def gathered_copies(value, axis, dim):
    blocks = sent_to_all(value, axis)
    return laid_out(blocks, dim)


def transform_axis(real_part, imag_part, form, cosine, sine_table):
    hp = lax.Precision.HIGHEST
    out_real = jnp.einsum(form, real_part, cosine, precision=hp)
    out_imag = -jnp.einsum(form, real_part, sine_table, precision=hp)
    if imag_part is not None:
        out_real = out_real + jnp.einsum(form, imag_part, sine_table, precision=hp)
        out_imag = out_imag + jnp.einsum(form, imag_part, cosine, precision=hp)
    return (out_real, out_imag)


def body(valence, conduction, eps_val, eps_cond, omega, gmap):
    full_valence = lax.all_gather(valence, WIDE_NARROW, axis=1, tiled=True)
    num_val = full_valence.shape[0]
    num_local = conduction.shape[0]
    count_local = num_local * num_val
    cube = full_valence.reshape(1, num_val, GRID, GRID, GRID)
    bands = conduction.reshape(num_local, 1, GRID, GRID, GRID)
    product = (bands * cube).reshape(count_local, GRID, GRID, GRID)
    points = jnp.arange(GRID, dtype=jnp.int32)
    phase = points[:, None] * points[None, :] % GRID
    angles = phase.astype(jnp.float32) * (2.0 * math.pi / GRID)
    cosine = jnp.cos(angles)
    sine_table = jnp.sin(angles)
    real_part, imag_part = transform_axis(product, None, "bxyz,zk->bxyk", cosine, sine_table)
    real_part, imag_part = transform_axis(real_part, imag_part, "bxyz,yk->bxkz", cosine, sine_table)
    real_part, imag_part = transform_axis(real_part, imag_part, "bxyz,xk->bkyz", cosine, sine_table)
    total_grid = GRID * GRID * GRID
    norm_factor = 1.0 / jnp.sqrt(jnp.float32(total_grid))
    real_part = jnp.take(real_part.reshape(count_local, total_grid), gmap, axis=1) * norm_factor
    imag_part = jnp.take(imag_part.reshape(count_local, total_grid), gmap, axis=1) * norm_factor
    local_pairs = jnp.stack([real_part, imag_part]).astype(jnp.bfloat16)
    num_pairs = num_val * eps_cond.shape[0]
    energy_gap = (eps_cond[:, None] - eps_val[None, :]).reshape(num_pairs)
    weights = -2.0 * energy_gap[None, :] / (energy_gap[None, :] ** 2 + omega[:, None] ** 2)
    weights = weights / jnp.sqrt(jnp.float32(num_pairs))
    columns = lax.all_to_all(local_pairs, "narrow", split_axis=2, concat_axis=1, tiled=True)
    wide_count = lax.axis_size(WIDE)
    narrow_count = lax.axis_size("narrow")
    row_width = gmap.shape[0] // wide_count
    regrouped = exchange_by_chip(local_pairs, (("wide_0", "wide_1"), "wide_2"), (1, 0), 2, 1)
    gathered = gathered_copies(regrouped, "narrow", 1)
    gathered = gathered.reshape(2, narrow_count, wide_count, count_local, row_width)
    row_panel = jnp.transpose(gathered, (0, 2, 1, 3, 4)).reshape(2, num_pairs, row_width)
    scaled = (row_panel.astype(jnp.float32)[None] * weights[:, None, :, None]).astype(jnp.bfloat16)
    return jnp.einsum(
        "wkpr,kpc->wrc",
        scaled,
        lax.all_gather(columns, WIDE, axis=1, tiled=True),
        preferred_element_type=jnp.float32,
    )


def solution(mesh):
    torus = Mesh(
        mesh.devices.reshape(4, 4, 2, mesh.shape["narrow"]),
        ("wide_0", "wide_1", "wide_2", "narrow"),
    )
    return jax.shard_map(
        body,
        mesh=torus,
        in_specs=(P(None, WIDE_NARROW), P(WIDE_NARROW, None), P(), P(), P(), P()),
        out_specs=P(None, WIDE, "narrow"),
        check_vma=False,
    )
```

profile of v0, /device:TPU:1, one launch (start us, length us, event | category | flops | bytes accessed | tf_op | source)
XLA Modules:
  0.0 885.1 jit_solution(3337144209313246540)
XLA Ops:
  6.5 0.7 all-gather.3.cloned.1.call-update
  7.3 0.0 all-gather.5.cloned.1.call-start
  7.3 0.5 broadcast.123
  7.8 1.9 reduce.3
  9.7 0.2 mul.142
  9.9 0.8 compare_and_fusion
  10.6 0.8 fusion.35
  11.4 531.4 %all-gather.3.cloned.1.call-done = f32[8,32768]{1,0:T(8,128)} async-done(((f32[8,128]{1,0:T(8,128)}), f32[8,32768]{1,0:T(8,128)}) %all-gather.3.cloned.1.call-update) | async-done | bytes 1048592 | tf_op jit(solution)/shard_map/all_gather | solution.py:60
  542.8 4.6 reshape.120
  547.4 5.8 fusion.18
  553.3 3.7 fusion.20
  557.0 4.1 fusion.42
  561.1 3.8 fusion.49
  564.9 3.9 add_bitcast_fusion.2
  568.8 6.1 fusion.6
  574.9 5.9 fusion.8
  580.8 3.9 add_bitcast_fusion.3
  584.7 6.9 add_bitcast_fusion.1
  591.7 7.0 add_bitcast_fusion
  598.7 10.8 %copy.100 = f32[8,32,32,32]{0,3,2,1:T(8,128)} copy(f32[8,32,32,32]{3,1,2,0:T(8,128)} %add_bitcast_fusion) | data formatting | bytes 2097152 | tf_op jit(solution)/shard_map/reshape | solution.py:78
  609.5 10.8 %copy.99 = f32[8,32,32,32]{0,3,2,1:T(8,128)} copy(f32[8,32,32,32]{3,1,2,0:T(8,128)} %add_bitcast_fusion.1) | data formatting | bytes 2097152 | tf_op jit(solution)/shard_map/reshape | solution.py:77
  620.3 33.6 %gather_fusion.1 = f32[8192,8]{1,0:T(8,128)} fusion(f32[8,32768]{0,1:T(8,128)} %bitcast.84, s32[8192]{0:T(1024)S(1)} %fusion.35), kind=kCustom, calls=%fused_computation.1.clone | custom fusion | bytes 557056 | tf_op jit(solution)/shard_map/jit(_take)/gather | solution.py:78
  653.9 33.7 %gather_fusion = f32[8192,8]{1,0:T(8,128)} fusion(f32[8,32768]{0,1:T(8,128)} %bitcast.83, s32[8192]{0:T(1024)S(1)} %fusion.35), kind=kCustom, calls=%fused_computation.clone | custom fusion | bytes 557056 | tf_op jit(solution)/shard_map/jit(_take)/gather | solution.py:77
  687.6 6.8 fusion.5
  694.4 0.9 pad_maximum_fusion
  695.3 0.4 copy-done.1
  695.8 35.6 %copy.117 = bf16[2,8,8192]{1,0,2:T(2,128)(2,1)} copy(bf16[2,8,8192]{1,2,0:T(8,128)(2,1)S(1)} %pad_maximum_fusion) | data formatting | bytes 524288 | tf_op jit(solution)/shard_map/stack | solution.py:79
  731.4 5.8 reshape.165
  737.2 8.5 all_to_all.33
  745.7 5.9 reshape.166
  751.6 10.2 %copy.91 = bf16[2,8,8,1024]{3,1,2,0:T(8,128)(2,1)} copy(bf16[2,8,8,1024]{1,0,3,2:T(2,128)(2,1)} %bitcast.90) | data formatting | bytes 524288 | tf_op jit(solution)/shard_map/all_to_all | solution.py:84
  761.8 0.0 all-gather.5.cloned.1.call-update
  761.8 1.8 copy.83
  763.7 0.8 copy.82
  764.5 5.6 all_to_all.34
  770.1 21.8 %all_to_all.35 = bf16[16,2,2,8,256]{4,3,1,2,0:T(8,128)(2,1)S(1)} all-to-all(bf16[16,2,2,8,256]{4,3,1,2,0:T(8,128)(2,1)S(1)} %copy.85), channel_id=1, replica_groups=mesh['wide_0'=4,'wide_1'=4,'wide_2'=2,'narrow'=8] {'wide_0','wide_1'}, dimensions={0} | all-to-all | bytes 524288 | tf_op jit(solution)/shard_map/all_to_all | solution.py:29
  791.9 1.5 broadcast_in_dim.11
  793.4 3.9 all-to-all-start.2
  797.3 0.1 subtract_multiply_fusion.1
  797.5 0.1 mul.150
  797.6 0.1 integer_pow.16
  797.7 0.1 divide_multiply_fusion
  797.8 51.9 %all-to-all-done.2 = bf16[8,2,256,256]{3,2,1,0:T(8,128)(2,1)S(1)} async-done(((bf16[8,2,256,256]{3,2,1,0:T(8,128)(2,1)}), bf16[8,2,256,256]{3,2,1,0:T(8,128)(2,1)S(1)}, u32[]{:S(2)}, u32[]{:S(2)}) %all-to-all-start.2) | async-done | bytes 2097184 | tf_op jit(solution)/shard_map/all_to_all | solution.py:41
  849.7 0.4 convert_bitcast_fusion
  850.2 2.6 copy.88
  852.8 5.5 copy.89
  858.2 0.9 all-gather.5.cloned.1.call-done
  859.2 18.6 %fusion.22 = f32[6,256,1024]{2,1,0:T(8,128)} fusion(bf16[2,2048,1024]{2,1,0:T(8,128)(2,1)} %all-gather.5.cloned.1.call-done, f32[6,2048]{1,0:T(8,128)S(1)} %divide_multiply_fusion, f32[2,2048,256]{1,2,0:T(8,128)} %copy.89), kind=kOutput, calls=%fused_computation.33 | convolution fusion | flops 12897484800 | bytes 18923520 | tf_op jit(solution)/shard_map/wkpr,kpc->wrc/dot_general | solution.py:93
  (15 shorter events, 0.1 us)
Async XLA Ops:
  6.5 536.3 %all-gather.3.cloned.1.call-start = ((), (), s32[]{:S(2)}) async-start(), calls=%async_computation.4 | async-start | bytes 1052672 | tf_op jit(solution)/shard_map/all_gather | solution.py:60
  7.3 851.9 %all-gather.5.cloned.1.call-start = ((), (), s32[]{:S(2)}) async-start(), calls=%async_computation.5 | async-start | bytes 8650752 | tf_op jit(solution)/shard_map/all_gather | solution.py:96
  547.4 5.8 copy-start
  694.4 1.4 copy-start.1
  770.1 27.2 %copy-start.4 = (f32[6]{0:T(128)S(1)}, f32[6]{0:T(128)}, u32[]{:S(2)}) copy-start(f32[6]{0:T(128)} %param.12) | copy-start | bytes 76
  770.1 27.3 %copy-start.2 = (f32[256]{0:T(256)S(1)}, f32[256]{0:T(256)}, u32[]{:S(2)}) copy-start(f32[256]{0:T(256)} %param.11) | copy-start | bytes 3076
  770.1 27.3 %copy-start.3 = (f32[8]{0:T(128)S(1)}, f32[8]{0:T(128)}, u32[]{:S(2)}) copy-start(f32[8]{0:T(128)} %param.10) | copy-start | bytes 100
  793.4 56.3 %all-to-all-start.2 = ((bf16[8,2,256,256]{3,2,1,0:T(8,128)(2,1)}), bf16[8,2,256,256]{3,2,1,0:T(8,128)(2,1)S(1)}, u32[]{:S(2)}, u32[]{:S(2)}) async-start(bf16[8,2,256,256]{3,2,1,0:T(8,128)(2,1)} %broadcast_in_dim.11), calls=%async_computation.2 | async-start | bytes 4194304 | tf_op jit(solution)/shard_map/all_to_all | solution.py:41
Sparse Core Ops, SparseCore 0:
  9.1 533.6 all-gather.2
  761.9 97.2 all-gather.4
where the time goes:
time: 900 us; the launch traced here: 885 us
  waiting for transfers between devices  585 us (65%)
  local copies, waits for them, and re-layouts  165 us (18%)
  matrix products  69.8 us (8%)
  blocking collectives  35.9 us (4%)
  between operations  14.1 us (2%)
  other arithmetic  11.8 us (1%)
    all_gather x1, waiting for transfers between devices, body(): full_valence = lax.all_gather(valence, WIDE_NARROW, axis=1, tiled=True)  531 us
    all_to_all x1, waiting for transfers between devices, sent_to_all(): return lax.all_to_all(copies, axis, split_axis=0, concat_axis=0, tiled=True)  51.9 us
    another operation x3, local copies, waits for them, and re-layouts, body(): local_pairs = jnp.stack([real_part, imag_part]).astype(jnp.bfloat16)  38.3 us
    gather x1, local copies, waits for them, and re-layouts, body(): jnp.take(real_part.reshape(count_local, total_grid), gmap, axis=1)  33.7 us
    gather x1, local copies, waits for them, and re-layouts, body(): jnp.take(imag_part.reshape(count_local, total_grid), gmap, axis=1)  33.6 us
    all_to_all x2, blocking collectives, exchange_in_order(): whole = lax.all_to_all(whole, axes[k], k, k, tiled=True)  27.3 us
    dot_general x1, matrix products, body(): jnp.einsum('wkpr,kpc->wrc', scaled, lax.all_gather(columns, WIDE, axis=1,...  18.6 us
  transfers between devices with their start and end apart: 3, of which 3 were waited for; matrix products, arithmetic and copies ran while one was open for 2% of the time, Pallas kernels for 0%

commit v1 on v0

v1 whole, which is shorter than its diff:
```python
import jax
import jax.numpy as jnp
import ml_dtypes
import numpy as np
from jax import lax
from jax.experimental import pallas as pl
from jax.experimental.pallas import tpu as pltpu
from jax.sharding import Mesh
from jax.sharding import PartitionSpec as P

GRID = 32
AXES = ("zh", "y", "co", "zl", "x")
WIDE = ("zh", "y", "co")
NARROW = ("zl", "x")
NPW = 8192
DISC = 256
NKX = 26
CAN = 640
BF = jnp.bfloat16
F32 = jnp.float32


def split_bf16(value):
    high = value.astype(BF)
    return high, (value - high.astype(value.dtype)).astype(BF)


def tables():
    k = np.arange(GRID)
    fold = np.where(k < GRID // 2, k, k - GRID)
    length = fold[:, None, None] ** 2 + fold[None, :, None] ** 2 + fold[None, None, :] ** 2
    ordered = np.sort(length.ravel())[:NPW]
    limit = ordered[-1]
    disc = []
    for ky in range(-15, 16):
        for kz in range(0, 16):
            if ky * ky + kz * kz <= limit and (kz > 0 or ky >= 0):
                disc.append((ky, kz))
    assert len(disc) <= DISC
    points = np.arange(GRID)
    wave = np.zeros((GRID, GRID, 2 * DISC))
    key = np.full((DISC, 1), -9000, np.int32)
    for m, (ky, kz) in enumerate(disc):
        angle = 2 * np.pi * ((ky * points[:, None] + kz * points[None, :]) % GRID) / GRID
        wave[:, :, m] = np.cos(angle)
        wave[:, :, DISC + m] = -np.sin(angle)
        key[m, 0] = ky * 64 + kz
    kx = np.arange(NKX) - 12
    assert limit < 13 * 13
    angle = 2 * np.pi * (kx[:, None] * points[None, :] % GRID) / GRID
    eye = np.eye(8)
    along = np.concatenate([np.kron(np.cos(angle), eye), np.kron(np.sin(angle), eye)])
    blocks = 8
    col_key = np.full((blocks, 1, CAN), -8000, np.int32)
    col_kx = np.zeros((blocks, 1, CAN), np.int32)
    col_id = np.full((blocks, CAN, 1), -(1 << 20), np.int32)
    size = NPW // blocks
    for j in range(blocks):
        low, high = ordered[j * size], ordered[(j + 1) * size - 1]
        n = 0
        for ky, kz in disc:
            for x in range(-12, 13):
                if (ky, kz) == (0, 0) and x < 0:
                    continue
                if low <= x * x + ky * ky + kz * kz <= high:
                    col_key[j, 0, n] = ky * 64 + kz
                    col_kx[j, 0, n] = x + 12
                    col_id[j, n, 0] = (x * 64 + ky) * 64 + kz
                    n += 1
        assert n <= CAN
    wave = wave.reshape(GRID * GRID, 2 * DISC).astype(np.float32)
    along = along.astype(np.float32)
    return split_np(wave) + split_np(along) + (key, col_key, col_kx, col_id)


def split_np(value):


    high = value.astype(ml_dtypes.bfloat16)
    low = (value - high.astype(np.float32)).astype(ml_dtypes.bfloat16)
    return high, low


def folded(index):
    def fold(k):
        return jnp.where(k < GRID // 2, k, k - GRID)

    return (
        fold(lax.shift_right_logical(index, 10)),
        fold(lax.shift_right_logical(index, 5) & 31),
        fold(index & 31),
    )


def dot(a, b):
    return jnp.dot(a, b, preferred_element_type=F32)


def transform_kernel(pos, own, other, cond, wave_hi, wave_lo, along_hi, along_lo, key, col_key, col_kx, gmap,
                     cols, rows, a_hi, a_lo, spectrum):
    zh, y, co, zl, x = (pos[i] for i in range(5))

    def product(q, carry):
        szh = (zh - q // 4) & 3
        sy = (y - q % 4) & 3
        band = cond[pl.ds(pl.multiple_of(q * 16, 16), 16), :]
        for n in range(8):
            szl = (zl - n // 4) & 1
            sx = (x - n % 4) & 3
            mine = own[sx, sy, szl, szh]
            theirs = other[sx, sy, szl, szh]
            first = jnp.where(co == 0, mine, theirs) * band[n : n + 1, :]
            second = jnp.where(co == 0, theirs, mine) * band[8 + n : 9 + n, :]
            high, low = split_bf16(jnp.concatenate([first, second], axis=0))
            at = pl.ds(pl.multiple_of(q * 16, 16), 16)
            a_hi[at, n * 128 : (n + 1) * 128] = high
            a_lo[at, n * 128 : (n + 1) * 128] = low
        return carry

    lax.fori_loop(0, 16, product, 0)
    field = dot(a_hi[...], wave_hi[...]) + (dot(a_lo[...], wave_hi[...]) + dot(a_hi[...], wave_lo[...]))
    f_hi, f_lo = split_bf16(field)
    full = dot(along_hi[...], f_hi) + (dot(along_lo[...], f_hi) + dot(along_hi[...], f_lo))
    half = NKX * 8
    norm = jnp.float32(1.0) / jnp.sqrt(jnp.float32(GRID**3))
    real = full[:half, :DISC] + full[half:, DISC:]
    imag = full[:half, DISC:] - full[half:, :DISC]
    spectrum[:half, :] = (real * norm).astype(BF)
    spectrum[half:, :] = (imag * norm).astype(BF)

    def picked(wanted, kx):
        hot = jnp.where(key[...] == wanted, jnp.float32(1), jnp.float32(0)).astype(BF)
        found = dot(spectrum[...], hot)
        real = jnp.zeros((8, wanted.shape[1]), F32)
        imag = jnp.zeros((8, wanted.shape[1]), F32)
        for i in range(NKX - 1):
            here = jnp.broadcast_to(kx == i, real.shape)
            real = jnp.where(here, found[i * 8 : i * 8 + 8], real)
            imag = jnp.where(here, found[half + i * 8 : half + i * 8 + 8], imag)
        return real, imag

    def columns(j, carry):
        real, imag = picked(col_key[j], col_kx[j])
        cols[j] = jnp.concatenate([real, imag], axis=0).astype(BF)
        return carry

    lax.fori_loop(0, 8, columns, 0)

    def row_blocks(r, carry):
        kx, ky, kz = folded(gmap[r])
        flip = jnp.where((kz < 0) | ((kz == 0) & (ky < 0)), -1, 1)
        real, imag = picked(flip * (ky * 64 + kz), flip * kx + 12)
        both = jnp.concatenate([real, imag * flip.astype(F32)], axis=0).astype(BF)
        rows[2 * r] = both[:, :256]
        rows[2 * r + 1] = both[:, 256:]
        return carry

    lax.fori_loop(0, 16, row_blocks, 0)


def transform(pos, own, other, cond, gmap):
    wave_hi, wave_lo, along_hi, along_lo, key, col_key, col_kx, _ = (jnp.asarray(t) for t in tables())
    vmem = pl.BlockSpec(memory_space=pltpu.VMEM)
    return pl.pallas_call(
        transform_kernel,
        grid_spec=pltpu.PrefetchScalarGridSpec(
            num_scalar_prefetch=1,
            grid=(),
            in_specs=[vmem] * 11,
            out_specs=[vmem, vmem],
            scratch_shapes=[
                pltpu.VMEM((256, 1024), BF),
                pltpu.VMEM((256, 1024), BF),
                pltpu.VMEM((2 * NKX * 8, DISC), BF),
            ],
        ),
        out_shape=[
            jax.ShapeDtypeStruct((8, 16, CAN), BF),
            jax.ShapeDtypeStruct((32, 16, 256), BF),
        ],
        compiler_params=pltpu.CompilerParams(vmem_limit_bytes=48 << 20),
        name="pair_transform",
    )(pos, own, other, cond, wave_hi, wave_lo, along_hi, along_lo, key, col_key, col_kx, gmap.reshape(16, 1, 512))


def product_body(pos, mine, theirs, row_refs, weights, gmap, ident, add, out, hot, cols, row_k, row_t, wgt):
    zh, y, co, zl, x = (pos[i] for i in range(5))
    w = pl.program_id(0)

    @pl.when(w == 0)
    def _():
        kx, ky, kz = folded(gmap[0])
        flip = jnp.where((kz < 0) | ((kz == 0) & ((ky < 0) | ((ky == 0) & (kx < 0)))), -1, 1)
        wanted = flip * ((kx * 64 + ky) * 64 + kz)
        hot[...] = jnp.where(ident[0] == wanted, jnp.float32(1), jnp.float32(0)).astype(BF)
        sign = jnp.concatenate([jnp.ones((8, 1024), F32), jnp.broadcast_to(flip.astype(F32), (8, 1024))], axis=0)
        for side, ref in enumerate((mine, theirs)):
            co_at = co if side == 0 else 1 - co
            for s in range(4):
                base = (side * 4 + s) * 128
                zh_at = (zh - s) & 3
                full = dot(ref[s].reshape(128, CAN), hot[...]).reshape(8, 16, 1024) * sign[None]
                cols[base : base + 128, :] = full.reshape(128, 1024).astype(BF)
                wgt[:, base : base + 128] = weights[zh_at, 0, co_at]
                for sx in range(4):
                    for szl in range(2):
                        n = (zl ^ szl) * 4 + ((x - sx) & 3)
                        row_k[pl.ds(pl.multiple_of(base + n * 16, 16), 16), :] = row_refs[sx][szl, zh_at, 0, co_at]
                row_t[:, base : base + 128] = row_k[base : base + 128, :].astype(F32).T

    scaled = (row_t[...] * wgt[pl.ds(w, 1), :]).astype(BF)
    part = dot(scaled, cols[...])
    out[0] = part if add is None else add[0] + part


def product_step(pos, sy, mine, theirs, rows, weights, gmap, ident, total):
    first = total is None

    def kernel(pos, *refs):
        mine, theirs, r0, r1, r2, r3, weights, gmap, ident = refs[:9]
        add = None if first else refs[9]
        product_body(pos, mine, theirs, (r0, r1, r2, r3), weights, gmap, ident, add, *refs[9 if first else 10 :])

    def y_at(pos):
        return (pos[1] - sy) & 3

    whole = lambda w, pos: (0, 0, 0, 0)
    row_spec = pl.BlockSpec((2, 4, 1, 2, 16, 256), lambda w, pos: (0, 0, y_at(pos), 0, 0, 0))
    acc_spec = pl.BlockSpec((1, 256, 1024), lambda w, pos: (w, 0, 0))
    col_spec = pl.BlockSpec((4, 8, 16, CAN), whole)
    in_specs = [
        col_spec,
        col_spec,
        row_spec,
        row_spec,
        row_spec,
        row_spec,
        pl.BlockSpec((4, 1, 2, 6, 128), lambda w, pos: (0, y_at(pos), 0, 0, 0)),
        pl.BlockSpec((1, 1, 1024), lambda w, pos: (pos[3] * 4 + pos[4], 0, 0)),
        pl.BlockSpec((1, CAN, 1), lambda w, pos: (pos[3] * 4 + pos[4], 0, 0)),
    ]
    operands = [mine, theirs, *rows, weights, gmap.reshape(8, 1, 1024), ident]
    if not first:
        in_specs.append(acc_spec)
        operands.append(total)
    return pl.pallas_call(
        kernel,
        grid_spec=pltpu.PrefetchScalarGridSpec(
            num_scalar_prefetch=1,
            grid=(6,),
            in_specs=in_specs,
            out_specs=acc_spec,
            scratch_shapes=[
                pltpu.VMEM((CAN, 1024), BF),
                pltpu.VMEM((1024, 1024), BF),
                pltpu.VMEM((1024, 256), BF),
                pltpu.VMEM((256, 1024), F32),
                pltpu.VMEM((6, 1024), F32),
            ],
        ),
        out_shape=jax.ShapeDtypeStruct((6, 256, 1024), F32),
        input_output_aliases={} if first else {10: 0},
        compiler_params=pltpu.CompilerParams(
            dimension_semantics=("arbitrary",), vmem_limit_bytes=48 << 20
        ),
        name="response_product",
    )(pos, *operands)


def shifted(value, axis, shift):
    size = lax.axis_size(axis)
    return lax.ppermute(value, axis, [(i, (i + shift) % size) for i in range(size)])


def around(value, axis):
    return [value] + [shifted(value, axis, s) for s in range(1, lax.axis_size(axis))]


def body(valence, conduction, eps_val, eps_cond, omega, gmap):
    pos = jnp.stack([lax.axis_index(a) for a in AXES]).astype(jnp.int32)
    own = valence
    for axis in ("zh", "zl", "y", "x"):
        own = jnp.stack(around(own, axis))
    other = shifted(own, "co", 1)
    cols, rows = transform(pos, own, other, conduction.reshape(256, 128), gmap)

    cols = lax.all_to_all(cols, NARROW, 0, 0, tiled=True)
    cols = jnp.stack(around(cols, "zh"))
    cols = around(cols, "y")
    rows = lax.all_to_all(rows, WIDE, 0, 0, tiled=True)
    rows = jnp.stack(around(rows, "zl")).reshape(2, 4, 4, 2, 16, 256)
    rows = around(rows, "x")

    num_pairs = eps_val.shape[0] * eps_cond.shape[0]
    energy_gap = (eps_cond[:, None] - eps_val[None, :]).reshape(num_pairs)
    weights = -2.0 * energy_gap[None, :] / (energy_gap[None, :] ** 2 + omega[:, None] ** 2)
    weights = weights / jnp.sqrt(jnp.float32(num_pairs))
    weights = jnp.broadcast_to(weights.reshape(6, 32, 8, 1, 8), (6, 32, 8, 2, 8))
    weights = jnp.transpose(weights.reshape(6, 32, 128), (1, 0, 2)).reshape(4, 4, 2, 6, 128)
    ident = jnp.asarray(tables()[-1])
    total = None
    for sy, mine in enumerate(cols):
        theirs = shifted(mine, "co", 1)
        total = product_step(pos, sy, mine, theirs, rows, weights, gmap, ident, total)
    return total


def solution(mesh):
    torus = Mesh(mesh.devices.reshape(4, 4, 2, 2, 4), AXES)
    return jax.shard_map(
        body,
        mesh=torus,
        in_specs=(P(None, AXES), P(AXES, None), P(), P(), P(), P()),
        out_specs=P(None, WIDE, NARROW),
        check_vma=False,
    )
```

time: 900 us -> 211 us (0.23); the launches traced: 885 us -> 209 us
  waiting for transfers between devices: 585 us -> 58.7 us
  local copies, waits for them, and re-layouts: 165 us -> 15.4 us
  matrix products: 69.8 us -> 0 us
  starting transfers between devices: 3.94 us -> 66.2 us
  Pallas kernels: 0 us -> 56.6 us
  blocking collectives: 35.9 us -> 9.6 us
  between operations: 14.1 us -> 0.14 us
  other arithmetic: 11.8 us -> 2 us
    all_gather x2 -> x0, waiting for transfers between devices: 532 us -> none  [the longest x1 531 us: body(): full_valence = lax.all_gather(valence, WIDE_NARROW, axis=1, tiled=True)]
    dot_general x11 -> x0, matrix products: 69.8 us -> none  [the longest x1 18.6 us: body(): jnp.einsum('wkpr,kpc->wrc', scaled, lax.all_gather(columns, WIDE, axis=1,...]
    gather x2 -> x0, local copies, waits for them, and re-layouts: 67.3 us -> none  [the longest x1 33.7 us: body(): jnp.take(real_part.reshape(count_local, total_grid), gmap, axis=1)]
    ppermute x0 -> x25, starting transfers between devices: none -> 57.2 us  [shifted(): lax.ppermute(value, axis, [(i, (i + shift) % size) for i in range(size)])]
    pallas_call x0 -> x5, Pallas kernels: none -> 56.6 us  [the longest x4 43.6 us: product_step(): pl.pallas_call(kernel, grid_spec=pltpu.PrefetchScalarGridSpec(num_scalar_...]
    ppermute x0 -> x25, waiting for transfers between devices: none -> 53.1 us  [shifted(): lax.ppermute(value, axis, [(i, (i + shift) % size) for i in range(size)])]
    all_to_all x1, waiting for transfers between devices: 51.9 us -> 5.57 us  [body(): rows = lax.all_to_all(rows, WIDE, 0, 0, tiled=True)]
    another operation x3 -> x1, local copies, waits for them, and re-layouts: 38.3 us -> 0.08 us  [body(): pos = jnp.stack([lax.axis_index(a) for a in AXES]).astype(jnp.int32)]
  transfers between devices with their start and end apart: 3 -> 26, of which waited for: 3 -> 15; matrix products, arithmetic and copies ran while one was open for 2% -> 2% of each run, Pallas kernels for 0% -> 15%
where the time goes in v1:
time: 211 us; the launch traced here: 209 us
  starting transfers between devices  66.2 us (31%)
  waiting for transfers between devices  58.7 us (28%)
  Pallas kernels  56.6 us (27%)
  local copies, waits for them, and re-layouts  15.4 us (7%)
  blocking collectives  9.6 us (5%)
    ppermute x25, starting transfers between devices, shifted(): lax.ppermute(value, axis, [(i, (i + shift) % size) for i in range(size)])  57.2 us
    ppermute x25, waiting for transfers between devices, shifted(): lax.ppermute(value, axis, [(i, (i + shift) % size) for i in range(size)])  53.1 us
    pallas_call x4, Pallas kernels, product_step(): pl.pallas_call(kernel, grid_spec=pltpu.PrefetchScalarGridSpec(num_scalar_...  43.6 us
    unnamed x42, local copies, waits for them, and re-layouts  13.2 us
    pallas_call x1, Pallas kernels, transform(): pl.pallas_call(transform_kernel, grid_spec=pltpu.PrefetchScalarGridSpec(n...  13 us
    all_to_all x1, blocking collectives, body(): cols = lax.all_to_all(cols, NARROW, 0, 0, tiled=True)  9.6 us
    all_to_all x1, starting transfers between devices, body(): rows = lax.all_to_all(rows, WIDE, 0, 0, tiled=True)  8.99 us
    all_to_all x1, waiting for transfers between devices, body(): rows = lax.all_to_all(rows, WIDE, 0, 0, tiled=True)  5.57 us
  transfers between devices with their start and end apart: 26, of which 15 were waited for; matrix products, arithmetic and copies ran while one was open for 2% of the time, Pallas kernels for 15%

profile of v1, /device:TPU:1, one launch (start us, length us, event | category | flops | bytes accessed | tf_op | source)
XLA Modules:
  0.0 208.7 jit_solution(419989052845534479)
XLA Ops:
  0.0 3.8 %collective-permute-start = (f32[8,128]{1,0:T(8,128)}, f32[8,128]{1,0:T(8,128)S(1)}, u32[]{:S(2)}, u32[]{:S(2)}) collective-permute-start(f32[8,128]{1,0:T(8,128)} %param.14), channel_id=1, source_target_pairs={{0,64},{64,128},{128,192},{192,0},{1,65},{65,129},{129,193},{193,1... | collective-permute-start | bytes 12296 | tf_op jit(solution)/shard_map/ppermute | solution.py:272
  3.8 5.1 %collective-permute-start.1 = (f32[8,128]{1,0:T(8,128)}, f32[8,128]{1,0:T(8,128)S(1)}, u32[]{:S(2)}, u32[]{:S(2)}) collective-permute-start(f32[8,128]{1,0:T(8,128)} %param.14), channel_id=1, source_target_pairs={{0,128},{64,192},{128,0},{192,64},{1,129},{65,193},{129,1},{193,65... | collective-permute-start | bytes 12296 | tf_op jit(solution)/shard_map/ppermute | solution.py:272
  8.9 2.4 %collective-permute-start.2 = (f32[8,128]{1,0:T(8,128)}, f32[8,128]{1,0:T(8,128)S(1)}, u32[]{:S(2)}, u32[]{:S(2)}) collective-permute-start(f32[8,128]{1,0:T(8,128)} %param.14), channel_id=1, source_target_pairs={{0,192},{64,0},{128,64},{192,128},{1,193},{65,1},{129,65},{193,129... | collective-permute-start | bytes 12296 | tf_op jit(solution)/shard_map/ppermute | solution.py:272
  11.3 1.2 collective-permute-done.2
  13.2 1.0 collective-permute-start.3
  14.2 1.6 collective-permute-done.3
  15.8 1.3 collective-permute-start.4
  17.1 2.6 %collective-permute-start.5 = (f32[2,4,8,128]{3,2,1,0:T(8,128)S(1)}, f32[2,4,8,128]{3,2,1,0:T(8,128)S(1)}, u32[]{:S(2)}, u32[]{:S(2)}) collective-permute-start(f32[2,4,8,128]{3,2,1,0:T(8,128)S(1)} %get-tuple-element.12), channel_id=1, source_target_pairs={{0,32},{16,48},{32,0},{48,16},{1,33},{17,49},{33,1},{49,17},{2,34}... | collective-permute-start | bytes 98312 | tf_op jit(solution)/shard_map/ppermute | solution.py:272
  19.7 1.1 collective-permute-start.6
  21.4 1.1 collective-permute-done.6
  22.5 1.3 collective-permute-start.7
  23.8 2.5 %collective-permute-start.8 = (f32[4,2,4,8,128]{4,3,2,1,0:T(8,128)S(1)}, f32[4,2,4,8,128]{4,3,2,1,0:T(8,128)S(1)}, u32[]{:S(2)}, u32[]{:S(2)}) collective-permute-start(f32[4,2,4,8,128]{4,3,2,1,0:T(8,128)S(1)} %get-tuple-element.10), channel_id=1, source_target_pairs={{0,2},{1,3},{2,0},{3,1},{4,6},{5,7},{6,4},{7,5},{8,10},{9,11},{10,... | collective-permute-start | bytes 393224 | tf_op jit(solution)/shard_map/ppermute | solution.py:272
  26.2 1.2 collective-permute-start.9
  27.6 2.4 %collective-permute-done.8 = f32[4,2,4,8,128]{4,3,2,1,0:T(8,128)S(1)} collective-permute-done((f32[4,2,4,8,128]{4,3,2,1,0:T(8,128)S(1)}, f32[4,2,4,8,128]{4,3,2,1,0:T(8,128)S(1)}, u32[]{:S(2)}, u32[]{:S(2)}) %collective-permute-start.8) | collective-permute-done | bytes 131104 | tf_op jit(solution)/shard_map/ppermute | solution.py:272
  30.1 7.0 %collective-permute-start.10 = (f32[4,4,2,4,8,128]{5,4,3,2,1,0:T(8,128)S(1)}, f32[4,4,2,4,8,128]{5,4,3,2,1,0:T(8,128)}, u32[]{:S(2)}, u32[]{:S(2)}) collective-permute-start(f32[4,4,2,4,8,128]{5,4,3,2,1,0:T(8,128)S(1)} %pad_maximum_fusion.1.own), channel_id=1, source_target_pairs={{0,8},{8,0},{1,9},{9,1},{2,10},{10,2},{3,11},{11,3},{4,12},{12,4},... | collective-permute-start | bytes 1572872 | tf_op jit(solution)/shard_map/ppermute | solution.py:272
  37.2 1.6 collective-permute-done.10.other
  38.8 1.2 copy-done.6
  40.0 1.2 copy-done.7
  43.0 0.9 copy-done.13
  47.2 13.0 %pair_transform.1 = (bf16[8,16,640]{2,1,0:T(8,128)(2,1)S(1)}, bf16[32,16,256]{2,1,0:T(8,128)(2,1)}) custom-call(s32[5]{0:T(128)S(1)} %stack.101.pos, f32[4,4,2,4,8,128]{5,4,3,2,1,0:T(8,128)S(1)} %pad_maximum_fusion.1.own, f32[4,4,2,4,8,128]{5,4,3,2,1,0:T(8,128)} %collective-permute-done.10.other, f32[256,128]{1,0:T(8,128)S(1)} %bitcast.44, ...), custom_call_target="tpu_custom_call" | custom-call | tf_op jit(solution)/shard_map/pair_transform/pallas_call | solution.py:164
  60.2 9.6 %all_to_all.10 = bf16[8,16,640]{2,1,0:T(8,128)(2,1)S(1)} all-to-all(bf16[8,16,640]{2,1,0:T(8,128)(2,1)S(1)} %get-tuple-element.7), channel_id=1, replica_groups=mesh['zh'=4,'y'=4,'co'=2,'zl'=2,'x'=4] {'zl','x'}, dimensions={0} | all-to-all | bytes 327680 | tf_op jit(solution)/shard_map/all_to_all | solution.py:287
  69.8 9.0 %all-to-all-start.1 = ((bf16[32,16,256]{2,1,0:T(8,128)(2,1)}), bf16[32,16,256]{2,1,0:T(8,128)(2,1)S(1)}, u32[]{:S(2)}, u32[]{:S(2)}) async-start(bf16[32,16,256]{2,1,0:T(8,128)(2,1)} %get-tuple-element.8), calls=%async_computation.1 | async-start | bytes 524288 | tf_op jit(solution)/shard_map/all_to_all | solution.py:290
  78.8 2.4 %collective-permute-start.11 = (bf16[8,16,640]{2,1,0:T(8,128)(2,1)S(1)}, bf16[8,16,640]{2,1,0:T(8,128)(2,1)S(1)}, u32[]{:S(2)}, u32[]{:S(2)}) collective-permute-start(bf16[8,16,640]{2,1,0:T(8,128)(2,1)S(1)} %all_to_all.10), channel_id=1, source_target_pairs={{0,64},{64,128},{128,192},{192,0},{1,65},{65,129},{129,193},{193,1... | collective-permute-start | bytes 491528 | tf_op jit(solution)/shard_map/ppermute | solution.py:272
  81.2 3.3 %collective-permute-start.12 = (bf16[8,16,640]{2,1,0:T(8,128)(2,1)S(1)}, bf16[8,16,640]{2,1,0:T(8,128)(2,1)S(1)}, u32[]{:S(2)}, u32[]{:S(2)}) collective-permute-start(bf16[8,16,640]{2,1,0:T(8,128)(2,1)S(1)} %all_to_all.10), channel_id=1, source_target_pairs={{0,128},{64,192},{128,0},{192,64},{1,129},{65,193},{129,1},{193,65... | collective-permute-start | bytes 491528 | tf_op jit(solution)/shard_map/ppermute | solution.py:272
  84.5 3.3 %collective-permute-start.13 = (bf16[8,16,640]{2,1,0:T(8,128)(2,1)S(1)}, bf16[8,16,640]{2,1,0:T(8,128)(2,1)}, u32[]{:S(2)}, u32[]{:S(2)}) collective-permute-start(bf16[8,16,640]{2,1,0:T(8,128)(2,1)S(1)} %all_to_all.10), channel_id=1, source_target_pairs={{0,192},{64,0},{128,64},{192,128},{1,193},{65,1},{129,65},{193,129... | collective-permute-start | bytes 491528 | tf_op jit(solution)/shard_map/ppermute | solution.py:272
  87.7 5.6 %all-to-all-done.1 = bf16[32,16,256]{2,1,0:T(8,128)(2,1)S(1)} async-done(((bf16[32,16,256]{2,1,0:T(8,128)(2,1)}), bf16[32,16,256]{2,1,0:T(8,128)(2,1)S(1)}, u32[]{:S(2)}, u32[]{:S(2)}) %all-to-all-start.1) | async-done | bytes 262176 | tf_op jit(solution)/shard_map/all_to_all | solution.py:290
  93.3 1.2 collective-permute-done.11
  94.5 8.0 %collective-permute-done.12 = bf16[8,16,640]{2,1,0:T(8,128)(2,1)S(1)} collective-permute-done((bf16[8,16,640]{2,1,0:T(8,128)(2,1)S(1)}, bf16[8,16,640]{2,1,0:T(8,128)(2,1)S(1)}, u32[]{:S(2)}, u32[]{:S(2)}) %collective-permute-start.12) | collective-permute-done | bytes 163872 | tf_op jit(solution)/shard_map/ppermute | solution.py:272
  102.5 1.0 pad_maximum_fusion.refs_0_
  103.5 1.6 collective-permute-start.22
  105.2 2.3 %collective-permute-start.20 = (bf16[4,8,16,640]{3,2,1,0:T(8,128)(2,1)S(1)}, bf16[4,8,16,640]{3,2,1,0:T(8,128)(2,1)}, u32[]{:S(2)}, u32[]{:S(2)}) collective-permute-start(bf16[4,8,16,640]{3,2,1,0:T(8,128)(2,1)S(1)} %pad_maximum_fusion.refs_0_), channel_id=1, source_target_pairs={{0,32},{16,48},{32,0},{48,16},{1,33},{17,49},{33,1},{49,17},{2,34}... | collective-permute-start | bytes 1966088 | tf_op jit(solution)/shard_map/ppermute | solution.py:272
  107.5 1.2 collective-permute-start.14
  108.7 3.0 %collective-permute-start.24 = (bf16[4,8,16,640]{3,2,1,0:T(8,128)(2,1)S(1)}, bf16[4,8,16,640]{3,2,1,0:T(8,128)(2,1)S(1)}, u32[]{:S(2)}, u32[]{:S(2)}) collective-permute-start(bf16[4,8,16,640]{3,2,1,0:T(8,128)(2,1)S(1)} %pad_maximum_fusion.refs_0_), channel_id=1, source_target_pairs={{0,8},{8,0},{1,9},{9,1},{2,10},{10,2},{3,11},{11,3},{4,12},{12,4},... | collective-permute-start | bytes 1966088 | tf_op jit(solution)/shard_map/ppermute | solution.py:272
  112.4 6.3 %collective-permute-done.22.refs_0_ = bf16[4,8,16,640]{3,2,1,0:T(8,128)(2,1)} collective-permute-done((bf16[4,8,16,640]{3,2,1,0:T(8,128)(2,1)S(1)}, bf16[4,8,16,640]{3,2,1,0:T(8,128)(2,1)}, u32[]{:S(2)}, u32[]{:S(2)}) %collective-permute-start.22) | collective-permute-done | bytes 655392 | tf_op jit(solution)/shard_map/ppermute | solution.py:272
  118.6 5.0 %collective-permute-start.23 = (bf16[4,8,16,640]{3,2,1,0:T(8,128)(2,1)}, bf16[4,8,16,640]{3,2,1,0:T(8,128)(2,1)}, u32[]{:S(2)}, u32[]{:S(2)}) collective-permute-start(bf16[4,8,16,640]{3,2,1,0:T(8,128)(2,1)} %collective-permute-done.22.refs_0_), channel_id=1, source_target_pairs={{0,8},{8,0},{1,9},{9,1},{2,10},{10,2},{3,11},{11,3},{4,12},{12,4},... | collective-permute-start | bytes 1966088 | tf_op jit(solution)/shard_map/ppermute | solution.py:272
  123.7 10.5 %collective-permute-done.20.refs_0_ = bf16[4,8,16,640]{3,2,1,0:T(8,128)(2,1)} collective-permute-done((bf16[4,8,16,640]{3,2,1,0:T(8,128)(2,1)S(1)}, bf16[4,8,16,640]{3,2,1,0:T(8,128)(2,1)}, u32[]{:S(2)}, u32[]{:S(2)}) %collective-permute-start.20) | collective-permute-done | bytes 655392 | tf_op jit(solution)/shard_map/ppermute | solution.py:272
  134.1 3.2 %collective-permute-start.21 = (bf16[4,8,16,640]{3,2,1,0:T(8,128)(2,1)}, bf16[4,8,16,640]{3,2,1,0:T(8,128)(2,1)}, u32[]{:S(2)}, u32[]{:S(2)}) collective-permute-start(bf16[4,8,16,640]{3,2,1,0:T(8,128)(2,1)} %collective-permute-done.20.refs_0_), channel_id=1, source_target_pairs={{0,8},{8,0},{1,9},{9,1},{2,10},{10,2},{3,11},{11,3},{4,12},{12,4},... | collective-permute-start | bytes 1966088 | tf_op jit(solution)/shard_map/ppermute | solution.py:272
  139.0 2.0 collective-permute-start.19
  142.1 1.2 copy.19
  143.3 9.4 %collective-permute-done.18.refs_4_ = bf16[2,4,4,2,16,256]{5,4,3,2,1,0:T(8,128)(2,1)} collective-permute-done((bf16[2,4,4,2,16,256]{5,4,3,2,1,0:T(8,128)(2,1)S(1)}, bf16[2,4,4,2,16,256]{5,4,3,2,1,0:T(8,128)(2,1)}, u32[]{:S(2)}, u32[]{:S(2)}) %collective-permute-start.18) | collective-permute-done | bytes 524320 | tf_op jit(solution)/shard_map/ppermute | solution.py:272
  152.7 9.1 %collective-permute-done.19.refs_5_ = bf16[2,4,4,2,16,256]{5,4,3,2,1,0:T(8,128)(2,1)} collective-permute-done((bf16[2,4,4,2,16,256]{5,4,3,2,1,0:T(8,128)(2,1)S(1)}, bf16[2,4,4,2,16,256]{5,4,3,2,1,0:T(8,128)(2,1)}, u32[]{:S(2)}, u32[]{:S(2)}) %collective-permute-start.19) | collective-permute-done | bytes 524320 | tf_op jit(solution)/shard_map/ppermute | solution.py:272
  161.9 1.0 copy-done.2
  162.9 1.1 copy-done.5
  164.0 1.1 copy-done.11
  165.1 9.3 %response_product.4.refs_9_ = f32[6,256,1024]{2,1,0:T(8,128)} custom-call(s32[5]{0:T(128)S(1)} %stack.101.pos, bf16[4,8,16,640]{3,2,1,0:T(8,128)(2,1)S(1)} %copy-done.5, bf16[4,8,16,640]{3,2,1,0:T(8,128)(2,1)S(1)} %copy-done.11, bf16[2,4,4,2,16,256]{5,4,3,2,1,0:T(8,128)(2,1)S(1)} %pad_maximum_fusion.2.refs_2_, bf16[2,4,4,2,16,256]{5,4,3,2,1,0:T(8,128)(2,1)S(1)} %copy-done.2, ...), custom_call_target="tpu_custom_call" | custom-call | tf_op jit(solution)/shard_map/response_product/pallas_call | solution.py:246
  174.4 11.4 %response_product.5.refs_9_ = f32[6,256,1024]{2,1,0:T(8,128)} custom-call(s32[5]{0:T(128)S(1)} %stack.101.pos, bf16[4,8,16,640]{3,2,1,0:T(8,128)(2,1)} %collective-permute-done.22.refs_0_, bf16[4,8,16,640]{3,2,1,0:T(8,128)(2,1)} %collective-permute-done.23.refs_1_, ...), custom_call_target="tpu_custom_call", output_to_operand_aliasing={{}: (10, {})} | custom-call | tf_op jit(solution)/shard_map/response_product/pallas_call | solution.py:246
  185.9 11.4 %response_product.6.refs_9_ = f32[6,256,1024]{2,1,0:T(8,128)} custom-call(s32[5]{0:T(128)S(1)} %stack.101.pos, bf16[4,8,16,640]{3,2,1,0:T(8,128)(2,1)} %collective-permute-done.20.refs_0_, bf16[4,8,16,640]{3,2,1,0:T(8,128)(2,1)} %collective-permute-done.21.refs_1_, ...), custom_call_target="tpu_custom_call", output_to_operand_aliasing={{}: (10, {})} | custom-call | tf_op jit(solution)/shard_map/response_product/pallas_call | solution.py:246
  197.3 11.4 %response_product.7 = f32[6,256,1024]{2,1,0:T(8,128)} custom-call(s32[5]{0:T(128)S(1)} %stack.101.pos, bf16[4,8,16,640]{3,2,1,0:T(8,128)(2,1)} %collective-permute-done.14.refs_0_, bf16[4,8,16,640]{3,2,1,0:T(8,128)(2,1)} %collective-permute-done.15.refs_1_, ...), custom_call_target="tpu_custom_call", output_to_operand_aliasing={{}: (10, {})} | custom-call | tf_op jit(solution)/shard_map/response_product/pallas_call | solution.py:246
  (66 shorter events, 10.2 us)
Async XLA Ops:
  0.0 161.9 %copy-start = (s32[8,640,1]{2,1,0:T(8,128)S(1)}, s32[8,640,1]{2,1,0:T(8,128)}, u32[]{:S(2)}) copy-start(s32[8,640,1]{2,1,0:T(8,128)} %constant.48.clone.refs_8_) | copy-start | bytes 61444
  0.0 11.3 %collective-permute-start = (f32[8,128]{1,0:T(8,128)}, f32[8,128]{1,0:T(8,128)S(1)}, u32[]{:S(2)}, u32[]{:S(2)}) collective-permute-start(f32[8,128]{1,0:T(8,128)} %param.14), channel_id=1, source_target_pairs={{0,64},{64,128},{128,192},{192,0},{1,65},{65,129},{129,193},{193,1... | collective-permute-start | bytes 12296 | tf_op jit(solution)/shard_map/ppermute | solution.py:272
  3.8 7.5 %collective-permute-start.1 = (f32[8,128]{1,0:T(8,128)}, f32[8,128]{1,0:T(8,128)S(1)}, u32[]{:S(2)}, u32[]{:S(2)}) collective-permute-start(f32[8,128]{1,0:T(8,128)} %param.14), channel_id=1, source_target_pairs={{0,128},{64,192},{128,0},{192,64},{1,129},{65,193},{129,1},{193,65... | collective-permute-start | bytes 12296 | tf_op jit(solution)/shard_map/ppermute | solution.py:272
  8.9 3.6 %collective-permute-start.2 = (f32[8,128]{1,0:T(8,128)}, f32[8,128]{1,0:T(8,128)S(1)}, u32[]{:S(2)}, u32[]{:S(2)}) collective-permute-start(f32[8,128]{1,0:T(8,128)} %param.14), channel_id=1, source_target_pairs={{0,192},{64,0},{128,64},{192,128},{1,193},{65,1},{129,65},{193,129... | collective-permute-start | bytes 12296 | tf_op jit(solution)/shard_map/ppermute | solution.py:272
  13.2 2.6 %collective-permute-start.3 = (f32[4,8,128]{2,1,0:T(8,128)S(1)}, f32[4,8,128]{2,1,0:T(8,128)S(1)}, u32[]{:S(2)}, u32[]{:S(2)}) collective-permute-start(f32[4,8,128]{2,1,0:T(8,128)S(1)} %get-tuple-element.14), channel_id=1, source_target_pairs={{0,4},{4,0},{1,5},{5,1},{2,6},{6,2},{3,7},{7,3},{8,12},{12,8},{9,1... | collective-permute-start | bytes 49160 | tf_op jit(solution)/shard_map/ppermute | solution.py:272
  15.8 5.0 %collective-permute-start.4 = (f32[2,4,8,128]{3,2,1,0:T(8,128)S(1)}, f32[2,4,8,128]{3,2,1,0:T(8,128)S(1)}, u32[]{:S(2)}, u32[]{:S(2)}) collective-permute-start(f32[2,4,8,128]{3,2,1,0:T(8,128)S(1)} %get-tuple-element.12), channel_id=1, source_target_pairs={{0,16},{16,32},{32,48},{48,0},{1,17},{17,33},{33,49},{49,1},{2,18}... | collective-permute-start | bytes 98312 | tf_op jit(solution)/shard_map/ppermute | solution.py:272
  17.1 4.3 %collective-permute-start.5 = (f32[2,4,8,128]{3,2,1,0:T(8,128)S(1)}, f32[2,4,8,128]{3,2,1,0:T(8,128)S(1)}, u32[]{:S(2)}, u32[]{:S(2)}) collective-permute-start(f32[2,4,8,128]{3,2,1,0:T(8,128)S(1)} %get-tuple-element.12), channel_id=1, source_target_pairs={{0,32},{16,48},{32,0},{48,16},{1,33},{17,49},{33,1},{49,17},{2,34}... | collective-permute-start | bytes 98312 | tf_op jit(solution)/shard_map/ppermute | solution.py:272
  19.7 2.8 %collective-permute-start.6 = (f32[2,4,8,128]{3,2,1,0:T(8,128)S(1)}, f32[2,4,8,128]{3,2,1,0:T(8,128)S(1)}, u32[]{:S(2)}, u32[]{:S(2)}) collective-permute-start(f32[2,4,8,128]{3,2,1,0:T(8,128)S(1)} %get-tuple-element.12), channel_id=1, source_target_pairs={{0,48},{16,0},{32,16},{48,32},{1,49},{17,1},{33,17},{49,33},{2,50}... | collective-permute-start | bytes 98312 | tf_op jit(solution)/shard_map/ppermute | solution.py:272
  22.5 5.1 %collective-permute-start.7 = (f32[4,2,4,8,128]{4,3,2,1,0:T(8,128)S(1)}, f32[4,2,4,8,128]{4,3,2,1,0:T(8,128)S(1)}, u32[]{:S(2)}, u32[]{:S(2)}) collective-permute-start(f32[4,2,4,8,128]{4,3,2,1,0:T(8,128)S(1)} %get-tuple-element.10), channel_id=1, source_target_pairs={{0,1},{1,2},{2,3},{3,0},{4,5},{5,6},{6,7},{7,4},{8,9},{9,10},{10,1... | collective-permute-start | bytes 393224 | tf_op jit(solution)/shard_map/ppermute | solution.py:272
  23.8 6.2 %collective-permute-start.8 = (f32[4,2,4,8,128]{4,3,2,1,0:T(8,128)S(1)}, f32[4,2,4,8,128]{4,3,2,1,0:T(8,128)S(1)}, u32[]{:S(2)}, u32[]{:S(2)}) collective-permute-start(f32[4,2,4,8,128]{4,3,2,1,0:T(8,128)S(1)} %get-tuple-element.10), channel_id=1, source_target_pairs={{0,2},{1,3},{2,0},{3,1},{4,6},{5,7},{6,4},{7,5},{8,10},{9,11},{10,... | collective-permute-start | bytes 393224 | tf_op jit(solution)/shard_map/ppermute | solution.py:272
  26.2 3.8 %collective-permute-start.9 = (f32[4,2,4,8,128]{4,3,2,1,0:T(8,128)S(1)}, f32[4,2,4,8,128]{4,3,2,1,0:T(8,128)S(1)}, u32[]{:S(2)}, u32[]{:S(2)}) collective-permute-start(f32[4,2,4,8,128]{4,3,2,1,0:T(8,128)S(1)} %get-tuple-element.10), channel_id=1, source_target_pairs={{0,3},{1,0},{2,1},{3,2},{4,7},{5,4},{6,5},{7,6},{8,11},{9,8},{10,9... | collective-permute-start | bytes 393224 | tf_op jit(solution)/shard_map/ppermute | solution.py:272
  30.1 8.7 %collective-permute-start.10 = (f32[4,4,2,4,8,128]{5,4,3,2,1,0:T(8,128)S(1)}, f32[4,4,2,4,8,128]{5,4,3,2,1,0:T(8,128)}, u32[]{:S(2)}, u32[]{:S(2)}) collective-permute-start(f32[4,4,2,4,8,128]{5,4,3,2,1,0:T(8,128)S(1)} %pad_maximum_fusion.1.own), channel_id=1, source_target_pairs={{0,8},{8,0},{1,9},{9,1},{2,10},{10,2},{3,11},{11,3},{4,12},{12,4},... | collective-permute-start | bytes 1572872 | tf_op jit(solution)/shard_map/ppermute | solution.py:272
  38.8 1.2 copy-start.6
  40.0 1.2 copy-start.7
  41.3 0.8 copy-start.8
  42.0 0.9 copy-start.12
  43.0 0.9 copy-start.13
  43.9 0.9 copy-start.14
  44.8 0.9 copy-start.15
  45.7 0.7 copy-start.16
  46.4 0.7 copy-start.17
  47.2 93.8 %copy-start.18 = (f32[256]{0:T(256)S(1)}, f32[256]{0:T(256)}, u32[]{:S(2)}) copy-start(f32[256]{0:T(256)} %param.17) | copy-start | bytes 3076
  47.2 94.0 %copy-start.20 = (f32[6]{0:T(128)S(1)}, f32[6]{0:T(128)}, u32[]{:S(2)}) copy-start(f32[6]{0:T(128)} %param.18) | copy-start | bytes 76
  47.2 94.0 %copy-start.19 = (f32[8]{0:T(128)S(1)}, f32[8]{0:T(128)}, u32[]{:S(2)}) copy-start(f32[8]{0:T(128)} %param.16) | copy-start | bytes 100
  47.2 114.7 %copy-start.9 = (s32[8192]{0:T(1024)S(1)}, s32[8192]{0:T(1024)}, u32[]{:S(2)}) copy-start(s32[8192]{0:T(1024)} %param.19) | copy-start | bytes 98308
  69.8 23.5 %all-to-all-start.1 = ((bf16[32,16,256]{2,1,0:T(8,128)(2,1)}), bf16[32,16,256]{2,1,0:T(8,128)(2,1)S(1)}, u32[]{:S(2)}, u32[]{:S(2)}) async-start(bf16[32,16,256]{2,1,0:T(8,128)(2,1)} %get-tuple-element.8), calls=%async_computation.1 | async-start | bytes 524288 | tf_op jit(solution)/shard_map/all_to_all | solution.py:290
  78.8 15.7 %collective-permute-start.11 = (bf16[8,16,640]{2,1,0:T(8,128)(2,1)S(1)}, bf16[8,16,640]{2,1,0:T(8,128)(2,1)S(1)}, u32[]{:S(2)}, u32[]{:S(2)}) collective-permute-start(bf16[8,16,640]{2,1,0:T(8,128)(2,1)S(1)} %all_to_all.10), channel_id=1, source_target_pairs={{0,64},{64,128},{128,192},{192,0},{1,65},{65,129},{129,193},{193,1... | collective-permute-start | bytes 491528 | tf_op jit(solution)/shard_map/ppermute | solution.py:272
  81.2 21.3 %collective-permute-start.12 = (bf16[8,16,640]{2,1,0:T(8,128)(2,1)S(1)}, bf16[8,16,640]{2,1,0:T(8,128)(2,1)S(1)}, u32[]{:S(2)}, u32[]{:S(2)}) collective-permute-start(bf16[8,16,640]{2,1,0:T(8,128)(2,1)S(1)} %all_to_all.10), channel_id=1, source_target_pairs={{0,128},{64,192},{128,0},{192,64},{1,129},{65,193},{129,1},{193,65... | collective-permute-start | bytes 491528 | tf_op jit(solution)/shard_map/ppermute | solution.py:272
  84.5 18.0 %collective-permute-start.13 = (bf16[8,16,640]{2,1,0:T(8,128)(2,1)S(1)}, bf16[8,16,640]{2,1,0:T(8,128)(2,1)}, u32[]{:S(2)}, u32[]{:S(2)}) collective-permute-start(bf16[8,16,640]{2,1,0:T(8,128)(2,1)S(1)} %all_to_all.10), channel_id=1, source_target_pairs={{0,192},{64,0},{128,64},{192,128},{1,193},{65,1},{129,65},{193,129... | collective-permute-start | bytes 491528 | tf_op jit(solution)/shard_map/ppermute | solution.py:272
  93.3 18.4 %collective-permute-start.16 = (bf16[32,16,256]{2,1,0:T(8,128)(2,1)S(1)}, bf16[32,16,256]{2,1,0:T(8,128)(2,1)S(1)}, u32[]{:S(2)}, u32[]{:S(2)}) collective-permute-start(bf16[32,16,256]{2,1,0:T(8,128)(2,1)S(1)} %all-to-all-done.1), channel_id=1, source_target_pairs={{0,4},{4,0},{1,5},{5,1},{2,6},{6,2},{3,7},{7,3},{8,12},{12,8},{9,1... | collective-permute-start | bytes 786440 | tf_op jit(solution)/shard_map/ppermute | solution.py:272
  103.5 34.6 %copy-start.4 = (bf16[4,8,16,640]{3,2,1,0:T(8,128)(2,1)}, bf16[4,8,16,640]{3,2,1,0:T(8,128)(2,1)S(1)}, u32[]{:S(2)}) copy-start(bf16[4,8,16,640]{3,2,1,0:T(8,128)(2,1)S(1)} %pad_maximum_fusion.refs_0_) | copy-start | bytes 1966084
  103.5 15.1 %collective-permute-start.22 = (bf16[4,8,16,640]{3,2,1,0:T(8,128)(2,1)S(1)}, bf16[4,8,16,640]{3,2,1,0:T(8,128)(2,1)}, u32[]{:S(2)}, u32[]{:S(2)}) collective-permute-start(bf16[4,8,16,640]{3,2,1,0:T(8,128)(2,1)S(1)} %pad_maximum_fusion.refs_0_), channel_id=1, source_target_pairs={{0,16},{16,32},{32,48},{48,0},{1,17},{17,33},{33,49},{49,1},{2,18}... | collective-permute-start | bytes 1966088 | tf_op jit(solution)/shard_map/ppermute | solution.py:272
  105.2 29.0 %collective-permute-start.20 = (bf16[4,8,16,640]{3,2,1,0:T(8,128)(2,1)S(1)}, bf16[4,8,16,640]{3,2,1,0:T(8,128)(2,1)}, u32[]{:S(2)}, u32[]{:S(2)}) collective-permute-start(bf16[4,8,16,640]{3,2,1,0:T(8,128)(2,1)S(1)} %pad_maximum_fusion.refs_0_), channel_id=1, source_target_pairs={{0,32},{16,48},{32,0},{48,16},{1,33},{17,49},{33,1},{49,17},{2,34}... | collective-permute-start | bytes 1966088 | tf_op jit(solution)/shard_map/ppermute | solution.py:272
  107.5 29.8 %collective-permute-start.14 = (bf16[4,8,16,640]{3,2,1,0:T(8,128)(2,1)S(1)}, bf16[4,8,16,640]{3,2,1,0:T(8,128)(2,1)}, u32[]{:S(2)}, u32[]{:S(2)}) collective-permute-start(bf16[4,8,16,640]{3,2,1,0:T(8,128)(2,1)S(1)} %pad_maximum_fusion.refs_0_), channel_id=1, source_target_pairs={{0,48},{16,0},{32,16},{48,32},{1,49},{17,1},{33,17},{49,33},{2,50}... | collective-permute-start | bytes 1966088 | tf_op jit(solution)/shard_map/ppermute | solution.py:272
  108.7 28.6 %collective-permute-start.24 = (bf16[4,8,16,640]{3,2,1,0:T(8,128)(2,1)S(1)}, bf16[4,8,16,640]{3,2,1,0:T(8,128)(2,1)S(1)}, u32[]{:S(2)}, u32[]{:S(2)}) collective-permute-start(bf16[4,8,16,640]{3,2,1,0:T(8,128)(2,1)S(1)} %pad_maximum_fusion.refs_0_), channel_id=1, source_target_pairs={{0,8},{8,0},{1,9},{9,1},{2,10},{10,2},{3,11},{11,3},{4,12},{12,4},... | collective-permute-start | bytes 1966088 | tf_op jit(solution)/shard_map/ppermute | solution.py:272
  111.7 26.4 %collective-permute-start.17 = (bf16[2,4,4,2,16,256]{5,4,3,2,1,0:T(8,128)(2,1)S(1)}, bf16[2,4,4,2,16,256]{5,4,3,2,1,0:T(8,128)(2,1)S(1)}, u32[]{:S(2)}, u32[]{:S(2)}) collective-permute-start(bf16[2,4,4,2,16,256]{5,4,3,2,1,0:T(8,128)(2,1)S(1)} %pad_maximum_fusion.2.refs_2_), channel_id=1, source_target_pairs={{0,1},{1,2},{2,3},{3,0},{4,5},{5,6},{6,7},{7,4},{8,9},{9,10},{10,1... | collective-permute-start | bytes 1572872 | tf_op jit(solution)/shard_map/ppermute | solution.py:272
  118.6 55.8 %collective-permute-start.23 = (bf16[4,8,16,640]{3,2,1,0:T(8,128)(2,1)}, bf16[4,8,16,640]{3,2,1,0:T(8,128)(2,1)}, u32[]{:S(2)}, u32[]{:S(2)}) collective-permute-start(bf16[4,8,16,640]{3,2,1,0:T(8,128)(2,1)} %collective-permute-done.22.refs_0_), channel_id=1, source_target_pairs={{0,8},{8,0},{1,9},{9,1},{2,10},{10,2},{3,11},{11,3},{4,12},{12,4},... | collective-permute-start | bytes 1966088 | tf_op jit(solution)/shard_map/ppermute | solution.py:272
  134.1 51.7 %collective-permute-start.21 = (bf16[4,8,16,640]{3,2,1,0:T(8,128)(2,1)}, bf16[4,8,16,640]{3,2,1,0:T(8,128)(2,1)}, u32[]{:S(2)}, u32[]{:S(2)}) collective-permute-start(bf16[4,8,16,640]{3,2,1,0:T(8,128)(2,1)} %collective-permute-done.20.refs_0_), channel_id=1, source_target_pairs={{0,8},{8,0},{1,9},{9,1},{2,10},{10,2},{3,11},{11,3},{4,12},{12,4},... | collective-permute-start | bytes 1966088 | tf_op jit(solution)/shard_map/ppermute | solution.py:272
  137.3 60.0 %collective-permute-start.15 = (bf16[4,8,16,640]{3,2,1,0:T(8,128)(2,1)}, bf16[4,8,16,640]{3,2,1,0:T(8,128)(2,1)}, u32[]{:S(2)}, u32[]{:S(2)}) collective-permute-start(bf16[4,8,16,640]{3,2,1,0:T(8,128)(2,1)} %collective-permute-done.14.refs_0_), channel_id=1, source_target_pairs={{0,8},{8,0},{1,9},{9,1},{2,10},{10,2},{3,11},{11,3},{4,12},{12,4},... | collective-permute-start | bytes 1966088 | tf_op jit(solution)/shard_map/ppermute | solution.py:272
  137.3 0.8 copy-start.10
  138.2 14.6 %collective-permute-start.18 = (bf16[2,4,4,2,16,256]{5,4,3,2,1,0:T(8,128)(2,1)S(1)}, bf16[2,4,4,2,16,256]{5,4,3,2,1,0:T(8,128)(2,1)}, u32[]{:S(2)}, u32[]{:S(2)}) collective-permute-start(bf16[2,4,4,2,16,256]{5,4,3,2,1,0:T(8,128)(2,1)S(1)} %pad_maximum_fusion.2.refs_2_), channel_id=1, source_target_pairs={{0,2},{1,3},{2,0},{3,1},{4,6},{5,7},{6,4},{7,5},{8,10},{9,11},{10,... | collective-permute-start | bytes 1572872 | tf_op jit(solution)/shard_map/ppermute | solution.py:272
  138.2 0.8 copy-start.1
  139.0 22.9 %collective-permute-start.19 = (bf16[2,4,4,2,16,256]{5,4,3,2,1,0:T(8,128)(2,1)S(1)}, bf16[2,4,4,2,16,256]{5,4,3,2,1,0:T(8,128)(2,1)}, u32[]{:S(2)}, u32[]{:S(2)}) collective-permute-start(bf16[2,4,4,2,16,256]{5,4,3,2,1,0:T(8,128)(2,1)S(1)} %pad_maximum_fusion.2.refs_2_), channel_id=1, source_target_pairs={{0,3},{1,0},{2,1},{3,2},{4,7},{5,4},{6,5},{7,6},{8,11},{9,8},{10,9... | collective-permute-start | bytes 1572872 | tf_op jit(solution)/shard_map/ppermute | solution.py:272
  161.9 1.0 copy-start.2
  162.9 1.1 copy-start.5
  164.0 1.1 copy-start.11
  165.1 9.3 %copy-start.3 = (bf16[2,4,4,2,16,256]{5,4,3,2,1,0:T(8,128)(2,1)S(1)}, bf16[2,4,4,2,16,256]{5,4,3,2,1,0:T(8,128)(2,1)}, u32[]{:S(2)}) copy-start(bf16[2,4,4,2,16,256]{5,4,3,2,1,0:T(8,128)(2,1)} %copy-done.1) | copy-start | bytes 1572868

commit v2 on v1

v2 whole, which is shorter than its diff:
```python
import jax
import jax.numpy as jnp
import ml_dtypes
import numpy as np
from jax import lax
from jax.experimental import pallas as pl
from jax.experimental.pallas import tpu as pltpu
from jax.sharding import Mesh
from jax.sharding import PartitionSpec as P

GRID = 32
AXES = ("zh", "y", "co", "zl", "x")
WIDE = ("zh", "y", "co")
NARROW = ("zl", "x")
NPW = 8192
DISC = 256
NKX = 26
CAN = 640
BF = jnp.bfloat16
F32 = jnp.float32


def split_bf16(value):
    high = value.astype(BF)
    return high, (value - high.astype(value.dtype)).astype(BF)


def tables():
    k = np.arange(GRID)
    fold = np.where(k < GRID // 2, k, k - GRID)
    length = fold[:, None, None] ** 2 + fold[None, :, None] ** 2 + fold[None, None, :] ** 2
    ordered = np.sort(length.ravel())[:NPW]
    limit = ordered[-1]
    disc = []
    for ky in range(-15, 16):
        for kz in range(0, 16):
            if ky * ky + kz * kz <= limit and (kz > 0 or ky >= 0):
                disc.append((ky, kz))
    assert len(disc) <= DISC
    points = np.arange(GRID)
    wave = np.zeros((GRID, GRID, 2 * DISC))
    key = np.full((DISC, 1), -9000, np.int32)
    for m, (ky, kz) in enumerate(disc):
        angle = 2 * np.pi * ((ky * points[:, None] + kz * points[None, :]) % GRID) / GRID
        wave[:, :, m] = np.cos(angle)
        wave[:, :, DISC + m] = -np.sin(angle)
        key[m, 0] = ky * 64 + kz
    kx = np.arange(NKX) - 12
    assert limit < 13 * 13
    angle = 2 * np.pi * (kx[:, None] * points[None, :] % GRID) / GRID
    eye = np.eye(8)
    along = np.concatenate([np.kron(np.cos(angle), eye), np.kron(np.sin(angle), eye)])
    blocks = 8
    col_key = np.full((blocks, 1, CAN), -8000, np.int32)
    col_kx = np.zeros((blocks, 1, CAN), np.int32)
    col_id = np.full((blocks, 1, CAN), -(1 << 20), np.int32)
    size = NPW // blocks
    for j in range(blocks):
        low, high = ordered[j * size], ordered[(j + 1) * size - 1]
        n = 0
        for ky, kz in disc:
            for x in range(-12, 13):
                if (ky, kz) == (0, 0) and x < 0:
                    continue
                if low <= x * x + ky * ky + kz * kz <= high:
                    col_key[j, 0, n] = ky * 64 + kz
                    col_kx[j, 0, n] = x + 12
                    col_id[j, 0, n] = (x * 64 + ky) * 64 + kz
                    n += 1
        assert n <= CAN
    wave = wave.reshape(GRID * GRID, 2 * DISC).astype(np.float32)
    along = along.astype(np.float32)
    return split_np(wave) + split_np(along) + (key, col_key, col_kx, col_id)


def split_np(value):


    high = value.astype(ml_dtypes.bfloat16)
    low = (value - high.astype(np.float32)).astype(ml_dtypes.bfloat16)
    return high, low


def folded(index):
    def fold(k):
        return jnp.where(k < GRID // 2, k, k - GRID)

    return (
        fold(lax.shift_right_logical(index, 10)),
        fold(lax.shift_right_logical(index, 5) & 31),
        fold(index & 31),
    )


def dot(a, b):
    return jnp.dot(a, b, preferred_element_type=F32)


def transform_kernel(pos, own, other, band0, band1, band2, band3, wave_hi_hbm, wave_lo_hbm, along_hi, along_lo, key,
                     col_key, col_kx, gmap, cols, rows, wave_hi, wave_lo, a_hi, a_lo, spectrum, sems):
    zh, y, co = pos[0], pos[1], pos[2]
    copies = [
        pltpu.make_async_copy(wave_hi_hbm, wave_hi, sems.at[0]),
        pltpu.make_async_copy(wave_lo_hbm, wave_lo, sems.at[1]),
    ]
    for copy in copies:
        copy.start()

    def product(q, carry):
        szh = (zh - q // 4) & 3
        sy = (y - q % 4) & 3
        start = pl.multiple_of(q * 16, 16)
        rows_of = [band[pl.ds(start, 16), :] for band in (band0, band1, band2, band3)]
        for n in range(8):
            mine = own[sy, szh, n]
            theirs = other[sy, szh, n]
            first = jnp.where(co == 0, mine, theirs)
            second = jnp.where(co == 0, theirs, mine)
            for s in range(4):
                pair = [first * rows_of[s][n : n + 1, :], second * rows_of[s][8 + n : 9 + n, :]]
                high, low = split_bf16(jnp.concatenate(pair, axis=0))
                at = pl.ds(pl.multiple_of(s * 256 + start, 16), 16)
                a_hi[at, n * 128 : (n + 1) * 128] = high
                a_lo[at, n * 128 : (n + 1) * 128] = low
        return carry

    lax.fori_loop(0, 16, product, 0)
    for copy in copies:
        copy.wait()
    field = dot(a_hi[...], wave_hi[...]) + (dot(a_lo[...], wave_hi[...]) + dot(a_hi[...], wave_lo[...]))
    half = NKX * 8
    norm = jnp.float32(1.0) / jnp.sqrt(jnp.float32(GRID**3))
    for s in range(4):
        f_hi, f_lo = split_bf16(field[s * 256 : s * 256 + 256])
        full = dot(along_hi[...], f_hi) + (dot(along_lo[...], f_hi) + dot(along_hi[...], f_lo))
        real = full[:half, :DISC] + full[half:, DISC:]
        imag = full[:half, DISC:] - full[half:, :DISC]
        spectrum[2 * s * half : (2 * s + 1) * half, :] = (real * norm).astype(BF)
        spectrum[(2 * s + 1) * half : (2 * s + 2) * half, :] = (imag * norm).astype(BF)

    def picked(wanted, kx, store):
        hot = jnp.where(key[...] == wanted, jnp.float32(1), jnp.float32(0)).astype(BF)
        found = dot(spectrum[...], hot)
        masks = [jnp.broadcast_to(kx == i, (8, wanted.shape[1])) for i in range(NKX - 1)]
        for s in range(4):
            parts = []
            for part in range(2):
                base = (2 * s + part) * half
                value = found[base : base + 8]
                for i in range(1, NKX - 1):
                    value = jnp.where(masks[i], found[base + i * 8 : base + i * 8 + 8], value)
                parts.append(value)
            store((zh - s) & 3, *parts)

    def columns(j, carry):
        kx = col_kx[j]

        def store(at, real, imag):
            cols[j, at] = jnp.concatenate([real, imag], axis=0).astype(BF)

        picked(col_key[j], kx, store)
        return carry

    lax.fori_loop(0, 8, columns, 0)

    def row_blocks(r, carry):
        kx, ky, kz = folded(gmap[zh * 4 + r])
        flip = jnp.where((kz < 0) | ((kz == 0) & (ky < 0)), -1, 1)
        sign = flip.astype(F32)

        def store(at, real, imag):
            both = jnp.concatenate([real, imag * sign], axis=0).astype(BF)
            rows[2 * r, at] = both[:, :256]
            rows[2 * r + 1, at] = both[:, 256:]

        picked(flip * (ky * 64 + kz), flip * kx + 12, store)
        return carry

    lax.fori_loop(0, 4, row_blocks, 0)


def transform(pos, own, other, bands, gmap):
    wave_hi, wave_lo, along_hi, along_lo, key, col_key, col_kx, _ = (jnp.asarray(t) for t in tables())

    def whole(value):
        return pl.BlockSpec(value.shape, lambda i, pos: (0,) * value.ndim, pipeline_mode=pl.Buffered(1))

    gmap = gmap.reshape(16, 1, 512)
    anywhere = pl.BlockSpec(memory_space=pl.ANY)
    operands = [own, other, *bands, wave_hi, wave_lo, along_hi, along_lo, key, col_key, col_kx, gmap]
    specs = [whole(v) for v in operands]
    specs[6] = specs[7] = anywhere
    outs = [jax.ShapeDtypeStruct((8, 4, 16, CAN), BF), jax.ShapeDtypeStruct((8, 4, 16, 256), BF)]
    return pl.pallas_call(
        transform_kernel,
        grid_spec=pltpu.PrefetchScalarGridSpec(
            num_scalar_prefetch=1,
            grid=(1,),
            in_specs=specs,
            out_specs=[whole(v) for v in outs],
            scratch_shapes=[
                pltpu.VMEM((1024, 2 * DISC), BF),
                pltpu.VMEM((1024, 2 * DISC), BF),
                pltpu.VMEM((1024, 1024), BF),
                pltpu.VMEM((1024, 1024), BF),
                pltpu.VMEM((8 * NKX * 8, DISC), BF),
                pltpu.SemaphoreType.DMA((2,)),
            ],
        ),
        out_shape=outs,
        compiler_params=pltpu.CompilerParams(vmem_limit_bytes=56 << 20),
        cost_estimate=pl.CostEstimate(flops=12 * 10**9, transcendentals=0, bytes_accessed=6 * 2**20),
        name="pair_transform",
    )(pos, *operands)


def prepare_kernel(pos, omega, r0, r1, r2, r3, gap, gmap, ident, scaled, hot, sign, row_k):
    co, zl, x = pos[2], pos[3], pos[4]

    @pl.when(pl.program_id(0) == 0)
    def _():
        kx, ky, kz = folded(gmap[0])
        flip = jnp.where((kz < 0) | ((kz == 0) & ((ky < 0) | ((ky == 0) & (kx < 0)))), -1, 1)
        wanted = (flip * ((kx * 64 + ky) * 64 + kz)).astype(F32)
        names = jnp.broadcast_to(ident[0].astype(F32), (128, CAN)).T
        for t in range(8):
            at = slice(t * 128, (t + 1) * 128)
            hot[:, at] = jnp.where(names == wanted[:, at], jnp.float32(1), jnp.float32(0)).astype(BF)
        sign[...] = jnp.concatenate([jnp.ones((8, 1024), F32), jnp.broadcast_to(flip.astype(F32), (8, 1024))], axis=0)

    for side in range(2):
        co_at = co if side == 0 else 1 - co
        for sx, ref in enumerate((r0, r1, r2, r3)):
            for szl in range(2):
                n = (zl ^ szl) * 4 + ((x - sx) & 3)
                to = pl.multiple_of(side * 512 + n * 64, 64)
                row_k[pl.ds(to, 64), :] = ref[szl, 0, co_at].reshape(64, 256)
        energy = gap[0, co_at]
        total = row_k[side * 512 : side * 512 + 512, :].astype(F32).T
        for w in range(6):
            weight = -2.0 * energy / (energy * energy + omega[w] * omega[w])
            weight = weight / jnp.sqrt(jnp.float32(2048))
            scaled[0, w * 256 : (w + 1) * 256, side * 512 : side * 512 + 512] = (total * weight).astype(BF)


def prepare(pos, omega, rows, gap, gmap, ident):
    row_spec = pl.BlockSpec((2, 1, 2, 4, 16, 256), lambda s, pos, om: (0, (pos[1] - s) & 3, 0, 0, 0, 0))
    return pl.pallas_call(
        prepare_kernel,
        grid_spec=pltpu.PrefetchScalarGridSpec(
            num_scalar_prefetch=2,
            grid=(4,),
            in_specs=[row_spec] * 4
            + [
                pl.BlockSpec((1, 2, 1, 512), lambda s, pos, om: ((pos[1] - s) & 3, 0, 0, 0)),
                pl.BlockSpec((1, 1, 1024), lambda s, pos, om: (pos[3] * 4 + pos[4], 0, 0)),
                pl.BlockSpec((1, 1, CAN), lambda s, pos, om: (pos[3] * 4 + pos[4], 0, 0)),
            ],
            out_specs=[
                pl.BlockSpec((1, 1536, 1024), lambda s, pos, om: (s, 0, 0)),
                pl.BlockSpec((CAN, 1024), lambda s, pos, om: (0, 0)),
                pl.BlockSpec((16, 1024), lambda s, pos, om: (0, 0)),
            ],
            scratch_shapes=[pltpu.VMEM((1024, 256), BF)],
        ),
        out_shape=[
            jax.ShapeDtypeStruct((4, 1536, 1024), BF),
            jax.ShapeDtypeStruct((CAN, 1024), BF),
            jax.ShapeDtypeStruct((16, 1024), F32),
        ],
        compiler_params=pltpu.CompilerParams(vmem_limit_bytes=48 << 20),
        cost_estimate=pl.CostEstimate(flops=10**9, transcendentals=0, bytes_accessed=20 * 2**20),
        name="scaled_rows",
    )(pos, omega, *rows, gap, gmap.reshape(8, 1, 1024), ident)


def product_body(mine, theirs, scaled, hot, sign, add, out, cols):
    n = pl.program_id(0)

    @pl.when(n == 0)
    def _():
        for side, ref in enumerate((mine, theirs)):
            full = dot(ref[...].reshape(512, CAN), hot[...]).reshape(32, 16, 1024) * sign[...][None]
            full = full.reshape(512, 1024).astype(BF)
            for t in range(4):
                cols[t, side * 512 : side * 512 + 512, :] = full[:, t * 256 : (t + 1) * 256]

    part = dot(scaled[0], cols[n]).reshape(6, 256, 256)
    out[...] = part if add is None else add[...] + part


def product_step(sy, mine, theirs, scaled, hot, sign, total):
    first = total is None

    def kernel(*refs):
        add = None if first else refs[5]
        product_body(*refs[:5], add, *refs[5 if first else 6 :])

    def fixed(shape, index):
        return pl.BlockSpec(shape, lambda n: index, pipeline_mode=pl.Buffered(1))

    acc_spec = pl.BlockSpec((6, 256, 256), lambda n: (0, 0, n))
    col_spec = fixed((8, 4, 16, CAN), (0, 0, 0, 0))
    in_specs = [
        col_spec,
        col_spec,
        fixed((1, 1536, 1024), (sy, 0, 0)),
        fixed((CAN, 1024), (0, 0)),
        fixed((16, 1024), (0, 0)),
    ]
    operands = [mine, theirs, scaled, hot, sign]
    if not first:
        in_specs.append(acc_spec)
        operands.append(total)
    return pl.pallas_call(
        kernel,
        grid=(4,),
        in_specs=in_specs,
        out_specs=acc_spec,
        scratch_shapes=[pltpu.VMEM((4, 1024, 256), BF)],
        out_shape=jax.ShapeDtypeStruct((6, 256, 1024), F32),
        input_output_aliases={} if first else {5: 0},
        compiler_params=pltpu.CompilerParams(vmem_limit_bytes=48 << 20),
        cost_estimate=pl.CostEstimate(flops=46 * 10**8, transcendentals=0, bytes_accessed=18 * 2**20),
        name="response_product",
    )(*operands)


def shifted(value, axis, shift):
    size = lax.axis_size(axis)
    return lax.ppermute(value, axis, [(i, (i + shift) % size) for i in range(size)])


def around(value, axis):
    return [value] + [shifted(value, axis, s) for s in range(1, lax.axis_size(axis))]


def body(valence, conduction, eps_val, eps_cond, omega, gmap):
    pos = jnp.stack([lax.axis_index(a) for a in AXES]).astype(jnp.int32)
    bands = around(conduction.reshape(256, 128), "zh")
    own = lax.all_to_all(jnp.broadcast_to(valence, (8, *valence.shape)), NARROW, 0, 0, tiled=True)
    own, bands = lax.optimization_barrier((own, bands))
    for axis in ("zh", "y"):
        own = jnp.stack(around(own, axis))
    other = shifted(own, "co", 1)
    cols, rows = transform(pos, own, other, bands, gmap)

    rows = lax.all_to_all(rows, ("y", "co"), 0, 0, tiled=True)
    cols = lax.all_to_all(cols, NARROW, 0, 0, tiled=True)
    cols = around(cols, "y")
    rows = jnp.stack(around(rows, "zl")).reshape(2, 4, 2, 4, 16, 256)
    rows = around(rows, "x")

    ec = jnp.transpose(eps_cond.reshape(4, 4, 2, 8), (1, 2, 3, 0)).reshape(4, 2, 32, 1, 1)
    gap = jnp.broadcast_to(ec - eps_val, (4, 2, 32, 2, 8)).reshape(4, 2, 1, 512)
    ident = jnp.asarray(tables()[-1])
    scaled, hot, sign = prepare(pos, omega, rows, gap, gmap, ident)
    total = None
    for sy in (0, 1, 3, 2):
        mine = cols[sy]
        if sy == 2:
            mine, total = lax.optimization_barrier((mine, total))
        theirs = shifted(mine, "co", 1)
        total = product_step(sy, mine, theirs, scaled, hot, sign, total)
    return total


def solution(mesh):
    torus = Mesh(mesh.devices.reshape(4, 4, 2, 2, 4), AXES)
    return jax.shard_map(
        body,
        mesh=torus,
        in_specs=(P(None, AXES), P(AXES, None), P(), P(), P(), P()),
        out_specs=P(None, WIDE, NARROW),
        check_vma=False,
    )
```

time: 211 us -> 181 us (0.86)
  waiting for transfers between devices: 58.7 us -> 34.6 us
  starting transfers between devices: 66.2 us -> 49.3 us
  blocking collectives: 9.6 us -> 20.6 us
  Pallas kernels: 56.6 us -> 67.5 us
  local copies, waits for them, and re-layouts: 15.4 us -> 6.39 us
    ppermute x25 -> x21, waiting for transfers between devices: 53.1 us -> 34.6 us  [shifted(): lax.ppermute(value, axis, [(i, (i + shift) % size) for i in range(size)])]
    ppermute x25 -> x21, starting transfers between devices: 57.2 us -> 45.8 us  [shifted(): lax.ppermute(value, axis, [(i, (i + shift) % size) for i in range(size)])]
    all_to_all x1 -> x2, blocking collectives: 9.6 us -> 20.6 us  [the longest x1 10.7 us: body(): rows = lax.all_to_all(rows, ('y', 'co'), 0, 0, tiled=True)]
    unnamed x42 -> x26, local copies, waits for them, and re-layouts: 13.2 us -> 2.65 us
    pallas_call x1, Pallas kernels: 13 us -> 19.3 us  [transform(): pl.pallas_call(transform_kernel, grid_spec=pltpu.PrefetchScalarGridSpec(n...]
    all_to_all x1, waiting for transfers between devices: 5.57 us -> 0.01 us  [body(): cols = lax.all_to_all(cols, NARROW, 0, 0, tiled=True)]
    all_to_all x1, starting transfers between devices: 8.99 us -> 3.54 us  [body(): cols = lax.all_to_all(cols, NARROW, 0, 0, tiled=True)]
    pallas_call x4 -> x5, Pallas kernels: 43.6 us -> 48.2 us  [the longest x4 40.3 us: product_step(): pl.pallas_call(kernel, grid=(4,), in_specs=in_specs, out_specs=acc_spec,...]
  transfers between devices with their start and end apart: 26 -> 22, of which waited for: 15 -> 13; matrix products, arithmetic and copies ran while one was open for 2% -> 3% of each run, Pallas kernels for 15% -> 21%
where the time goes in v2:
time: 181 us; the launch traced here: 180 us
  Pallas kernels  67.5 us (37%)
  starting transfers between devices  49.3 us (27%)
  waiting for transfers between devices  34.6 us (19%)
  blocking collectives  20.6 us (11%)
  local copies, waits for them, and re-layouts  6.39 us (4%)
    ppermute x21, starting transfers between devices, shifted(): lax.ppermute(value, axis, [(i, (i + shift) % size) for i in range(size)])  45.8 us
    pallas_call x4, Pallas kernels, product_step(): pl.pallas_call(kernel, grid=(4,), in_specs=in_specs, out_specs=acc_spec,...  40.3 us
    ppermute x21, waiting for transfers between devices, shifted(): lax.ppermute(value, axis, [(i, (i + shift) % size) for i in range(size)])  34.6 us
    pallas_call x1, Pallas kernels, transform(): pl.pallas_call(transform_kernel, grid_spec=pltpu.PrefetchScalarGridSpec(n...  19.3 us
    all_to_all x1, blocking collectives, body(): rows = lax.all_to_all(rows, ('y', 'co'), 0, 0, tiled=True)  10.7 us
    all_to_all x1, blocking collectives, body(): lax.all_to_all(jnp.broadcast_to(valence, (8, *valence.shape)), NARROW, 0,...  9.86 us
    pallas_call x1, Pallas kernels, prepare(): pl.pallas_call(prepare_kernel, grid_spec=pltpu.PrefetchScalarGridSpec(num...  7.91 us
  transfers between devices with their start and end apart: 22, of which 13 were waited for; matrix products, arithmetic and copies ran while one was open for 3% of the time, Pallas kernels for 21%

profile of v2, /device:TPU:1, one launch (start us, length us, event | category | flops | bytes accessed | tf_op | source)
XLA Modules:
  0.0 179.6 jit_solution(11037236063315753542)
XLA Ops:
  0.0 3.8 %collective-permute-start = (f32[256,128]{1,0:T(8,128)}, f32[256,128]{1,0:T(8,128)S(1)}, u32[]{:S(2)}, u32[]{:S(2)}) collective-permute-start(f32[256,128]{1,0:T(8,128)} %bitcast.34), channel_id=1, source_target_pairs={{0,64},{64,128},{128,192},{192,0},{1,65},{65,129},{129,193},{193,1... | collective-permute-start | bytes 393224 | tf_op jit(solution)/shard_map/ppermute | solution.py:331
  3.8 5.1 %collective-permute-start.1 = (f32[256,128]{1,0:T(8,128)}, f32[256,128]{1,0:T(8,128)S(1)}, u32[]{:S(2)}, u32[]{:S(2)}) collective-permute-start(f32[256,128]{1,0:T(8,128)} %bitcast.35), channel_id=1, source_target_pairs={{0,128},{64,192},{128,0},{192,64},{1,129},{65,193},{129,1},{193,65... | collective-permute-start | bytes 393224 | tf_op jit(solution)/shard_map/ppermute | solution.py:331
  8.9 2.4 %collective-permute-start.2 = (f32[256,128]{1,0:T(8,128)}, f32[256,128]{1,0:T(8,128)S(1)}, u32[]{:S(2)}, u32[]{:S(2)}) collective-permute-start(f32[256,128]{1,0:T(8,128)} %bitcast.36), channel_id=1, source_target_pairs={{0,192},{64,0},{128,64},{192,128},{1,193},{65,1},{129,65},{193,129... | collective-permute-start | bytes 393224 | tf_op jit(solution)/shard_map/ppermute | solution.py:331
  11.3 0.7 broadcast_in_dim.4
  12.0 9.9 %all_to_all.15 = f32[8,8,128]{2,1,0:T(8,128)S(1)} all-to-all(f32[8,8,128]{2,1,0:T(8,128)S(1)} %broadcast_in_dim.4), channel_id=1, replica_groups=mesh['zh'=4,'y'=4,'co'=2,'zl'=2,'x'=4] {'zl','x'}, dimensions={0} | all-to-all | bytes 65536 | tf_op jit(solution)/shard_map/all_to_all | solution.py:341
  22.0 1.1 collective-permute-start.3
  23.1 4.1 %collective-permute-start.4 = (f32[8,8,128]{2,1,0:T(8,128)S(1)}, f32[8,8,128]{2,1,0:T(8,128)S(1)}, u32[]{:S(2)}, u32[]{:S(2)}) collective-permute-start(f32[8,8,128]{2,1,0:T(8,128)S(1)} %all_to_all.15), channel_id=1, source_target_pairs={{0,128},{64,192},{128,0},{192,64},{1,129},{65,193},{129,1},{193,65... | collective-permute-start | bytes 98312 | tf_op jit(solution)/shard_map/ppermute | solution.py:331
  27.2 2.0 %collective-permute-start.5 = (f32[8,8,128]{2,1,0:T(8,128)S(1)}, f32[8,8,128]{2,1,0:T(8,128)S(1)}, u32[]{:S(2)}, u32[]{:S(2)}) collective-permute-start(f32[8,8,128]{2,1,0:T(8,128)S(1)} %all_to_all.15), channel_id=1, source_target_pairs={{0,192},{64,0},{128,64},{192,128},{1,193},{65,1},{129,65},{193,129... | collective-permute-start | bytes 98312 | tf_op jit(solution)/shard_map/ppermute | solution.py:331
  29.2 0.6 collective-permute-done.4
  29.8 1.4 collective-permute-done.5
  31.1 1.4 collective-permute-start.6
  32.5 2.6 %collective-permute-start.7 = (f32[4,8,8,128]{3,2,1,0:T(8,128)S(1)}, f32[4,8,8,128]{3,2,1,0:T(8,128)S(1)}, u32[]{:S(2)}, u32[]{:S(2)}) collective-permute-start(f32[4,8,8,128]{3,2,1,0:T(8,128)S(1)} %get-tuple-element.30), channel_id=1, source_target_pairs={{0,32},{16,48},{32,0},{48,16},{1,33},{17,49},{33,1},{49,17},{2,34}... | collective-permute-start | bytes 393224 | tf_op jit(solution)/shard_map/ppermute | solution.py:331
  35.1 1.1 collective-permute-start.8
  36.3 2.6 %collective-permute-done.7 = f32[4,8,8,128]{3,2,1,0:T(8,128)S(1)} collective-permute-done((f32[4,8,8,128]{3,2,1,0:T(8,128)S(1)}, f32[4,8,8,128]{3,2,1,0:T(8,128)S(1)}, u32[]{:S(2)}, u32[]{:S(2)}) %collective-permute-start.7) | collective-permute-done | bytes 131104 | tf_op jit(solution)/shard_map/ppermute | solution.py:331
  38.9 0.3 collective-permute-done.8
  39.3 4.7 %collective-permute-start.9 = (f32[4,4,8,8,128]{4,3,2,1,0:T(8,128)S(1)}, f32[4,4,8,8,128]{4,3,2,1,0:T(8,128)S(1)}, u32[]{:S(2)}, u32[]{:S(2)}) collective-permute-start(f32[4,4,8,8,128]{4,3,2,1,0:T(8,128)S(1)} %pad_maximum_fusion.own), channel_id=1, source_target_pairs={{0,8},{8,0},{1,9},{9,1},{2,10},{10,2},{3,11},{11,3},{4,12},{12,4},... | collective-permute-start | bytes 1572872 | tf_op jit(solution)/shard_map/ppermute | solution.py:331
  44.0 0.6 stack.62.pos
  44.6 0.9 collective-permute-done.9.other
  45.5 0.8 copy-done.9
  46.3 19.3 %pair_transform.1 = (bf16[8,4,16,640]{3,2,1,0:T(8,128)(2,1)}, bf16[8,4,16,256]{3,2,1,0:T(8,128)(2,1)}) custom-call(s32[5]{0:T(128)} %stack.62.pos, f32[4,4,8,8,128]{4,3,2,1,0:T(8,128)} %copy-done.6, f32[4,4,8,8,128]{4,3,2,1,0:T(8,128)} %copy-done.9, f32[256,128]{1,0:T(8,128)} %bitcast.37, f32[256,128]{1,0:T(8,128)} %copy-done.10, f32[256,128]{1,0:T(8,128)} %copy-done.11, ...), custom_call_target="tpu_custom_call" | custom-call | flops 12000000000 | bytes 6291456 | tf_op jit(solution)/shard_map/pair_transform/pallas_call | solution.py:194
  65.6 10.7 %all_to_all.16 = bf16[8,4,16,256]{3,2,1,0:T(8,128)(2,1)S(1)} all-to-all(bf16[8,4,16,256]{3,2,1,0:T(8,128)(2,1)} %get-tuple-element.23), channel_id=1, replica_groups=mesh['zh'=4,'y'=4,'co'=2,'zl'=2,'x'=4] {'y','co'}, dimensions={0} | all-to-all | bytes 524288 | tf_op jit(solution)/shard_map/all_to_all | solution.py:348
  76.3 3.5 %all-to-all-start.1 = ((bf16[8,4,16,640]{3,2,1,0:T(8,128)(2,1)}), bf16[8,4,16,640]{3,2,1,0:T(8,128)(2,1)S(1)}, u32[]{:S(2)}, u32[]{:S(2)}) async-start(bf16[8,4,16,640]{3,2,1,0:T(8,128)(2,1)} %get-tuple-element.22), calls=%async_computation.1 | async-start | bytes 1310720 | tf_op jit(solution)/shard_map/all_to_all | solution.py:349
  79.9 1.4 collective-permute-start.13
  81.3 12.5 %collective-permute-done.13 = bf16[8,4,16,256]{3,2,1,0:T(8,128)(2,1)S(1)} collective-permute-done((bf16[8,4,16,256]{3,2,1,0:T(8,128)(2,1)S(1)}, bf16[8,4,16,256]{3,2,1,0:T(8,128)(2,1)S(1)}, u32[]{:S(2)}, u32[]{:S(2)}) %collective-permute-start.13) | collective-permute-done | bytes 262176 | tf_op jit(solution)/shard_map/ppermute | solution.py:331
  93.8 0.9 pad_maximum_fusion.1.r0
  94.6 1.3 collective-permute-start.14
  95.9 0.3 collective-permute-start.17
  96.2 2.4 %collective-permute-start.11 = (bf16[8,4,16,640]{3,2,1,0:T(8,128)(2,1)S(1)}, bf16[8,4,16,640]{3,2,1,0:T(8,128)(2,1)S(1)}, u32[]{:S(2)}, u32[]{:S(2)}) collective-permute-start(bf16[8,4,16,640]{3,2,1,0:T(8,128)(2,1)S(1)} %all-to-all-done.1.refs_0_), channel_id=1, source_target_pairs={{0,48},{16,0},{32,16},{48,32},{1,49},{17,1},{33,17},{49,33},{2,50}... | collective-permute-start | bytes 1966088 | tf_op jit(solution)/shard_map/ppermute | solution.py:331
  98.6 2.8 %collective-permute-start.19 = (bf16[8,4,16,640]{3,2,1,0:T(8,128)(2,1)S(1)}, bf16[8,4,16,640]{3,2,1,0:T(8,128)(2,1)S(1)}, u32[]{:S(2)}, u32[]{:S(2)}) collective-permute-start(bf16[8,4,16,640]{3,2,1,0:T(8,128)(2,1)S(1)} %all-to-all-done.1.refs_0_), channel_id=1, source_target_pairs={{0,8},{8,0},{1,9},{9,1},{2,10},{10,2},{3,11},{11,3},{4,12},{12,4},... | collective-permute-start | bytes 1966088 | tf_op jit(solution)/shard_map/ppermute | solution.py:331
  101.4 2.4 %collective-permute-start.15 = (bf16[2,4,2,4,16,256]{5,4,3,2,1,0:T(8,128)(2,1)}, bf16[2,4,2,4,16,256]{5,4,3,2,1,0:T(8,128)(2,1)}, u32[]{:S(2)}, u32[]{:S(2)}) collective-permute-start(bf16[2,4,2,4,16,256]{5,4,3,2,1,0:T(8,128)(2,1)} %pad_maximum_fusion.1.r0), channel_id=1, source_target_pairs={{0,2},{1,3},{2,0},{3,1},{4,6},{5,7},{6,4},{7,5},{8,10},{9,11},{10,... | collective-permute-start | bytes 1572872 | tf_op jit(solution)/shard_map/ppermute | solution.py:331
  103.8 3.7 %collective-permute-done.14.r1 = bf16[2,4,2,4,16,256]{5,4,3,2,1,0:T(8,128)(2,1)S(1)} collective-permute-done((bf16[2,4,2,4,16,256]{5,4,3,2,1,0:T(8,128)(2,1)}, bf16[2,4,2,4,16,256]{5,4,3,2,1,0:T(8,128)(2,1)S(1)}, u32[]{:S(2)}, u32[]{:S(2)}) %collective-permute-start.14) | collective-permute-done | bytes 524320 | tf_op jit(solution)/shard_map/ppermute | solution.py:331
  107.5 0.8 copy-done.1
  108.3 1.4 collective-permute-start.16
  109.9 0.1 copy.18
  110.1 1.1 collective-permute-done.17.refs_0_
  111.2 4.5 %collective-permute-start.18 = (bf16[8,4,16,640]{3,2,1,0:T(8,128)(2,1)S(1)}, bf16[8,4,16,640]{3,2,1,0:T(8,128)(2,1)S(1)}, u32[]{:S(2)}, u32[]{:S(2)}) collective-permute-start(bf16[8,4,16,640]{3,2,1,0:T(8,128)(2,1)S(1)} %collective-permute-done.17.refs_0_), channel_id=1, source_target_pairs={{0,8},{8,0},{1,9},{9,1},{2,10},{10,2},{3,11},{11,3},{4,12},{12,4},... | collective-permute-start | bytes 1966088 | tf_op jit(solution)/shard_map/ppermute | solution.py:331
  115.7 0.8 broadcast_in_dim.10
  116.5 1.3 reshape.34.gap
  117.8 2.1 %collective-permute-done.15.r2 = bf16[2,4,2,4,16,256]{5,4,3,2,1,0:T(8,128)(2,1)} collective-permute-done((bf16[2,4,2,4,16,256]{5,4,3,2,1,0:T(8,128)(2,1)}, bf16[2,4,2,4,16,256]{5,4,3,2,1,0:T(8,128)(2,1)}, u32[]{:S(2)}, u32[]{:S(2)}) %collective-permute-start.15) | collective-permute-done | bytes 524320 | tf_op jit(solution)/shard_map/ppermute | solution.py:331
  119.9 7.2 %collective-permute-done.16.r3 = bf16[2,4,2,4,16,256]{5,4,3,2,1,0:T(8,128)(2,1)} collective-permute-done((bf16[2,4,2,4,16,256]{5,4,3,2,1,0:T(8,128)(2,1)}, bf16[2,4,2,4,16,256]{5,4,3,2,1,0:T(8,128)(2,1)}, u32[]{:S(2)}, u32[]{:S(2)}) %collective-permute-start.16) | collective-permute-done | bytes 524320 | tf_op jit(solution)/shard_map/ppermute | solution.py:331
  127.1 1.0 copy-done.2
  128.1 7.9 %scaled_rows.1 = (bf16[4,1536,1024]{2,1,0:T(8,128)(2,1)}, bf16[640,1024]{1,0:T(8,128)(2,1)S(1)}, f32[16,1024]{1,0:T(8,128)S(1)}) custom-call(s32[5]{0:T(128)S(1)} %copy-done, f32[6]{0:T(128)S(1)} %copy-done.4, bf16[2,4,2,4,16,256]{5,4,3,2,1,0:T(8,128)(2,1)} %pad_maximum_fusion.1.r0, bf16[2,4,2,4,16,256]{5,4,3,2,1,0:T(8,128)(2,1)S(1)} %copy-done.2, ...), custom_call_target="tpu_custom_call" | custom-call | flops 1000000000 | bytes 20971520 | tf_op jit(solution)/shard_map/scaled_rows/pallas_call | solution.py:248
  136.1 1.1 collective-permute-start.12
  137.1 8.9 %response_product.4.refs_5_ = f32[6,256,1024]{2,1,0:T(8,128)} custom-call(bf16[8,4,16,640]{3,2,1,0:T(8,128)(2,1)S(1)} %all-to-all-done.1.refs_0_, bf16[8,4,16,640]{3,2,1,0:T(8,128)(2,1)S(1)} %collective-permute-done.19.refs_1_, bf16[4,1536,1024]{2,1,0:T(8,128)(2,1)} %get-tuple-element.24.refs_2_, bf16[640,1024]{1,0:T(8,128)(2,1)S(1)} %get-tuple-element.25.refs_3_, ...), custom_call_target="tpu_custom_call" | custom-call | flops 4600000000 | bytes 18874368 | tf_op jit(solution)/shard_map/response_product/pallas_call | solution.py:315
  146.1 10.5 %response_product.5.refs_5_ = f32[6,256,1024]{2,1,0:T(8,128)} custom-call(bf16[8,4,16,640]{3,2,1,0:T(8,128)(2,1)S(1)} %collective-permute-done.17.refs_0_, bf16[8,4,16,640]{3,2,1,0:T(8,128)(2,1)S(1)} %collective-permute-done.18.refs_1_, bf16[4,1536,1024]{2,1,0:T(8,128)(2,1)} %get-tuple-element.24.refs_2_, ...), custom_call_target="tpu_custom_call", output_to_operand_aliasing={{}: (5, {})} | custom-call | flops 4600000000 | bytes 18874368 | tf_op jit(solution)/shard_map/response_product/pallas_call | solution.py:315
  156.6 10.5 %response_product.6.refs_5_ = f32[6,256,1024]{2,1,0:T(8,128)} custom-call(bf16[8,4,16,640]{3,2,1,0:T(8,128)(2,1)S(1)} %collective-permute-done.11.refs_0_, bf16[8,4,16,640]{3,2,1,0:T(8,128)(2,1)S(1)} %collective-permute-done.12.refs_1_, bf16[4,1536,1024]{2,1,0:T(8,128)(2,1)} %get-tuple-element.24.refs_2_, ...), custom_call_target="tpu_custom_call", output_to_operand_aliasing={{}: (5, {})} | custom-call | flops 4600000000 | bytes 18874368 | tf_op jit(solution)/shard_map/response_product/pallas_call | solution.py:315
  167.1 2.1 %collective-permute-done.20.refs_1_ = bf16[8,4,16,640]{3,2,1,0:T(8,128)(2,1)S(1)} collective-permute-done((bf16[8,4,16,640]{3,2,1,0:T(8,128)(2,1)S(1)}, bf16[8,4,16,640]{3,2,1,0:T(8,128)(2,1)S(1)}, u32[]{:S(2)}, u32[]{:S(2)}) %collective-permute-start.20) | collective-permute-done | bytes 655392 | tf_op jit(solution)/shard_map/ppermute | solution.py:331
  169.1 10.4 %response_product.7 = f32[6,256,1024]{2,1,0:T(8,128)} custom-call(bf16[8,4,16,640]{3,2,1,0:T(8,128)(2,1)S(1)} %collective-permute-done.10.refs_0_, bf16[8,4,16,640]{3,2,1,0:T(8,128)(2,1)S(1)} %collective-permute-done.20.refs_1_, bf16[4,1536,1024]{2,1,0:T(8,128)(2,1)} %get-tuple-element.24.refs_2_, ...), custom_call_target="tpu_custom_call", output_to_operand_aliasing={{}: (5, {})} | custom-call | flops 4600000000 | bytes 18874368 | tf_op jit(solution)/shard_map/response_product/pallas_call | solution.py:315
  (41 shorter events, 0.6 us)
Async XLA Ops:
  0.0 21.9 %collective-permute-start = (f32[256,128]{1,0:T(8,128)}, f32[256,128]{1,0:T(8,128)S(1)}, u32[]{:S(2)}, u32[]{:S(2)}) collective-permute-start(f32[256,128]{1,0:T(8,128)} %bitcast.34), channel_id=1, source_target_pairs={{0,64},{64,128},{128,192},{192,0},{1,65},{65,129},{129,193},{193,1... | collective-permute-start | bytes 393224 | tf_op jit(solution)/shard_map/ppermute | solution.py:331
  3.8 18.1 %collective-permute-start.1 = (f32[256,128]{1,0:T(8,128)}, f32[256,128]{1,0:T(8,128)S(1)}, u32[]{:S(2)}, u32[]{:S(2)}) collective-permute-start(f32[256,128]{1,0:T(8,128)} %bitcast.35), channel_id=1, source_target_pairs={{0,128},{64,192},{128,0},{192,64},{1,129},{65,193},{129,1},{193,65... | collective-permute-start | bytes 393224 | tf_op jit(solution)/shard_map/ppermute | solution.py:331
  8.9 13.0 %collective-permute-start.2 = (f32[256,128]{1,0:T(8,128)}, f32[256,128]{1,0:T(8,128)S(1)}, u32[]{:S(2)}, u32[]{:S(2)}) collective-permute-start(f32[256,128]{1,0:T(8,128)} %bitcast.36), channel_id=1, source_target_pairs={{0,192},{64,0},{128,64},{192,128},{1,193},{65,1},{129,65},{193,129... | collective-permute-start | bytes 393224 | tf_op jit(solution)/shard_map/ppermute | solution.py:331
  21.9 23.6 %copy-start.10 = (f32[256,128]{1,0:T(8,128)}, f32[256,128]{1,0:T(8,128)S(1)}, u32[]{:S(2)}) copy-start(f32[256,128]{1,0:T(8,128)S(1)} %collective-permute-done.band1) | copy-start | bytes 393220
  21.9 23.6 %copy-start.11 = (f32[256,128]{1,0:T(8,128)}, f32[256,128]{1,0:T(8,128)S(1)}, u32[]{:S(2)}) copy-start(f32[256,128]{1,0:T(8,128)S(1)} %collective-permute-done.1.band2) | copy-start | bytes 393220
  22.0 23.5 %copy-start.12 = (f32[256,128]{1,0:T(8,128)}, f32[256,128]{1,0:T(8,128)S(1)}, u32[]{:S(2)}) copy-start(f32[256,128]{1,0:T(8,128)S(1)} %collective-permute-done.2.band3) | copy-start | bytes 393220
  22.0 7.2 %collective-permute-start.3 = (f32[8,8,128]{2,1,0:T(8,128)S(1)}, f32[8,8,128]{2,1,0:T(8,128)S(1)}, u32[]{:S(2)}, u32[]{:S(2)}) collective-permute-start(f32[8,8,128]{2,1,0:T(8,128)S(1)} %all_to_all.15), channel_id=1, source_target_pairs={{0,64},{64,128},{128,192},{192,0},{1,65},{65,129},{129,193},{193,1... | collective-permute-start | bytes 98312 | tf_op jit(solution)/shard_map/ppermute | solution.py:331
  23.1 6.7 %collective-permute-start.4 = (f32[8,8,128]{2,1,0:T(8,128)S(1)}, f32[8,8,128]{2,1,0:T(8,128)S(1)}, u32[]{:S(2)}, u32[]{:S(2)}) collective-permute-start(f32[8,8,128]{2,1,0:T(8,128)S(1)} %all_to_all.15), channel_id=1, source_target_pairs={{0,128},{64,192},{128,0},{192,64},{1,129},{65,193},{129,1},{193,65... | collective-permute-start | bytes 98312 | tf_op jit(solution)/shard_map/ppermute | solution.py:331
  27.2 3.9 %collective-permute-start.5 = (f32[8,8,128]{2,1,0:T(8,128)S(1)}, f32[8,8,128]{2,1,0:T(8,128)S(1)}, u32[]{:S(2)}, u32[]{:S(2)}) collective-permute-start(f32[8,8,128]{2,1,0:T(8,128)S(1)} %all_to_all.15), channel_id=1, source_target_pairs={{0,192},{64,0},{128,64},{192,128},{1,193},{65,1},{129,65},{193,129... | collective-permute-start | bytes 98312 | tf_op jit(solution)/shard_map/ppermute | solution.py:331
  31.1 5.2 %collective-permute-start.6 = (f32[4,8,8,128]{3,2,1,0:T(8,128)S(1)}, f32[4,8,8,128]{3,2,1,0:T(8,128)S(1)}, u32[]{:S(2)}, u32[]{:S(2)}) collective-permute-start(f32[4,8,8,128]{3,2,1,0:T(8,128)S(1)} %get-tuple-element.30), channel_id=1, source_target_pairs={{0,16},{16,32},{32,48},{48,0},{1,17},{17,33},{33,49},{49,1},{2,18}... | collective-permute-start | bytes 393224 | tf_op jit(solution)/shard_map/ppermute | solution.py:331
  32.5 6.4 %collective-permute-start.7 = (f32[4,8,8,128]{3,2,1,0:T(8,128)S(1)}, f32[4,8,8,128]{3,2,1,0:T(8,128)S(1)}, u32[]{:S(2)}, u32[]{:S(2)}) collective-permute-start(f32[4,8,8,128]{3,2,1,0:T(8,128)S(1)} %get-tuple-element.30), channel_id=1, source_target_pairs={{0,32},{16,48},{32,0},{48,16},{1,33},{17,49},{33,1},{49,17},{2,34}... | collective-permute-start | bytes 393224 | tf_op jit(solution)/shard_map/ppermute | solution.py:331
  35.1 4.1 %collective-permute-start.8 = (f32[4,8,8,128]{3,2,1,0:T(8,128)S(1)}, f32[4,8,8,128]{3,2,1,0:T(8,128)S(1)}, u32[]{:S(2)}, u32[]{:S(2)}) collective-permute-start(f32[4,8,8,128]{3,2,1,0:T(8,128)S(1)} %get-tuple-element.30), channel_id=1, source_target_pairs={{0,48},{16,0},{32,16},{48,32},{1,49},{17,1},{33,17},{49,33},{2,50}... | collective-permute-start | bytes 393224 | tf_op jit(solution)/shard_map/ppermute | solution.py:331
  39.3 6.2 %copy-start.6 = (f32[4,4,8,8,128]{4,3,2,1,0:T(8,128)}, f32[4,4,8,8,128]{4,3,2,1,0:T(8,128)S(1)}, u32[]{:S(2)}) copy-start(f32[4,4,8,8,128]{4,3,2,1,0:T(8,128)S(1)} %pad_maximum_fusion.own) | copy-start | bytes 1572868
  39.3 6.2 %collective-permute-start.9 = (f32[4,4,8,8,128]{4,3,2,1,0:T(8,128)S(1)}, f32[4,4,8,8,128]{4,3,2,1,0:T(8,128)S(1)}, u32[]{:S(2)}, u32[]{:S(2)}) collective-permute-start(f32[4,4,8,8,128]{4,3,2,1,0:T(8,128)S(1)} %pad_maximum_fusion.own), channel_id=1, source_target_pairs={{0,8},{8,0},{1,9},{9,1},{2,10},{10,2},{3,11},{11,3},{4,12},{12,4},... | collective-permute-start | bytes 1572872 | tf_op jit(solution)/shard_map/ppermute | solution.py:331
  45.5 0.8 copy-start.9
  46.3 63.5 %copy-start.7 = (f32[256]{0:T(256)S(1)}, f32[256]{0:T(256)}, u32[]{:S(2)}) copy-start(f32[256]{0:T(256)} %param.17) | copy-start | bytes 3076
  46.3 69.3 %copy-start.8 = (f32[8]{0:T(128)S(1)}, f32[8]{0:T(128)}, u32[]{:S(2)}) copy-start(f32[8]{0:T(128)} %param.16) | copy-start | bytes 100
  46.3 80.8 %copy-start = (s32[5]{0:T(128)S(1)}, s32[5]{0:T(128)}, u32[]{:S(2)}) copy-start(s32[5]{0:T(128)} %stack.62.pos) | copy-start | bytes 64
  46.3 80.8 %copy-start.3 = (s32[8192]{0:T(1024)S(1)}, s32[8192]{0:T(1024)}, u32[]{:S(2)}) copy-start(s32[8192]{0:T(1024)} %param.19) | copy-start | bytes 98308
  46.3 80.8 %copy-start.4 = (f32[6]{0:T(128)S(1)}, f32[6]{0:T(128)}, u32[]{:S(2)}) copy-start(f32[6]{0:T(128)} %omega.1) | copy-start | bytes 76
  46.3 80.8 %copy-start.5 = (s32[8,1,640]{2,1,0:T(1,128)S(1)}, s32[8,1,640]{2,1,0:T(1,128)}, u32[]{:S(2)}) copy-start(s32[8,1,640]{2,1,0:T(1,128)} %constant.43.clone.ident) | copy-start | bytes 61444
  76.3 19.6 %all-to-all-start.1 = ((bf16[8,4,16,640]{3,2,1,0:T(8,128)(2,1)}), bf16[8,4,16,640]{3,2,1,0:T(8,128)(2,1)S(1)}, u32[]{:S(2)}, u32[]{:S(2)}) async-start(bf16[8,4,16,640]{3,2,1,0:T(8,128)(2,1)} %get-tuple-element.22), calls=%async_computation.1 | async-start | bytes 1310720 | tf_op jit(solution)/shard_map/all_to_all | solution.py:349
  79.9 13.9 %collective-permute-start.13 = (bf16[8,4,16,256]{3,2,1,0:T(8,128)(2,1)S(1)}, bf16[8,4,16,256]{3,2,1,0:T(8,128)(2,1)S(1)}, u32[]{:S(2)}, u32[]{:S(2)}) collective-permute-start(bf16[8,4,16,256]{3,2,1,0:T(8,128)(2,1)S(1)} %all_to_all.16), channel_id=1, source_target_pairs={{0,4},{4,0},{1,5},{5,1},{2,6},{6,2},{3,7},{7,3},{8,12},{12,8},{9,1... | collective-permute-start | bytes 786440 | tf_op jit(solution)/shard_map/ppermute | solution.py:331
  94.6 12.9 %collective-permute-start.14 = (bf16[2,4,2,4,16,256]{5,4,3,2,1,0:T(8,128)(2,1)}, bf16[2,4,2,4,16,256]{5,4,3,2,1,0:T(8,128)(2,1)S(1)}, u32[]{:S(2)}, u32[]{:S(2)}) collective-permute-start(bf16[2,4,2,4,16,256]{5,4,3,2,1,0:T(8,128)(2,1)} %pad_maximum_fusion.1.r0), channel_id=1, source_target_pairs={{0,1},{1,2},{2,3},{3,0},{4,5},{5,6},{6,7},{7,4},{8,9},{9,10},{10,1... | collective-permute-start | bytes 1572872 | tf_op jit(solution)/shard_map/ppermute | solution.py:331
  95.9 15.2 %collective-permute-start.17 = (bf16[8,4,16,640]{3,2,1,0:T(8,128)(2,1)S(1)}, bf16[8,4,16,640]{3,2,1,0:T(8,128)(2,1)S(1)}, u32[]{:S(2)}, u32[]{:S(2)}) collective-permute-start(bf16[8,4,16,640]{3,2,1,0:T(8,128)(2,1)S(1)} %all-to-all-done.1.refs_0_), channel_id=1, source_target_pairs={{0,16},{16,32},{32,48},{48,0},{1,17},{17,33},{33,49},{49,1},{2,18}... | collective-permute-start | bytes 1966088 | tf_op jit(solution)/shard_map/ppermute | solution.py:331
  96.2 39.8 %collective-permute-start.11 = (bf16[8,4,16,640]{3,2,1,0:T(8,128)(2,1)S(1)}, bf16[8,4,16,640]{3,2,1,0:T(8,128)(2,1)S(1)}, u32[]{:S(2)}, u32[]{:S(2)}) collective-permute-start(bf16[8,4,16,640]{3,2,1,0:T(8,128)(2,1)S(1)} %all-to-all-done.1.refs_0_), channel_id=1, source_target_pairs={{0,48},{16,0},{32,16},{48,32},{1,49},{17,1},{33,17},{49,33},{2,50}... | collective-permute-start | bytes 1966088 | tf_op jit(solution)/shard_map/ppermute | solution.py:331
  98.6 38.5 %collective-permute-start.19 = (bf16[8,4,16,640]{3,2,1,0:T(8,128)(2,1)S(1)}, bf16[8,4,16,640]{3,2,1,0:T(8,128)(2,1)S(1)}, u32[]{:S(2)}, u32[]{:S(2)}) collective-permute-start(bf16[8,4,16,640]{3,2,1,0:T(8,128)(2,1)S(1)} %all-to-all-done.1.refs_0_), channel_id=1, source_target_pairs={{0,8},{8,0},{1,9},{9,1},{2,10},{10,2},{3,11},{11,3},{4,12},{12,4},... | collective-permute-start | bytes 1966088 | tf_op jit(solution)/shard_map/ppermute | solution.py:331
  101.4 18.5 %collective-permute-start.15 = (bf16[2,4,2,4,16,256]{5,4,3,2,1,0:T(8,128)(2,1)}, bf16[2,4,2,4,16,256]{5,4,3,2,1,0:T(8,128)(2,1)}, u32[]{:S(2)}, u32[]{:S(2)}) collective-permute-start(bf16[2,4,2,4,16,256]{5,4,3,2,1,0:T(8,128)(2,1)} %pad_maximum_fusion.1.r0), channel_id=1, source_target_pairs={{0,2},{1,3},{2,0},{3,1},{4,6},{5,7},{6,4},{7,5},{8,10},{9,11},{10,... | collective-permute-start | bytes 1572872 | tf_op jit(solution)/shard_map/ppermute | solution.py:331
  107.5 0.8 copy-start.1
  108.3 18.8 %collective-permute-start.16 = (bf16[2,4,2,4,16,256]{5,4,3,2,1,0:T(8,128)(2,1)}, bf16[2,4,2,4,16,256]{5,4,3,2,1,0:T(8,128)(2,1)}, u32[]{:S(2)}, u32[]{:S(2)}) collective-permute-start(bf16[2,4,2,4,16,256]{5,4,3,2,1,0:T(8,128)(2,1)} %pad_maximum_fusion.1.r0), channel_id=1, source_target_pairs={{0,3},{1,0},{2,1},{3,2},{4,7},{5,4},{6,5},{7,6},{8,11},{9,8},{10,9... | collective-permute-start | bytes 1572872 | tf_op jit(solution)/shard_map/ppermute | solution.py:331
  111.2 34.9 %collective-permute-start.18 = (bf16[8,4,16,640]{3,2,1,0:T(8,128)(2,1)S(1)}, bf16[8,4,16,640]{3,2,1,0:T(8,128)(2,1)S(1)}, u32[]{:S(2)}, u32[]{:S(2)}) collective-permute-start(bf16[8,4,16,640]{3,2,1,0:T(8,128)(2,1)S(1)} %collective-permute-done.17.refs_0_), channel_id=1, source_target_pairs={{0,8},{8,0},{1,9},{9,1},{2,10},{10,2},{3,11},{11,3},{4,12},{12,4},... | collective-permute-start | bytes 1966088 | tf_op jit(solution)/shard_map/ppermute | solution.py:331
  127.1 1.0 copy-start.2
  136.0 31.0 %collective-permute-start.10 = (bf16[8,4,16,640]{3,2,1,0:T(8,128)(2,1)S(1)}, bf16[8,4,16,640]{3,2,1,0:T(8,128)(2,1)S(1)}, u32[]{:S(2)}, u32[]{:S(2)}) collective-permute-start(bf16[8,4,16,640]{3,2,1,0:T(8,128)(2,1)S(1)} %all-to-all-done.1.refs_0_), channel_id=1, source_target_pairs={{0,32},{16,48},{32,0},{48,16},{1,33},{17,49},{33,1},{49,17},{2,34}... | collective-permute-start | bytes 1966088 | tf_op jit(solution)/shard_map/ppermute | solution.py:331
  136.1 20.5 %collective-permute-start.12 = (bf16[8,4,16,640]{3,2,1,0:T(8,128)(2,1)S(1)}, bf16[8,4,16,640]{3,2,1,0:T(8,128)(2,1)S(1)}, u32[]{:S(2)}, u32[]{:S(2)}) collective-permute-start(bf16[8,4,16,640]{3,2,1,0:T(8,128)(2,1)S(1)} %collective-permute-done.11.refs_0_), channel_id=1, source_target_pairs={{0,8},{8,0},{1,9},{9,1},{2,10},{10,2},{3,11},{11,3},{4,12},{12,4},... | collective-permute-start | bytes 1966088 | tf_op jit(solution)/shard_map/ppermute | solution.py:331
  167.0 2.1 %collective-permute-start.20 = (bf16[8,4,16,640]{3,2,1,0:T(8,128)(2,1)S(1)}, bf16[8,4,16,640]{3,2,1,0:T(8,128)(2,1)S(1)}, u32[]{:S(2)}, u32[]{:S(2)}) collective-permute-start(bf16[8,4,16,640]{3,2,1,0:T(8,128)(2,1)S(1)} %collective-permute-done.10.refs_0_), channel_id=1, source_target_pairs={{0,8},{8,0},{1,9},{9,1},{2,10},{10,2},{3,11},{11,3},{4,12},{12,4},... | collective-permute-start | bytes 1966088 | tf_op jit(solution)/shard_map/ppermute | solution.py:331

commit v3 on v2

--- a/solution.py
+++ b/solution.py
@@ -96,15 +96,53 @@
     return jnp.dot(a, b, preferred_element_type=F32)
 
 
-def transform_kernel(pos, own, other, band0, band1, band2, band3, wave_hi_hbm, wave_lo_hbm, along_hi, along_lo, key,
-                     col_key, col_kx, gmap, cols, rows, wave_hi, wave_lo, a_hi, a_lo, spectrum, sems):
-    zh, y, co = pos[0], pos[1], pos[2]
-    copies = [
-        pltpu.make_async_copy(wave_hi_hbm, wave_hi, sems.at[0]),
-        pltpu.make_async_copy(wave_lo_hbm, wave_lo, sems.at[1]),
-    ]
+def picked(spectrum, key, wanted, kx, zh, store):
+    half = NKX * 8
+    hot = jnp.where(key[...] == wanted, jnp.float32(1), jnp.float32(0)).astype(BF)
+    found = dot(spectrum[...], hot)
+    masks = [jnp.broadcast_to(kx == i, (8, wanted.shape[1])) for i in range(NKX - 1)]
+    for s in range(4):
+        parts = []
+        for part in range(2):
+            base = (2 * s + part) * half
+            value = found[base : base + 8]
+            for i in range(1, NKX - 1):
+                value = jnp.where(masks[i], found[base + i * 8 : base + i * 8 + 8], value)
+            parts.append(value)
+        store((zh - s) & 3, *parts)
+
+
+def fetch(sources, targets, sems):
+    copies = [pltpu.make_async_copy(s, t, sems.at[i]) for i, (s, t) in enumerate(zip(sources, targets))]
     for copy in copies:
         copy.start()
+    return copies
+
+
+def column_kernel(pos, *refs):
+    cols = refs[4]
+    spectrum, key, col_key, col_kx = refs[5:9]
+    for copy in fetch(refs[:4], refs[5:9], refs[9]):
+        copy.wait()
+
+    def columns(j, carry):
+        def store(at, real, imag):
+            cols[j, at] = jnp.concatenate([real, imag], axis=0).astype(BF)
+
+        picked(spectrum, key, col_key[j], col_kx[j], pos[0], store)
+        return carry
+
+    lax.fori_loop(0, 8, columns, 0)
+
+
+def transform_kernel(pos, *refs):
+    sources, rows, spectrum, targets = refs[:12], refs[12], refs[13], refs[14:26]
+    a_hi, a_lo, sems = refs[26:]
+    own, other, band0, band1, band2, band3, wave_hi, wave_lo, along_hi, along_lo, key, gmap = targets
+    zh, y, co = pos[0], pos[1], pos[2]
+    copies = fetch(sources, targets, sems)
+    for copy in copies[:6]:
+        copy.wait()
 
     def product(q, carry):
         szh = (zh - q // 4) & 3
@@ -125,7 +163,7 @@
         return carry
 
     lax.fori_loop(0, 16, product, 0)
-    for copy in copies:
+    for copy in copies[6:]:
         copy.wait()
     field = dot(a_hi[...], wave_hi[...]) + (dot(a_lo[...], wave_hi[...]) + dot(a_hi[...], wave_lo[...]))
     half = NKX * 8
@@ -138,31 +176,6 @@
         spectrum[2 * s * half : (2 * s + 1) * half, :] = (real * norm).astype(BF)
         spectrum[(2 * s + 1) * half : (2 * s + 2) * half, :] = (imag * norm).astype(BF)
 
-    def picked(wanted, kx, store):
-        hot = jnp.where(key[...] == wanted, jnp.float32(1), jnp.float32(0)).astype(BF)
-        found = dot(spectrum[...], hot)
-        masks = [jnp.broadcast_to(kx == i, (8, wanted.shape[1])) for i in range(NKX - 1)]
-        for s in range(4):
-            parts = []
-            for part in range(2):
-                base = (2 * s + part) * half
-                value = found[base : base + 8]
-                for i in range(1, NKX - 1):
-                    value = jnp.where(masks[i], found[base + i * 8 : base + i * 8 + 8], value)
-                parts.append(value)
-            store((zh - s) & 3, *parts)
-
-    def columns(j, carry):
-        kx = col_kx[j]
-
-        def store(at, real, imag):
-            cols[j, at] = jnp.concatenate([real, imag], axis=0).astype(BF)
-
-        picked(col_key[j], kx, store)
-        return carry
-
-    lax.fori_loop(0, 8, columns, 0)
-
     def row_blocks(r, carry):
         kx, ky, kz = folded(gmap[zh * 4 + r])
         flip = jnp.where((kz < 0) | ((kz == 0) & (ky < 0)), -1, 1)
@@ -173,45 +186,59 @@
             rows[2 * r, at] = both[:, :256]
             rows[2 * r + 1, at] = both[:, 256:]
 
-        picked(flip * (ky * 64 + kz), flip * kx + 12, store)
+        picked(spectrum, key, flip * (ky * 64 + kz), flip * kx + 12, zh, store)
         return carry
 
     lax.fori_loop(0, 4, row_blocks, 0)
+
+
+def whole(value):
+    zeros = (0,) * len(value.shape)
+    return pl.BlockSpec(value.shape, lambda *_: zeros, pipeline_mode=pl.Buffered(1))
+
+
+def resident():
+    return pl.BlockSpec(memory_space=pltpu.VMEM)
 
 
 def transform(pos, own, other, bands, gmap):
     wave_hi, wave_lo, along_hi, along_lo, key, col_key, col_kx, _ = (jnp.asarray(t) for t in tables())
-
-    def whole(value):
-        return pl.BlockSpec(value.shape, lambda i, pos: (0,) * value.ndim, pipeline_mode=pl.Buffered(1))
-
     gmap = gmap.reshape(16, 1, 512)
+    operands = [own, other, *bands, wave_hi, wave_lo, along_hi, along_lo, key, gmap]
     anywhere = pl.BlockSpec(memory_space=pl.ANY)
-    operands = [own, other, *bands, wave_hi, wave_lo, along_hi, along_lo, key, col_key, col_kx, gmap]
-    specs = [whole(v) for v in operands]
-    specs[6] = specs[7] = anywhere
-    outs = [jax.ShapeDtypeStruct((8, 4, 16, CAN), BF), jax.ShapeDtypeStruct((8, 4, 16, 256), BF)]
-    return pl.pallas_call(
+    in_hbm = pl.BlockSpec(memory_space=pltpu.HBM)
+    lines = 8 * NKX * 8
+    rows, spectrum = pl.pallas_call(
         transform_kernel,
         grid_spec=pltpu.PrefetchScalarGridSpec(
             num_scalar_prefetch=1,
             grid=(1,),
-            in_specs=specs,
-            out_specs=[whole(v) for v in outs],
-            scratch_shapes=[
-                pltpu.VMEM((1024, 2 * DISC), BF),
-                pltpu.VMEM((1024, 2 * DISC), BF),
-                pltpu.VMEM((1024, 1024), BF),
-                pltpu.VMEM((1024, 1024), BF),
-                pltpu.VMEM((8 * NKX * 8, DISC), BF),
-                pltpu.SemaphoreType.DMA((2,)),
-            ],
+            in_specs=[anywhere] * 2 + [in_hbm] + [anywhere] * 3 + [in_hbm] * 6,
+            out_specs=[whole(np.zeros((8, 4, 16, 256))), whole(np.zeros((lines, DISC)))],
+            scratch_shapes=[pltpu.VMEM(v.shape, v.dtype) for v in operands]
+            + [pltpu.VMEM((1024, 1024), BF), pltpu.VMEM((1024, 1024), BF), pltpu.SemaphoreType.DMA((len(operands),))],
         ),
-        out_shape=outs,
-        compiler_params=pltpu.CompilerParams(vmem_limit_bytes=56 << 20),
-        cost_estimate=pl.CostEstimate(flops=12 * 10**9, transcendentals=0, bytes_accessed=6 * 2**20),
+        out_shape=[jax.ShapeDtypeStruct((8, 4, 16, 256), BF), jax.ShapeDtypeStruct((lines, DISC), BF)],
+        compiler_params=pltpu.CompilerParams(vmem_limit_bytes=60 << 20),
+        cost_estimate=pl.CostEstimate(flops=8 * 10**9, transcendentals=0, bytes_accessed=6 * 2**20),
         name="pair_transform",
     )(pos, *operands)
+    cols = pl.pallas_call(
+        column_kernel,
+        grid_spec=pltpu.PrefetchScalarGridSpec(
+            num_scalar_prefetch=1,
+            grid=(1,),
+            in_specs=[in_hbm] * 4,
+            out_specs=whole(np.zeros((8, 4, 16, CAN))),
+            scratch_shapes=[pltpu.VMEM(v.shape, v.dtype) for v in (spectrum, key, col_key, col_kx)]
+            + [pltpu.SemaphoreType.DMA((4,))],
+        ),
+        out_shape=jax.ShapeDtypeStruct((8, 4, 16, CAN), BF),
+        compiler_params=pltpu.CompilerParams(vmem_limit_bytes=60 << 20),
+        cost_estimate=pl.CostEstimate(flops=8 * 10**9, transcendentals=0, bytes_accessed=2 * 2**20),
+        name="column_pairs",
+    )(pos, spectrum, key, col_key, col_kx)
+    return cols, rows
 
 
 def prepare_kernel(pos, omega, r0, r1, r2, r3, gap, gmap, ident, scaled, hot, sign, row_k):
@@ -240,11 +267,13 @@
         for w in range(6):
             weight = -2.0 * energy / (energy * energy + omega[w] * omega[w])
             weight = weight / jnp.sqrt(jnp.float32(2048))
-            scaled[0, w * 256 : (w + 1) * 256, side * 512 : side * 512 + 512] = (total * weight).astype(BF)
+            scaled[pl.program_id(0), w * 256 : (w + 1) * 256, side * 512 : side * 512 + 512] = (total * weight).astype(BF)
 
 
 def prepare(pos, omega, rows, gap, gmap, ident):
     row_spec = pl.BlockSpec((2, 1, 2, 4, 16, 256), lambda s, pos, om: (0, (pos[1] - s) & 3, 0, 0, 0, 0))
+    rows = [pltpu.with_memory_space_constraint(r, pltpu.HBM) for r in rows]
+    gmap, ident = (pltpu.with_memory_space_constraint(v, pltpu.HBM) for v in (gmap.reshape(8, 1, 1024), ident))
     return pl.pallas_call(
         prepare_kernel,
         grid_spec=pltpu.PrefetchScalarGridSpec(
@@ -256,72 +285,52 @@
                 pl.BlockSpec((1, 1, 1024), lambda s, pos, om: (pos[3] * 4 + pos[4], 0, 0)),
                 pl.BlockSpec((1, 1, CAN), lambda s, pos, om: (pos[3] * 4 + pos[4], 0, 0)),
             ],
-            out_specs=[
-                pl.BlockSpec((1, 1536, 1024), lambda s, pos, om: (s, 0, 0)),
-                pl.BlockSpec((CAN, 1024), lambda s, pos, om: (0, 0)),
-                pl.BlockSpec((16, 1024), lambda s, pos, om: (0, 0)),
-            ],
+            out_specs=[resident(), resident(), resident()],
             scratch_shapes=[pltpu.VMEM((1024, 256), BF)],
         ),
-        out_shape=[
-            jax.ShapeDtypeStruct((4, 1536, 1024), BF),
-            jax.ShapeDtypeStruct((CAN, 1024), BF),
-            jax.ShapeDtypeStruct((16, 1024), F32),
-        ],
-        compiler_params=pltpu.CompilerParams(vmem_limit_bytes=48 << 20),
+        out_shape=[pltpu.VMEM((4, 1536, 1024), BF), pltpu.VMEM((CAN, 1024), BF), pltpu.VMEM((16, 1024), F32)],
+        compiler_params=pltpu.CompilerParams(vmem_limit_bytes=20 << 20),
         cost_estimate=pl.CostEstimate(flops=10**9, transcendentals=0, bytes_accessed=20 * 2**20),
         name="scaled_rows",
-    )(pos, omega, *rows, gap, gmap.reshape(8, 1, 1024), ident)
-
-
-def product_body(mine, theirs, scaled, hot, sign, add, out, cols):
-    n = pl.program_id(0)
-
-    @pl.when(n == 0)
-    def _():
-        for side, ref in enumerate((mine, theirs)):
-            full = dot(ref[...].reshape(512, CAN), hot[...]).reshape(32, 16, 1024) * sign[...][None]
-            full = full.reshape(512, 1024).astype(BF)
-            for t in range(4):
-                cols[t, side * 512 : side * 512 + 512, :] = full[:, t * 256 : (t + 1) * 256]
-
-    part = dot(scaled[0], cols[n]).reshape(6, 256, 256)
-    out[...] = part if add is None else add[...] + part
-
-
-def product_step(sy, mine, theirs, scaled, hot, sign, total):
-    first = total is None
-
-    def kernel(*refs):
-        add = None if first else refs[5]
-        product_body(*refs[:5], add, *refs[5 if first else 6 :])
-
-    def fixed(shape, index):
-        return pl.BlockSpec(shape, lambda n: index, pipeline_mode=pl.Buffered(1))
-
-    acc_spec = pl.BlockSpec((6, 256, 256), lambda n: (0, 0, n))
-    col_spec = fixed((8, 4, 16, CAN), (0, 0, 0, 0))
-    in_specs = [
-        col_spec,
-        col_spec,
-        fixed((1, 1536, 1024), (sy, 0, 0)),
-        fixed((CAN, 1024), (0, 0)),
-        fixed((16, 1024), (0, 0)),
-    ]
-    operands = [mine, theirs, scaled, hot, sign]
-    if not first:
-        in_specs.append(acc_spec)
-        operands.append(total)
+    )(pos, omega, *rows, gap, gmap, ident)
+
+
+def expand(mine, theirs, hot, sign, cols):
+    for side, ref in enumerate((mine, theirs)):
+        full = dot(ref[...].reshape(512, CAN), hot[...]).reshape(32, 16, 1024) * sign[...][None]
+        full = full.reshape(512, 1024).astype(BF)
+        for t in range(4):
+            cols[t, side * 512 : side * 512 + 512, :] = full[:, t * 256 : (t + 1) * 256]
+
+
+def product_step(sy, mine, theirs, scaled, hot, sign, total, last):
+    def kernel(mine, theirs, scaled, hot, sign, *refs):
+        out, cols = refs[-2:]
+        add = None if total is None else refs[0]
+        if last:
+            n = pl.program_id(0)
+            pl.when(n == 0)(lambda: expand(mine, theirs, hot, sign, cols))
+            at = pl.ds(pl.multiple_of(n * 256, 256), 256)
+            out[...] = add[:, :, at] + dot(scaled[sy], cols[n]).reshape(6, 256, 256)
+        else:
+            expand(mine, theirs, hot, sign, cols)
+            for n in range(4):
+                at = slice(n * 256, n * 256 + 256)
+                part = dot(scaled[sy], cols[n]).reshape(6, 256, 256)
+                out[:, :, at] = part if add is None else add[:, :, at] + part
+
+    operands = [mine, theirs, scaled, hot, sign] + ([] if total is None else [total])
+    aliases = {} if total is None or last else {5: 0}
     return pl.pallas_call(
         kernel,
-        grid=(4,),
-        in_specs=in_specs,
-        out_specs=acc_spec,
+        grid=(4 if last else 1,),
+        in_specs=[resident()] * len(operands),
+        out_specs=pl.BlockSpec((6, 256, 256), lambda n: (0, 0, n)) if last else resident(),
         scratch_shapes=[pltpu.VMEM((4, 1024, 256), BF)],
-        out_shape=jax.ShapeDtypeStruct((6, 256, 1024), F32),
-        input_output_aliases={} if first else {5: 0},
-        compiler_params=pltpu.CompilerParams(vmem_limit_bytes=48 << 20),
-        cost_estimate=pl.CostEstimate(flops=46 * 10**8, transcendentals=0, bytes_accessed=18 * 2**20),
+        out_shape=(jax.ShapeDtypeStruct if last else pltpu.VMEM)((6, 256, 1024), F32),
+        input_output_aliases=aliases,
+        compiler_params=pltpu.CompilerParams(vmem_limit_bytes=20 << 20),
+        cost_estimate=pl.CostEstimate(flops=46 * 10**8, transcendentals=0, bytes_accessed=10 * 2**20),
         name="response_product",
     )(*operands)
 
@@ -333,6 +342,14 @@
 
 def around(value, axis):
     return [value] + [shifted(value, axis, s) for s in range(1, lax.axis_size(axis))]
+
+
+def ring(value, axis):
+    behind = shifted(value, axis, 1)
+    ahead = shifted(value, axis, 3)
+    half = value.shape[0] // 2
+    opposite = [shifted(ahead[:half], axis, 3), shifted(behind[half:], axis, 1)]
+    return [value, behind, opposite, ahead]
 
 
 def body(valence, conduction, eps_val, eps_cond, omega, gmap):
@@ -347,22 +364,24 @@
 
     rows = lax.all_to_all(rows, ("y", "co"), 0, 0, tiled=True)
     cols = lax.all_to_all(cols, NARROW, 0, 0, tiled=True)
-    cols = around(cols, "y")
+    cols = ring(cols, "y")
+    far_cols = cols.pop(2)
     rows = jnp.stack(around(rows, "zl")).reshape(2, 4, 2, 4, 16, 256)
-    rows = around(rows, "x")
-
+    rows = ring(rows, "x")
+    rows[2] = jnp.concatenate(rows[2])
+
+    rows, cols = lax.optimization_barrier((rows, cols))
     ec = jnp.transpose(eps_cond.reshape(4, 4, 2, 8), (1, 2, 3, 0)).reshape(4, 2, 32, 1, 1)
     gap = jnp.broadcast_to(ec - eps_val, (4, 2, 32, 2, 8)).reshape(4, 2, 1, 512)
     ident = jnp.asarray(tables()[-1])
     scaled, hot, sign = prepare(pos, omega, rows, gap, gmap, ident)
     total = None
-    for sy in (0, 1, 3, 2):
-        mine = cols[sy]
-        if sy == 2:
-            mine, total = lax.optimization_barrier((mine, total))
+    for sy, mine in zip((0, 1, 3), cols):
         theirs = shifted(mine, "co", 1)
-        total = product_step(sy, mine, theirs, scaled, hot, sign, total)
-    return total
+        total = product_step(sy, mine, theirs, scaled, hot, sign, total, False)
+    mine = jnp.concatenate(far_cols)
+    theirs = shifted(mine, "co", 1)
+    return product_step(2, mine, theirs, scaled, hot, sign, total, True)
 
 
 def solution(mesh):

time: 181 us -> 159 us (0.88)
  Pallas kernels: 67.5 us -> 49.9 us
  blocking collectives: 20.6 us -> 9.86 us
  waiting for transfers between devices: 34.6 us -> 38.5 us
  starting transfers between devices: 49.3 us -> 52.3 us
    all_to_all x1 -> x0, blocking collectives: 10.7 us -> none  [body(): rows = lax.all_to_all(rows, ('y', 'co'), 0, 0, tiled=True)]
    pallas_call x1, Pallas kernels: 19.3 us -> 11.6 us  [transform(): pl.pallas_call(transform_kernel, grid_spec=pltpu.PrefetchScalarGridSpec(n...]
    pallas_call x4 -> x5, Pallas kernels: 40.3 us -> 33.3 us  [the longest x4 23.2 us: product_step(): pl.pallas_call(kernel, grid=(4 if last else 1,), in_specs=[resident()] *...]
    all_to_all x0 -> x1, starting transfers between devices: none -> 4.22 us  [body(): rows = lax.all_to_all(rows, ('y', 'co'), 0, 0, tiled=True)]
    ppermute x21 -> x23, waiting for transfers between devices: 34.6 us -> 38.5 us  [shifted(): lax.ppermute(value, axis, [(i, (i + shift) % size) for i in range(size)])]
    pallas_call x1, Pallas kernels: 7.91 us -> 5.07 us  [prepare(): pl.pallas_call(prepare_kernel, grid_spec=pltpu.PrefetchScalarGridSpec(num...]
    ppermute x21 -> x23, starting transfers between devices: 45.8 us -> 44.5 us  [shifted(): lax.ppermute(value, axis, [(i, (i + shift) % size) for i in range(size)])]
  transfers between devices with their start and end apart: 22 -> 25, of which waited for: 13 -> 13; matrix products, arithmetic and copies ran while one was open for 3% -> 4% of each run, Pallas kernels for 21% -> 20%
where the time goes in v3:
time: 159 us; the launch traced here: 158 us
  starting transfers between devices  52.3 us (33%)
  Pallas kernels  49.9 us (31%)
  waiting for transfers between devices  38.5 us (24%)
  blocking collectives  9.86 us (6%)
  local copies, waits for them, and re-layouts  6.45 us (4%)
    ppermute x23, starting transfers between devices, shifted(): lax.ppermute(value, axis, [(i, (i + shift) % size) for i in range(size)])  44.5 us
    ppermute x23, waiting for transfers between devices, shifted(): lax.ppermute(value, axis, [(i, (i + shift) % size) for i in range(size)])  38.5 us
    pallas_call x4, Pallas kernels, product_step(): pl.pallas_call(kernel, grid=(4 if last else 1,), in_specs=[resident()] *...  23.2 us
    pallas_call x1, Pallas kernels, transform(): pl.pallas_call(transform_kernel, grid_spec=pltpu.PrefetchScalarGridSpec(n...  11.6 us
    pallas_call x1, Pallas kernels, transform(): pl.pallas_call(column_kernel, grid_spec=pltpu.PrefetchScalarGridSpec(num_...  10.1 us
    all_to_all x1, blocking collectives, body(): lax.all_to_all(jnp.broadcast_to(valence, (8, *valence.shape)), NARROW, 0,...  9.86 us
    pallas_call x1, Pallas kernels, prepare(): pl.pallas_call(prepare_kernel, grid_spec=pltpu.PrefetchScalarGridSpec(num...  5.07 us
    all_to_all x1, starting transfers between devices, body(): rows = lax.all_to_all(rows, ('y', 'co'), 0, 0, tiled=True)  4.22 us
  transfers between devices with their start and end apart: 25, of which 13 were waited for; matrix products, arithmetic and copies ran while one was open for 4% of the time, Pallas kernels for 20%

profile of v3, /device:TPU:1, one launch (start us, length us, event | category | flops | bytes accessed | tf_op | source)
XLA Modules:
  0.0 158.3 jit_solution(15045838691647881340)
XLA Ops:
  0.0 3.8 %collective-permute-start = (f32[256,128]{1,0:T(8,128)}, f32[256,128]{1,0:T(8,128)S(1)}, u32[]{:S(2)}, u32[]{:S(2)}) collective-permute-start(f32[256,128]{1,0:T(8,128)} %bitcast.32), channel_id=1, source_target_pairs={{0,64},{64,128},{128,192},{192,0},{1,65},{65,129},{129,193},{193,1... | collective-permute-start | bytes 393224 | tf_op jit(solution)/shard_map/ppermute | solution.py:340
  3.8 5.1 %collective-permute-start.1 = (f32[256,128]{1,0:T(8,128)}, f32[256,128]{1,0:T(8,128)S(1)}, u32[]{:S(2)}, u32[]{:S(2)}) collective-permute-start(f32[256,128]{1,0:T(8,128)} %bitcast.33), channel_id=1, source_target_pairs={{0,128},{64,192},{128,0},{192,64},{1,129},{65,193},{129,1},{193,65... | collective-permute-start | bytes 393224 | tf_op jit(solution)/shard_map/ppermute | solution.py:340
  8.9 2.4 %collective-permute-start.2 = (f32[256,128]{1,0:T(8,128)}, f32[256,128]{1,0:T(8,128)S(1)}, u32[]{:S(2)}, u32[]{:S(2)}) collective-permute-start(f32[256,128]{1,0:T(8,128)} %bitcast.34), channel_id=1, source_target_pairs={{0,192},{64,0},{128,64},{192,128},{1,193},{65,1},{129,65},{193,129... | collective-permute-start | bytes 393224 | tf_op jit(solution)/shard_map/ppermute | solution.py:340
  11.3 0.7 broadcast_in_dim.4
  12.0 9.9 %all_to_all.15 = f32[8,8,128]{2,1,0:T(8,128)S(1)} all-to-all(f32[8,8,128]{2,1,0:T(8,128)S(1)} %broadcast_in_dim.4), channel_id=1, replica_groups=mesh['zh'=4,'y'=4,'co'=2,'zl'=2,'x'=4] {'zl','x'}, dimensions={0} | all-to-all | bytes 65536 | tf_op jit(solution)/shard_map/all_to_all | solution.py:358
  22.0 1.1 collective-permute-start.3
  23.1 4.1 %collective-permute-start.4 = (f32[8,8,128]{2,1,0:T(8,128)S(1)}, f32[8,8,128]{2,1,0:T(8,128)S(1)}, u32[]{:S(2)}, u32[]{:S(2)}) collective-permute-start(f32[8,8,128]{2,1,0:T(8,128)S(1)} %all_to_all.15), channel_id=1, source_target_pairs={{0,128},{64,192},{128,0},{192,64},{1,129},{65,193},{129,1},{193,65... | collective-permute-start | bytes 98312 | tf_op jit(solution)/shard_map/ppermute | solution.py:340
  27.2 2.0 %collective-permute-start.5 = (f32[8,8,128]{2,1,0:T(8,128)S(1)}, f32[8,8,128]{2,1,0:T(8,128)S(1)}, u32[]{:S(2)}, u32[]{:S(2)}) collective-permute-start(f32[8,8,128]{2,1,0:T(8,128)S(1)} %all_to_all.15), channel_id=1, source_target_pairs={{0,192},{64,0},{128,64},{192,128},{1,193},{65,1},{129,65},{193,129... | collective-permute-start | bytes 98312 | tf_op jit(solution)/shard_map/ppermute | solution.py:340
  29.2 0.6 collective-permute-done.4
  29.8 1.4 collective-permute-done.5
  31.1 1.4 collective-permute-start.6
  32.5 2.6 %collective-permute-start.7 = (f32[4,8,8,128]{3,2,1,0:T(8,128)S(1)}, f32[4,8,8,128]{3,2,1,0:T(8,128)S(1)}, u32[]{:S(2)}, u32[]{:S(2)}) collective-permute-start(f32[4,8,8,128]{3,2,1,0:T(8,128)S(1)} %get-tuple-element.40), channel_id=1, source_target_pairs={{0,32},{16,48},{32,0},{48,16},{1,33},{17,49},{33,1},{49,17},{2,34}... | collective-permute-start | bytes 393224 | tf_op jit(solution)/shard_map/ppermute | solution.py:340
  35.1 1.1 collective-permute-start.8
  36.3 2.6 %collective-permute-done.7 = f32[4,8,8,128]{3,2,1,0:T(8,128)S(1)} collective-permute-done((f32[4,8,8,128]{3,2,1,0:T(8,128)S(1)}, f32[4,8,8,128]{3,2,1,0:T(8,128)S(1)}, u32[]{:S(2)}, u32[]{:S(2)}) %collective-permute-start.7) | collective-permute-done | bytes 131104 | tf_op jit(solution)/shard_map/ppermute | solution.py:340
  38.9 0.3 collective-permute-done.8
  39.3 4.7 %collective-permute-start.9 = (f32[4,4,8,8,128]{4,3,2,1,0:T(8,128)S(1)}, f32[4,4,8,8,128]{4,3,2,1,0:T(8,128)S(1)}, u32[]{:S(2)}, u32[]{:S(2)}) collective-permute-start(f32[4,4,8,8,128]{4,3,2,1,0:T(8,128)S(1)} %pad_maximum_fusion.refs_0_), channel_id=1, source_target_pairs={{0,8},{8,0},{1,9},{9,1},{2,10},{10,2},{3,11},{11,3},{4,12},{12,4},... | collective-permute-start | bytes 1572872 | tf_op jit(solution)/shard_map/ppermute | solution.py:340
  44.0 0.6 stack.62.pos
  44.5 1.0 collective-permute-done.9.refs_1_
  45.5 0.8 copy-done.8
  46.3 11.6 %pair_transform.1 = (bf16[8,4,16,256]{3,2,1,0:T(8,128)(2,1)}, bf16[1664,256]{1,0:T(8,128)(2,1)}) custom-call(s32[5]{0:T(128)} %stack.62.pos, f32[4,4,8,8,128]{4,3,2,1,0:T(8,128)} %copy-done.3, f32[4,4,8,8,128]{4,3,2,1,0:T(8,128)} %copy-done.8, f32[256,128]{1,0:T(8,128)} %bitcast.35, f32[256,128]{1,0:T(8,128)} %copy-done.9, f32[256,128]{1,0:T(8,128)} %copy-done.10, ...), custom_call_target="tpu_custom_call" | custom-call | flops 8000000000 | bytes 6291456 | tf_op jit(solution)/shard_map/pair_transform/pallas_call | solution.py:211
  57.9 4.2 %all-to-all-start.2 = ((bf16[8,4,16,256]{3,2,1,0:T(8,128)(2,1)}), bf16[8,4,16,256]{3,2,1,0:T(8,128)(2,1)S(1)}, u32[]{:S(2)}, u32[]{:S(2)}) async-start(bf16[8,4,16,256]{3,2,1,0:T(8,128)(2,1)} %get-tuple-element.28), calls=%async_computation.2 | async-start | bytes 524288 | tf_op jit(solution)/shard_map/all_to_all | solution.py:365
  62.1 10.1 %column_pairs.1 = bf16[8,4,16,640]{3,2,1,0:T(8,128)(2,1)} custom-call(s32[5]{0:T(128)} %stack.62.pos, bf16[1664,256]{1,0:T(8,128)(2,1)} %get-tuple-element.27.refs_0_, s32[256,1]{1,0:T(8,128)} %constant.40.clone.refs_10_.refs_1_, s32[8,1,640]{2,1,0:T(1,128)} %constant.41.clone.refs_2_, s32[8,1,640]{2,1,0:T(1,128)} %constant.42.clone.refs_3_), custom_call_target="tpu_custom_call" | custom-call | flops 8000000000 | bytes 2097152 | tf_op jit(solution)/shard_map/column_pairs/pallas_call | solution.py:226
  72.2 3.6 %all-to-all-start.1 = ((bf16[8,4,16,640]{3,2,1,0:T(8,128)(2,1)}), bf16[8,4,16,640]{3,2,1,0:T(8,128)(2,1)S(1)}, u32[]{:S(2)}, u32[]{:S(2)}) async-start(bf16[8,4,16,640]{3,2,1,0:T(8,128)(2,1)} %column_pairs.1), calls=%async_computation.1 | async-start | bytes 1310720 | tf_op jit(solution)/shard_map/all_to_all | solution.py:366
  75.8 1.4 collective-permute-start.15
  77.2 13.8 %collective-permute-done.15 = bf16[8,4,16,256]{3,2,1,0:T(8,128)(2,1)S(1)} collective-permute-done((bf16[8,4,16,256]{3,2,1,0:T(8,128)(2,1)S(1)}, bf16[8,4,16,256]{3,2,1,0:T(8,128)(2,1)S(1)}, u32[]{:S(2)}, u32[]{:S(2)}) %collective-permute-start.15) | collective-permute-done | bytes 262176 | tf_op jit(solution)/shard_map/ppermute | solution.py:340
  91.0 2.6 %collective-permute-start.17 = (bf16[2,4,2,4,16,256]{5,4,3,2,1,0:T(8,128)(2,1)S(1)}, bf16[2,4,2,4,16,256]{5,4,3,2,1,0:T(8,128)(2,1)S(1)}, u32[]{:S(2)}, u32[]{:S(2)}) collective-permute-start(bf16[2,4,2,4,16,256]{5,4,3,2,1,0:T(8,128)(2,1)S(1)} %pad_maximum_fusion.1.r0), channel_id=1, source_target_pairs={{0,3},{1,0},{2,1},{3,2},{4,7},{5,4},{6,5},{7,6},{8,11},{9,8},{10,9... | collective-permute-start | bytes 1572872 | tf_op jit(solution)/shard_map/ppermute | solution.py:340
  93.6 2.0 %collective-permute-start.10 = (bf16[8,4,16,640]{3,2,1,0:T(8,128)(2,1)S(1)}, bf16[8,4,16,640]{3,2,1,0:T(8,128)(2,1)S(1)}, u32[]{:S(2)}, u32[]{:S(2)}) collective-permute-start(bf16[8,4,16,640]{3,2,1,0:T(8,128)(2,1)S(1)} %all-to-all-done.1.mine), channel_id=1, source_target_pairs={{0,48},{16,0},{32,16},{48,32},{1,49},{17,1},{33,17},{49,33},{2,50}... | collective-permute-start | bytes 1966088 | tf_op jit(solution)/shard_map/ppermute | solution.py:340
  95.7 8.4 %collective-permute-done.17.r3 = bf16[2,4,2,4,16,256]{5,4,3,2,1,0:T(8,128)(2,1)S(1)} collective-permute-done((bf16[2,4,2,4,16,256]{5,4,3,2,1,0:T(8,128)(2,1)S(1)}, bf16[2,4,2,4,16,256]{5,4,3,2,1,0:T(8,128)(2,1)S(1)}, u32[]{:S(2)}, u32[]{:S(2)}) %collective-permute-start.17) | collective-permute-done | bytes 524320 | tf_op jit(solution)/shard_map/ppermute | solution.py:340
  104.1 3.5 %collective-permute-start.18 = (bf16[1,4,2,4,16,256]{5,4,3,2,1,0:T(8,128)(2,1)S(1)}, bf16[1,4,2,4,16,256]{5,4,3,2,1,0:T(8,128)(2,1)S(1)}, u32[]{:S(2)}, u32[]{:S(2)}) collective-permute-start(bf16[1,4,2,4,16,256]{5,4,3,2,1,0:T(8,128)(2,1)S(1)} %slice.18), channel_id=1, source_target_pairs={{0,3},{1,0},{2,1},{3,2},{4,7},{5,4},{6,5},{7,6},{8,11},{9,8},{10,9... | collective-permute-start | bytes 786440 | tf_op jit(solution)/shard_map/ppermute | solution.py:340
  107.7 3.8 %collective-permute-done.18 = bf16[1,4,2,4,16,256]{5,4,3,2,1,0:T(8,128)(2,1)S(1)} collective-permute-done((bf16[1,4,2,4,16,256]{5,4,3,2,1,0:T(8,128)(2,1)S(1)}, bf16[1,4,2,4,16,256]{5,4,3,2,1,0:T(8,128)(2,1)S(1)}, u32[]{:S(2)}, u32[]{:S(2)}) %collective-permute-start.18) | collective-permute-done | bytes 262176 | tf_op jit(solution)/shard_map/ppermute | solution.py:340
  111.5 3.2 %collective-permute-done.19 = bf16[1,4,2,4,16,256]{5,4,3,2,1,0:T(8,128)(2,1)S(1)} collective-permute-done((bf16[1,4,2,4,16,256]{5,4,3,2,1,0:T(8,128)(2,1)S(1)}, bf16[1,4,2,4,16,256]{5,4,3,2,1,0:T(8,128)(2,1)S(1)}, u32[]{:S(2)}, u32[]{:S(2)}) %collective-permute-start.19) | collective-permute-done | bytes 262176 | tf_op jit(solution)/shard_map/ppermute | solution.py:340
  114.7 0.9 pad_maximum_fusion.2.r2
  115.6 3.0 %collective-permute-start.22 = (bf16[8,4,16,640]{3,2,1,0:T(8,128)(2,1)S(1)}, bf16[8,4,16,640]{3,2,1,0:T(8,128)(2,1)S(1)}, u32[]{:S(2)}, u32[]{:S(2)}) collective-permute-start(bf16[8,4,16,640]{3,2,1,0:T(8,128)(2,1)S(1)} %all-to-all-done.1.mine), channel_id=1, source_target_pairs={{0,8},{8,0},{1,9},{9,1},{2,10},{10,2},{3,11},{11,3},{4,12},{12,4},... | collective-permute-start | bytes 1966088 | tf_op jit(solution)/shard_map/ppermute | solution.py:340
  118.6 0.7 slice.16
  119.3 1.7 %collective-permute-start.11 = (bf16[4,4,16,640]{3,2,1,0:T(8,128)(2,1)}, bf16[4,4,16,640]{3,2,1,0:T(8,128)(2,1)}, u32[]{:S(2)}, u32[]{:S(2)}) collective-permute-start(bf16[4,4,16,640]{3,2,1,0:T(8,128)(2,1)} %slice.16), channel_id=1, source_target_pairs={{0,48},{16,0},{32,16},{48,32},{1,49},{17,1},{33,17},{49,33},{2,50}... | collective-permute-start | bytes 983048 | tf_op jit(solution)/shard_map/ppermute | solution.py:340
  121.3 0.8 slice.17
  122.3 0.4 reshape.34.gap
  122.7 0.5 collective-permute-start.21
  123.3 5.1 %scaled_rows.1 = (bf16[4,1536,1024]{2,1,0:T(8,128)(2,1)S(1)}, bf16[640,1024]{1,0:T(8,128)(2,1)S(1)}, f32[16,1024]{1,0:T(8,128)S(1)}) custom-call(s32[5]{0:T(128)S(1)} %copy-done, f32[6]{0:T(128)S(1)} %copy-done.1, bf16[2,4,2,4,16,256]{5,4,3,2,1,0:T(8,128)(2,1)} %copy-done.2, bf16[2,4,2,4,16,256]{5,4,3,2,1,0:T(8,128)(2,1)} %copy-done.5, ...), custom_call_target="tpu_custom_call" | custom-call | flops 1000000000 | bytes 20971520 | tf_op jit(solution)/shard_map/scaled_rows/pallas_call | solution.py:277
  128.4 0.6 collective-permute-done.11
  129.0 1.0 constant_dynamic-update-slice_fusion.1
  130.0 2.6 %collective-permute-done.13 = bf16[4,4,16,640]{3,2,1,0:T(8,128)(2,1)} collective-permute-done((bf16[4,4,16,640]{3,2,1,0:T(8,128)(2,1)}, bf16[4,4,16,640]{3,2,1,0:T(8,128)(2,1)}, u32[]{:S(2)}, u32[]{:S(2)}) %collective-permute-start.13) | collective-permute-done | bytes 327712 | tf_op jit(solution)/shard_map/ppermute | solution.py:340
  132.6 1.0 constant_dynamic-update-slice_fusion.mine
  133.6 1.4 collective-permute-start.14
  135.1 5.1 %response_product.4.refs_0_ = f32[6,256,1024]{2,1,0:T(8,128)S(1)} custom-call(bf16[8,4,16,640]{3,2,1,0:T(8,128)(2,1)S(1)} %all-to-all-done.1.mine, bf16[8,4,16,640]{3,2,1,0:T(8,128)(2,1)S(1)} %collective-permute-done.22.theirs, bf16[4,1536,1024]{2,1,0:T(8,128)(2,1)S(1)} %get-tuple-element.33.scaled, bf16[640,1024]{1,0:T(8,128)(2,1)S(1)} %get-tuple-element.34.hot, ...), custom_call_target="tpu_custom_call" | custom-call | flops 4600000000 | bytes 10485760 | tf_op jit(solution)/shard_map/response_product/pallas_call | solution.py:324
  140.2 5.5 %response_product.5.refs_0_ = f32[6,256,1024]{2,1,0:T(8,128)S(1)} custom-call(bf16[8,4,16,640]{3,2,1,0:T(8,128)(2,1)S(1)} %collective-permute-done.12.mine, bf16[8,4,16,640]{3,2,1,0:T(8,128)(2,1)S(1)} %collective-permute-done.21.theirs, bf16[4,1536,1024]{2,1,0:T(8,128)(2,1)S(1)} %get-tuple-element.33.scaled, ...), custom_call_target="tpu_custom_call", output_to_operand_aliasing={{}: (5, {})} | custom-call | flops 4600000000 | bytes 10485760 | tf_op jit(solution)/shard_map/response_product/pallas_call | solution.py:324
  145.7 5.5 %response_product.6.refs_0_ = f32[6,256,1024]{2,1,0:T(8,128)S(1)} custom-call(bf16[8,4,16,640]{3,2,1,0:T(8,128)(2,1)S(1)} %collective-permute-done.10.mine, bf16[8,4,16,640]{3,2,1,0:T(8,128)(2,1)S(1)} %collective-permute-done.20.theirs, bf16[4,1536,1024]{2,1,0:T(8,128)(2,1)S(1)} %get-tuple-element.33.scaled, ...), custom_call_target="tpu_custom_call", output_to_operand_aliasing={{}: (5, {})} | custom-call | flops 4600000000 | bytes 10485760 | tf_op jit(solution)/shard_map/response_product/pallas_call | solution.py:324
  151.2 7.2 %response_product.7 = f32[6,256,1024]{2,1,0:T(8,128)} custom-call(bf16[8,4,16,640]{3,2,1,0:T(8,128)(2,1)S(1)} %constant_dynamic-update-slice_fusion.mine, bf16[8,4,16,640]{3,2,1,0:T(8,128)(2,1)S(1)} %collective-permute-done.14.theirs, bf16[4,1536,1024]{2,1,0:T(8,128)(2,1)S(1)} %get-tuple-element.33.scaled, bf16[640,1024]{1,0:T(8,128)(2,1)S(1)} %get-tuple-element.34.hot, ...), custom_call_target="tpu_custom_call" | custom-call | flops 4600000000 | bytes 10485760 | tf_op jit(solution)/shard_map/response_product/pallas_call | solution.py:324
  (52 shorter events, 1.1 us)
Async XLA Ops:
  0.0 21.9 %collective-permute-start = (f32[256,128]{1,0:T(8,128)}, f32[256,128]{1,0:T(8,128)S(1)}, u32[]{:S(2)}, u32[]{:S(2)}) collective-permute-start(f32[256,128]{1,0:T(8,128)} %bitcast.32), channel_id=1, source_target_pairs={{0,64},{64,128},{128,192},{192,0},{1,65},{65,129},{129,193},{193,1... | collective-permute-start | bytes 393224 | tf_op jit(solution)/shard_map/ppermute | solution.py:340
  3.8 18.1 %collective-permute-start.1 = (f32[256,128]{1,0:T(8,128)}, f32[256,128]{1,0:T(8,128)S(1)}, u32[]{:S(2)}, u32[]{:S(2)}) collective-permute-start(f32[256,128]{1,0:T(8,128)} %bitcast.33), channel_id=1, source_target_pairs={{0,128},{64,192},{128,0},{192,64},{1,129},{65,193},{129,1},{193,65... | collective-permute-start | bytes 393224 | tf_op jit(solution)/shard_map/ppermute | solution.py:340
  8.9 13.0 %collective-permute-start.2 = (f32[256,128]{1,0:T(8,128)}, f32[256,128]{1,0:T(8,128)S(1)}, u32[]{:S(2)}, u32[]{:S(2)}) collective-permute-start(f32[256,128]{1,0:T(8,128)} %bitcast.34), channel_id=1, source_target_pairs={{0,192},{64,0},{128,64},{192,128},{1,193},{65,1},{129,65},{193,129... | collective-permute-start | bytes 393224 | tf_op jit(solution)/shard_map/ppermute | solution.py:340
  21.9 23.6 %copy-start.9 = (f32[256,128]{1,0:T(8,128)}, f32[256,128]{1,0:T(8,128)S(1)}, u32[]{:S(2)}) copy-start(f32[256,128]{1,0:T(8,128)S(1)} %collective-permute-done.refs_3_) | copy-start | bytes 393220
  21.9 23.6 %copy-start.10 = (f32[256,128]{1,0:T(8,128)}, f32[256,128]{1,0:T(8,128)S(1)}, u32[]{:S(2)}) copy-start(f32[256,128]{1,0:T(8,128)S(1)} %collective-permute-done.1.refs_4_) | copy-start | bytes 393220
  22.0 23.5 %copy-start.11 = (f32[256,128]{1,0:T(8,128)}, f32[256,128]{1,0:T(8,128)S(1)}, u32[]{:S(2)}) copy-start(f32[256,128]{1,0:T(8,128)S(1)} %collective-permute-done.2.refs_5_) | copy-start | bytes 393220
  22.0 7.2 %collective-permute-start.3 = (f32[8,8,128]{2,1,0:T(8,128)S(1)}, f32[8,8,128]{2,1,0:T(8,128)S(1)}, u32[]{:S(2)}, u32[]{:S(2)}) collective-permute-start(f32[8,8,128]{2,1,0:T(8,128)S(1)} %all_to_all.15), channel_id=1, source_target_pairs={{0,64},{64,128},{128,192},{192,0},{1,65},{65,129},{129,193},{193,1... | collective-permute-start | bytes 98312 | tf_op jit(solution)/shard_map/ppermute | solution.py:340
  23.1 6.7 %collective-permute-start.4 = (f32[8,8,128]{2,1,0:T(8,128)S(1)}, f32[8,8,128]{2,1,0:T(8,128)S(1)}, u32[]{:S(2)}, u32[]{:S(2)}) collective-permute-start(f32[8,8,128]{2,1,0:T(8,128)S(1)} %all_to_all.15), channel_id=1, source_target_pairs={{0,128},{64,192},{128,0},{192,64},{1,129},{65,193},{129,1},{193,65... | collective-permute-start | bytes 98312 | tf_op jit(solution)/shard_map/ppermute | solution.py:340
  27.2 3.9 %collective-permute-start.5 = (f32[8,8,128]{2,1,0:T(8,128)S(1)}, f32[8,8,128]{2,1,0:T(8,128)S(1)}, u32[]{:S(2)}, u32[]{:S(2)}) collective-permute-start(f32[8,8,128]{2,1,0:T(8,128)S(1)} %all_to_all.15), channel_id=1, source_target_pairs={{0,192},{64,0},{128,64},{192,128},{1,193},{65,1},{129,65},{193,129... | collective-permute-start | bytes 98312 | tf_op jit(solution)/shard_map/ppermute | solution.py:340
  31.1 5.2 %collective-permute-start.6 = (f32[4,8,8,128]{3,2,1,0:T(8,128)S(1)}, f32[4,8,8,128]{3,2,1,0:T(8,128)S(1)}, u32[]{:S(2)}, u32[]{:S(2)}) collective-permute-start(f32[4,8,8,128]{3,2,1,0:T(8,128)S(1)} %get-tuple-element.40), channel_id=1, source_target_pairs={{0,16},{16,32},{32,48},{48,0},{1,17},{17,33},{33,49},{49,1},{2,18}... | collective-permute-start | bytes 393224 | tf_op jit(solution)/shard_map/ppermute | solution.py:340
  32.5 6.4 %collective-permute-start.7 = (f32[4,8,8,128]{3,2,1,0:T(8,128)S(1)}, f32[4,8,8,128]{3,2,1,0:T(8,128)S(1)}, u32[]{:S(2)}, u32[]{:S(2)}) collective-permute-start(f32[4,8,8,128]{3,2,1,0:T(8,128)S(1)} %get-tuple-element.40), channel_id=1, source_target_pairs={{0,32},{16,48},{32,0},{48,16},{1,33},{17,49},{33,1},{49,17},{2,34}... | collective-permute-start | bytes 393224 | tf_op jit(solution)/shard_map/ppermute | solution.py:340
  35.1 4.1 %collective-permute-start.8 = (f32[4,8,8,128]{3,2,1,0:T(8,128)S(1)}, f32[4,8,8,128]{3,2,1,0:T(8,128)S(1)}, u32[]{:S(2)}, u32[]{:S(2)}) collective-permute-start(f32[4,8,8,128]{3,2,1,0:T(8,128)S(1)} %get-tuple-element.40), channel_id=1, source_target_pairs={{0,48},{16,0},{32,16},{48,32},{1,49},{17,1},{33,17},{49,33},{2,50}... | collective-permute-start | bytes 393224 | tf_op jit(solution)/shard_map/ppermute | solution.py:340
  39.3 6.2 %copy-start.3 = (f32[4,4,8,8,128]{4,3,2,1,0:T(8,128)}, f32[4,4,8,8,128]{4,3,2,1,0:T(8,128)S(1)}, u32[]{:S(2)}) copy-start(f32[4,4,8,8,128]{4,3,2,1,0:T(8,128)S(1)} %pad_maximum_fusion.refs_0_) | copy-start | bytes 1572868
  39.3 6.2 %collective-permute-start.9 = (f32[4,4,8,8,128]{4,3,2,1,0:T(8,128)S(1)}, f32[4,4,8,8,128]{4,3,2,1,0:T(8,128)S(1)}, u32[]{:S(2)}, u32[]{:S(2)}) collective-permute-start(f32[4,4,8,8,128]{4,3,2,1,0:T(8,128)S(1)} %pad_maximum_fusion.refs_0_), channel_id=1, source_target_pairs={{0,8},{8,0},{1,9},{9,1},{2,10},{10,2},{3,11},{11,3},{4,12},{12,4},... | collective-permute-start | bytes 1572872 | tf_op jit(solution)/shard_map/ppermute | solution.py:340
  45.5 0.8 copy-start.8
  57.9 14.3 %all-to-all-start.2 = ((bf16[8,4,16,256]{3,2,1,0:T(8,128)(2,1)}), bf16[8,4,16,256]{3,2,1,0:T(8,128)(2,1)S(1)}, u32[]{:S(2)}, u32[]{:S(2)}) async-start(bf16[8,4,16,256]{3,2,1,0:T(8,128)(2,1)} %get-tuple-element.28), calls=%async_computation.2 | async-start | bytes 524288 | tf_op jit(solution)/shard_map/all_to_all | solution.py:365
  62.1 58.9 %copy-start.6 = (f32[256]{0:T(256)S(1)}, f32[256]{0:T(256)}, u32[]{:S(2)}) copy-start(f32[256]{0:T(256)} %param.17) | copy-start | bytes 3076
  62.1 60.0 %copy-start.7 = (f32[8]{0:T(128)S(1)}, f32[8]{0:T(128)}, u32[]{:S(2)}) copy-start(f32[8]{0:T(128)} %param.16) | copy-start | bytes 100
  72.2 51.1 %copy-start = (s32[5]{0:T(128)S(1)}, s32[5]{0:T(128)}, u32[]{:S(2)}) copy-start(s32[5]{0:T(128)} %stack.62.pos) | copy-start | bytes 64
  72.2 51.1 %copy-start.1 = (f32[6]{0:T(128)S(1)}, f32[6]{0:T(128)}, u32[]{:S(2)}) copy-start(f32[6]{0:T(128)} %omega.1) | copy-start | bytes 76
  72.2 21.4 %all-to-all-start.1 = ((bf16[8,4,16,640]{3,2,1,0:T(8,128)(2,1)}), bf16[8,4,16,640]{3,2,1,0:T(8,128)(2,1)S(1)}, u32[]{:S(2)}, u32[]{:S(2)}) async-start(bf16[8,4,16,640]{3,2,1,0:T(8,128)(2,1)} %column_pairs.1), calls=%async_computation.1 | async-start | bytes 1310720 | tf_op jit(solution)/shard_map/all_to_all | solution.py:366
  75.8 15.1 %collective-permute-start.15 = (bf16[8,4,16,256]{3,2,1,0:T(8,128)(2,1)S(1)}, bf16[8,4,16,256]{3,2,1,0:T(8,128)(2,1)S(1)}, u32[]{:S(2)}, u32[]{:S(2)}) collective-permute-start(bf16[8,4,16,256]{3,2,1,0:T(8,128)(2,1)S(1)} %all-to-all-done.2), channel_id=1, source_target_pairs={{0,4},{4,0},{1,5},{5,1},{2,6},{6,2},{3,7},{7,3},{8,12},{12,8},{9,1... | collective-permute-start | bytes 786440 | tf_op jit(solution)/shard_map/ppermute | solution.py:340
  91.0 32.3 %copy-start.2 = (bf16[2,4,2,4,16,256]{5,4,3,2,1,0:T(8,128)(2,1)}, bf16[2,4,2,4,16,256]{5,4,3,2,1,0:T(8,128)(2,1)S(1)}, u32[]{:S(2)}) copy-start(bf16[2,4,2,4,16,256]{5,4,3,2,1,0:T(8,128)(2,1)S(1)} %pad_maximum_fusion.1.r0) | copy-start | bytes 1572868
  91.0 13.1 %collective-permute-start.17 = (bf16[2,4,2,4,16,256]{5,4,3,2,1,0:T(8,128)(2,1)S(1)}, bf16[2,4,2,4,16,256]{5,4,3,2,1,0:T(8,128)(2,1)S(1)}, u32[]{:S(2)}, u32[]{:S(2)}) collective-permute-start(bf16[2,4,2,4,16,256]{5,4,3,2,1,0:T(8,128)(2,1)S(1)} %pad_maximum_fusion.1.r0), channel_id=1, source_target_pairs={{0,3},{1,0},{2,1},{3,2},{4,7},{5,4},{6,5},{7,6},{8,11},{9,8},{10,9... | collective-permute-start | bytes 1572872 | tf_op jit(solution)/shard_map/ppermute | solution.py:340
  93.6 14.0 %collective-permute-start.16 = (bf16[2,4,2,4,16,256]{5,4,3,2,1,0:T(8,128)(2,1)S(1)}, bf16[2,4,2,4,16,256]{5,4,3,2,1,0:T(8,128)(2,1)S(1)}, u32[]{:S(2)}, u32[]{:S(2)}) collective-permute-start(bf16[2,4,2,4,16,256]{5,4,3,2,1,0:T(8,128)(2,1)S(1)} %pad_maximum_fusion.1.r0), channel_id=1, source_target_pairs={{0,1},{1,2},{2,3},{3,0},{4,5},{5,6},{6,7},{7,4},{8,9},{9,10},{10,1... | collective-permute-start | bytes 1572872 | tf_op jit(solution)/shard_map/ppermute | solution.py:340
  93.6 22.0 %collective-permute-start.10 = (bf16[8,4,16,640]{3,2,1,0:T(8,128)(2,1)S(1)}, bf16[8,4,16,640]{3,2,1,0:T(8,128)(2,1)S(1)}, u32[]{:S(2)}, u32[]{:S(2)}) collective-permute-start(bf16[8,4,16,640]{3,2,1,0:T(8,128)(2,1)S(1)} %all-to-all-done.1.mine), channel_id=1, source_target_pairs={{0,48},{16,0},{32,16},{48,32},{1,49},{17,1},{33,17},{49,33},{2,50}... | collective-permute-start | bytes 1966088 | tf_op jit(solution)/shard_map/ppermute | solution.py:340
  95.7 19.9 %collective-permute-start.12 = (bf16[8,4,16,640]{3,2,1,0:T(8,128)(2,1)S(1)}, bf16[8,4,16,640]{3,2,1,0:T(8,128)(2,1)S(1)}, u32[]{:S(2)}, u32[]{:S(2)}) collective-permute-start(bf16[8,4,16,640]{3,2,1,0:T(8,128)(2,1)S(1)} %all-to-all-done.1.mine), channel_id=1, source_target_pairs={{0,16},{16,32},{32,48},{48,0},{1,17},{17,33},{33,49},{49,1},{2,18}... | collective-permute-start | bytes 1966088 | tf_op jit(solution)/shard_map/ppermute | solution.py:340
  104.1 11.5 %copy-start.4 = (bf16[2,4,2,4,16,256]{5,4,3,2,1,0:T(8,128)(2,1)}, bf16[2,4,2,4,16,256]{5,4,3,2,1,0:T(8,128)(2,1)S(1)}, u32[]{:S(2)}) copy-start(bf16[2,4,2,4,16,256]{5,4,3,2,1,0:T(8,128)(2,1)S(1)} %collective-permute-done.17.r3) | copy-start | bytes 1572868
  104.1 7.4 %collective-permute-start.18 = (bf16[1,4,2,4,16,256]{5,4,3,2,1,0:T(8,128)(2,1)S(1)}, bf16[1,4,2,4,16,256]{5,4,3,2,1,0:T(8,128)(2,1)S(1)}, u32[]{:S(2)}, u32[]{:S(2)}) collective-permute-start(bf16[1,4,2,4,16,256]{5,4,3,2,1,0:T(8,128)(2,1)S(1)} %slice.18), channel_id=1, source_target_pairs={{0,3},{1,0},{2,1},{3,2},{4,7},{5,4},{6,5},{7,6},{8,11},{9,8},{10,9... | collective-permute-start | bytes 786440 | tf_op jit(solution)/shard_map/ppermute | solution.py:340
  107.6 8.0 %copy-start.5 = (bf16[2,4,2,4,16,256]{5,4,3,2,1,0:T(8,128)(2,1)}, bf16[2,4,2,4,16,256]{5,4,3,2,1,0:T(8,128)(2,1)S(1)}, u32[]{:S(2)}) copy-start(bf16[2,4,2,4,16,256]{5,4,3,2,1,0:T(8,128)(2,1)S(1)} %collective-permute-done.16.r1) | copy-start | bytes 1572868
  107.6 7.1 %collective-permute-start.19 = (bf16[1,4,2,4,16,256]{5,4,3,2,1,0:T(8,128)(2,1)S(1)}, bf16[1,4,2,4,16,256]{5,4,3,2,1,0:T(8,128)(2,1)S(1)}, u32[]{:S(2)}, u32[]{:S(2)}) collective-permute-start(bf16[1,4,2,4,16,256]{5,4,3,2,1,0:T(8,128)(2,1)S(1)} %slice.19), channel_id=1, source_target_pairs={{0,1},{1,2},{2,3},{3,0},{4,5},{5,6},{6,7},{7,4},{8,9},{9,10},{10,1... | collective-permute-start | bytes 786440 | tf_op jit(solution)/shard_map/ppermute | solution.py:340
  115.6 19.5 %collective-permute-start.22 = (bf16[8,4,16,640]{3,2,1,0:T(8,128)(2,1)S(1)}, bf16[8,4,16,640]{3,2,1,0:T(8,128)(2,1)S(1)}, u32[]{:S(2)}, u32[]{:S(2)}) collective-permute-start(bf16[8,4,16,640]{3,2,1,0:T(8,128)(2,1)S(1)} %all-to-all-done.1.mine), channel_id=1, source_target_pairs={{0,8},{8,0},{1,9},{9,1},{2,10},{10,2},{3,11},{11,3},{4,12},{12,4},... | collective-permute-start | bytes 1966088 | tf_op jit(solution)/shard_map/ppermute | solution.py:340
  119.3 9.6 %collective-permute-start.11 = (bf16[4,4,16,640]{3,2,1,0:T(8,128)(2,1)}, bf16[4,4,16,640]{3,2,1,0:T(8,128)(2,1)}, u32[]{:S(2)}, u32[]{:S(2)}) collective-permute-start(bf16[4,4,16,640]{3,2,1,0:T(8,128)(2,1)} %slice.16), channel_id=1, source_target_pairs={{0,48},{16,0},{32,16},{48,32},{1,49},{17,1},{33,17},{49,33},{2,50}... | collective-permute-start | bytes 983048 | tf_op jit(solution)/shard_map/ppermute | solution.py:340
  122.1 10.5 %collective-permute-start.13 = (bf16[4,4,16,640]{3,2,1,0:T(8,128)(2,1)}, bf16[4,4,16,640]{3,2,1,0:T(8,128)(2,1)}, u32[]{:S(2)}, u32[]{:S(2)}) collective-permute-start(bf16[4,4,16,640]{3,2,1,0:T(8,128)(2,1)} %slice.17), channel_id=1, source_target_pairs={{0,16},{16,32},{32,48},{48,0},{1,17},{17,33},{33,49},{49,1},{2,18}... | collective-permute-start | bytes 983048 | tf_op jit(solution)/shard_map/ppermute | solution.py:340
  122.7 17.5 %collective-permute-start.21 = (bf16[8,4,16,640]{3,2,1,0:T(8,128)(2,1)S(1)}, bf16[8,4,16,640]{3,2,1,0:T(8,128)(2,1)S(1)}, u32[]{:S(2)}, u32[]{:S(2)}) collective-permute-start(bf16[8,4,16,640]{3,2,1,0:T(8,128)(2,1)S(1)} %collective-permute-done.12.mine), channel_id=1, source_target_pairs={{0,8},{8,0},{1,9},{9,1},{2,10},{10,2},{3,11},{11,3},{4,12},{12,4},... | collective-permute-start | bytes 1966088 | tf_op jit(solution)/shard_map/ppermute | solution.py:340
  123.1 22.5 %collective-permute-start.20 = (bf16[8,4,16,640]{3,2,1,0:T(8,128)(2,1)S(1)}, bf16[8,4,16,640]{3,2,1,0:T(8,128)(2,1)S(1)}, u32[]{:S(2)}, u32[]{:S(2)}) collective-permute-start(bf16[8,4,16,640]{3,2,1,0:T(8,128)(2,1)S(1)} %collective-permute-done.10.mine), channel_id=1, source_target_pairs={{0,8},{8,0},{1,9},{9,1},{2,10},{10,2},{3,11},{11,3},{4,12},{12,4},... | collective-permute-start | bytes 1966088 | tf_op jit(solution)/shard_map/ppermute | solution.py:340
  133.6 17.5 %collective-permute-start.14 = (bf16[8,4,16,640]{3,2,1,0:T(8,128)(2,1)S(1)}, bf16[8,4,16,640]{3,2,1,0:T(8,128)(2,1)S(1)}, u32[]{:S(2)}, u32[]{:S(2)}) collective-permute-start(bf16[8,4,16,640]{3,2,1,0:T(8,128)(2,1)S(1)} %constant_dynamic-update-slice_fusion.mine), channel_id=1, source_target_pairs={{0,8},{8,0},{1,9},{9,1},{2,10},{10,2},{3,11},{11,3},{4,12},{12,4},... | collective-permute-start | bytes 1966088 | tf_op jit(solution)/shard_map/ppermute | solution.py:340

commit v4 on v3

--- a/solution.py
+++ b/solution.py
@@ -1,3 +1,5 @@
+import functools
+
 import jax
 import jax.numpy as jnp
 import ml_dtypes
@@ -119,20 +121,20 @@
     return copies
 
 
-def column_kernel(pos, *refs):
-    cols = refs[4]
-    spectrum, key, col_key, col_kx = refs[5:9]
-    for copy in fetch(refs[:4], refs[5:9], refs[9]):
+def column_kernel(first, count, pos, *refs):
+    cols = refs[-6]
+    spectrum, key, col_key, col_kx = refs[-5:-1]
+    for copy in fetch(refs[:4], refs[-5:-1], refs[-1]):
         copy.wait()
 
     def columns(j, carry):
         def store(at, real, imag):
             cols[j, at] = jnp.concatenate([real, imag], axis=0).astype(BF)
 
-        picked(spectrum, key, col_key[j], col_kx[j], pos[0], store)
+        picked(spectrum, key, col_key[first + j], col_kx[first + j], pos[0], store)
         return carry
 
-    lax.fori_loop(0, 8, columns, 0)
+    lax.fori_loop(0, count, columns, 0)
 
 
 def transform_kernel(pos, *refs):
@@ -202,7 +204,7 @@
 
 
 def transform(pos, own, other, bands, gmap):
-    wave_hi, wave_lo, along_hi, along_lo, key, col_key, col_kx, _ = (jnp.asarray(t) for t in tables())
+    wave_hi, wave_lo, along_hi, along_lo, key = (jnp.asarray(t) for t in tables()[:5])
     gmap = gmap.reshape(16, 1, 512)
     operands = [own, other, *bands, wave_hi, wave_lo, along_hi, along_lo, key, gmap]
     anywhere = pl.BlockSpec(memory_space=pl.ANY)
@@ -223,22 +225,28 @@
         cost_estimate=pl.CostEstimate(flops=8 * 10**9, transcendentals=0, bytes_accessed=6 * 2**20),
         name="pair_transform",
     )(pos, *operands)
-    cols = pl.pallas_call(
-        column_kernel,
+    return rows, spectrum
+
+
+def column_pairs(pos, spectrum, first, count, earlier):
+    key, col_key, col_kx = (jnp.asarray(t) for t in tables()[4:7])
+    in_hbm = pl.BlockSpec(memory_space=pltpu.HBM)
+    operands = [spectrum, key, col_key, col_kx] + ([] if earlier is None else [earlier])
+    return pl.pallas_call(
+        functools.partial(column_kernel, first, count),
         grid_spec=pltpu.PrefetchScalarGridSpec(
             num_scalar_prefetch=1,
             grid=(1,),
-            in_specs=[in_hbm] * 4,
-            out_specs=whole(np.zeros((8, 4, 16, CAN))),
-            scratch_shapes=[pltpu.VMEM(v.shape, v.dtype) for v in (spectrum, key, col_key, col_kx)]
-            + [pltpu.SemaphoreType.DMA((4,))],
+            in_specs=[in_hbm] * len(operands),
+            out_specs=pl.BlockSpec((count, 4, 16, CAN), lambda i, pos: (first // count, 0, 0, 0)),
+            scratch_shapes=[pltpu.VMEM(v.shape, v.dtype) for v in operands[:4]] + [pltpu.SemaphoreType.DMA((4,))],
         ),
         out_shape=jax.ShapeDtypeStruct((8, 4, 16, CAN), BF),
+        input_output_aliases={} if earlier is None else {5: 0},
         compiler_params=pltpu.CompilerParams(vmem_limit_bytes=60 << 20),
-        cost_estimate=pl.CostEstimate(flops=8 * 10**9, transcendentals=0, bytes_accessed=2 * 2**20),
+        cost_estimate=pl.CostEstimate(flops=count * 10**9, transcendentals=0, bytes_accessed=2 * 2**20),
         name="column_pairs",
-    )(pos, spectrum, key, col_key, col_kx)
-    return cols, rows
+    )(pos, *operands)
 
 
 def prepare_kernel(pos, omega, r0, r1, r2, r3, gap, gmap, ident, scaled, hot, sign, row_k):
@@ -357,31 +365,31 @@
     bands = around(conduction.reshape(256, 128), "zh")
     own = lax.all_to_all(jnp.broadcast_to(valence, (8, *valence.shape)), NARROW, 0, 0, tiled=True)
     own, bands = lax.optimization_barrier((own, bands))
-    for axis in ("zh", "y"):
-        own = jnp.stack(around(own, axis))
+    own = jnp.stack(around(own, "zh"))
+    ec = jnp.transpose(eps_cond.reshape(4, 4, 2, 8), (1, 2, 3, 0)).reshape(4, 2, 32, 1, 1)
+    gap = jnp.broadcast_to(ec - eps_val, (4, 2, 32, 2, 8)).reshape(4, 2, 1, 512)
+    own, gap = lax.optimization_barrier((own, gap))
+    own = jnp.stack(around(own, "y"))
     other = shifted(own, "co", 1)
-    cols, rows = transform(pos, own, other, bands, gmap)
+    rows, spectrum = transform(pos, own, other, bands, gmap)
 
     rows = lax.all_to_all(rows, ("y", "co"), 0, 0, tiled=True)
+    cols = column_pairs(pos, spectrum, 0, 8, None)
+    rows = jnp.stack(around(rows, "zl")).reshape(2, 4, 2, 4, 16, 256)
+    cols, rows = lax.optimization_barrier((cols, rows))
     cols = lax.all_to_all(cols, NARROW, 0, 0, tiled=True)
-    cols = ring(cols, "y")
-    far_cols = cols.pop(2)
-    rows = jnp.stack(around(rows, "zl")).reshape(2, 4, 2, 4, 16, 256)
     rows = ring(rows, "x")
     rows[2] = jnp.concatenate(rows[2])
-
-    rows, cols = lax.optimization_barrier((rows, cols))
-    ec = jnp.transpose(eps_cond.reshape(4, 4, 2, 8), (1, 2, 3, 0)).reshape(4, 2, 32, 1, 1)
-    gap = jnp.broadcast_to(ec - eps_val, (4, 2, 32, 2, 8)).reshape(4, 2, 1, 512)
     ident = jnp.asarray(tables()[-1])
+    behind, ahead = shifted(cols, "y", 1), shifted(cols, "y", 3)
     scaled, hot, sign = prepare(pos, omega, rows, gap, gmap, ident)
-    total = None
-    for sy, mine in zip((0, 1, 3), cols):
+    total = product_step(0, cols, shifted(cols, "co", 1), scaled, hot, sign, None, False)
+    total, behind, ahead = lax.optimization_barrier((total, behind, ahead))
+    far = jnp.concatenate([shifted(ahead[:4], "y", 3), shifted(behind[4:], "y", 1)])
+    for sy, mine in ((1, behind), (3, ahead), (2, far)):
         theirs = shifted(mine, "co", 1)
-        total = product_step(sy, mine, theirs, scaled, hot, sign, total, False)
-    mine = jnp.concatenate(far_cols)
-    theirs = shifted(mine, "co", 1)
-    return product_step(2, mine, theirs, scaled, hot, sign, total, True)
+        total = product_step(sy, mine, theirs, scaled, hot, sign, total, sy == 2)
+    return total
 
 
 def solution(mesh):

time: 159 us -> 158 us (level)
  local copies, waits for them, and re-layouts: 6.45 us -> 4.37 us
    ppermute x23, waiting for transfers between devices: 38.5 us -> 27 us  [shifted(): lax.ppermute(value, axis, [(i, (i + shift) % size) for i in range(size)])]
    all_to_all x1, waiting for transfers between devices: 0.01 us -> 6.35 us  [body(): lax.all_to_all(jnp.broadcast_to(valence, (8, *valence.shape)), NARROW, 0,...]
    all_to_all x1, waiting for transfers between devices: 0.01 us -> 5.58 us  [body(): cols = lax.all_to_all(cols, NARROW, 0, 0, tiled=True)]
    ppermute x23, starting transfers between devices: 44.5 us -> 42.9 us  [shifted(): lax.ppermute(value, axis, [(i, (i + shift) % size) for i in range(size)])]
  transfers between devices with their start and end apart: 25 -> 25, of which waited for: 13 -> 13; matrix products, arithmetic and copies ran while one was open for 4% -> 3% of each run, Pallas kernels for 20% -> 20%
where the time goes in v4:
time: 158 us
  starting transfers between devices  51.8 us (33%)
  Pallas kernels  49.7 us (31%)
  waiting for transfers between devices  38.9 us (25%)
  blocking collectives  10.7 us (7%)
  local copies, waits for them, and re-layouts  4.37 us (3%)
  other arithmetic  1.69 us (1%)
    ppermute x23, starting transfers between devices, shifted(): lax.ppermute(value, axis, [(i, (i + shift) % size) for i in range(size)])  42.9 us
    ppermute x23, waiting for transfers between devices, shifted(): lax.ppermute(value, axis, [(i, (i + shift) % size) for i in range(size)])  27 us
    pallas_call x4, Pallas kernels, product_step(): pl.pallas_call(kernel, grid=(4 if last else 1,), in_specs=[resident()] *...  23 us
    pallas_call x1, Pallas kernels, transform(): pl.pallas_call(transform_kernel, grid_spec=pltpu.PrefetchScalarGridSpec(n...  11.6 us
    all_to_all x1, blocking collectives, body(): rows = lax.all_to_all(rows, ('y', 'co'), 0, 0, tiled=True)  10.7 us
    pallas_call x1, Pallas kernels, column_pairs(): pl.pallas_call(functools.partial(column_kernel, first, count), grid_spec=...  10.1 us
    all_to_all x1, waiting for transfers between devices, body(): lax.all_to_all(jnp.broadcast_to(valence, (8, *valence.shape)), NARROW, 0,...  6.35 us
    all_to_all x1, waiting for transfers between devices, body(): cols = lax.all_to_all(cols, NARROW, 0, 0, tiled=True)  5.58 us
  transfers between devices with their start and end apart: 25, of which 13 were waited for; matrix products, arithmetic and copies ran while one was open for 3% of the time, Pallas kernels for 20%

profile of v4, /device:TPU:1, one launch (start us, length us, event | category | flops | bytes accessed | tf_op | source)
XLA Modules:
  0.0 157.5 jit_solution(3276249535157586085)
XLA Ops:
  0.0 3.8 %collective-permute-start = (f32[256,128]{1,0:T(8,128)}, f32[256,128]{1,0:T(8,128)S(1)}, u32[]{:S(2)}, u32[]{:S(2)}) collective-permute-start(f32[256,128]{1,0:T(8,128)} %bitcast.32), channel_id=1, source_target_pairs={{0,64},{64,128},{128,192},{192,0},{1,65},{65,129},{129,193},{193,1... | collective-permute-start | bytes 393224 | tf_op jit(solution)/shard_map/ppermute | solution.py:348
  3.8 5.1 %collective-permute-start.1 = (f32[256,128]{1,0:T(8,128)}, f32[256,128]{1,0:T(8,128)S(1)}, u32[]{:S(2)}, u32[]{:S(2)}) collective-permute-start(f32[256,128]{1,0:T(8,128)} %bitcast.33), channel_id=1, source_target_pairs={{0,128},{64,192},{128,0},{192,64},{1,129},{65,193},{129,1},{193,65... | collective-permute-start | bytes 393224 | tf_op jit(solution)/shard_map/ppermute | solution.py:348
  8.9 2.4 %collective-permute-start.2 = (f32[256,128]{1,0:T(8,128)}, f32[256,128]{1,0:T(8,128)S(1)}, u32[]{:S(2)}, u32[]{:S(2)}) collective-permute-start(f32[256,128]{1,0:T(8,128)} %bitcast.34), channel_id=1, source_target_pairs={{0,192},{64,0},{128,64},{192,128},{1,193},{65,1},{129,65},{193,129... | collective-permute-start | bytes 393224 | tf_op jit(solution)/shard_map/ppermute | solution.py:348
  11.3 1.3 broadcast_in_dim.4
  12.6 4.5 %all-to-all-start = ((f32[8,8,128]{2,1,0:T(8,128)}), f32[8,8,128]{2,1,0:T(8,128)S(1)}, u32[]{:S(2)}, u32[]{:S(2)}) async-start(f32[8,8,128]{2,1,0:T(8,128)} %broadcast_in_dim.4), calls=%async_computation | async-start | bytes 65536 | tf_op jit(solution)/shard_map/all_to_all | solution.py:366
  17.1 0.8 reshape.30
  18.1 6.3 %all-to-all-done = f32[8,8,128]{2,1,0:T(8,128)S(1)} async-done(((f32[8,8,128]{2,1,0:T(8,128)}), f32[8,8,128]{2,1,0:T(8,128)S(1)}, u32[]{:S(2)}, u32[]{:S(2)}) %all-to-all-start) | async-done | bytes 32800 | tf_op jit(solution)/shard_map/all_to_all | solution.py:366
  24.6 2.8 %collective-permute-start.4 = (f32[8,8,128]{2,1,0:T(8,128)S(1)}, f32[8,8,128]{2,1,0:T(8,128)S(1)}, u32[]{:S(2)}, u32[]{:S(2)}) collective-permute-start(f32[8,8,128]{2,1,0:T(8,128)S(1)} %all-to-all-done), channel_id=1, source_target_pairs={{0,128},{64,192},{128,0},{192,64},{1,129},{65,193},{129,1},{193,65... | collective-permute-start | bytes 98312 | tf_op jit(solution)/shard_map/ppermute | solution.py:348
  27.4 1.8 %collective-permute-start.5 = (f32[8,8,128]{2,1,0:T(8,128)S(1)}, f32[8,8,128]{2,1,0:T(8,128)S(1)}, u32[]{:S(2)}, u32[]{:S(2)}) collective-permute-start(f32[8,8,128]{2,1,0:T(8,128)S(1)} %all-to-all-done), channel_id=1, source_target_pairs={{0,192},{64,0},{128,64},{192,128},{1,193},{65,1},{129,65},{193,129... | collective-permute-start | bytes 98312 | tf_op jit(solution)/shard_map/ppermute | solution.py:348
  29.2 0.7 broadcast_subtract_fusion
  30.0 0.4 reshape.31
  30.4 1.3 collective-permute-done.4
  31.7 0.1 collective-permute-done.5
  31.8 1.4 collective-permute-start.6
  33.2 2.6 %collective-permute-start.7 = (f32[4,8,8,128]{3,2,1,0:T(8,128)S(1)}, f32[4,8,8,128]{3,2,1,0:T(8,128)S(1)}, u32[]{:S(2)}, u32[]{:S(2)}) collective-permute-start(f32[4,8,8,128]{3,2,1,0:T(8,128)S(1)} %pad_maximum_fusion.3), channel_id=1, source_target_pairs={{0,32},{16,48},{32,0},{48,16},{1,33},{17,49},{33,1},{49,17},{2,34}... | collective-permute-start | bytes 393224 | tf_op jit(solution)/shard_map/ppermute | solution.py:348
  35.8 1.1 collective-permute-start.8
  37.0 2.7 %collective-permute-done.7 = f32[4,8,8,128]{3,2,1,0:T(8,128)S(1)} collective-permute-done((f32[4,8,8,128]{3,2,1,0:T(8,128)S(1)}, f32[4,8,8,128]{3,2,1,0:T(8,128)S(1)}, u32[]{:S(2)}, u32[]{:S(2)}) %collective-permute-start.7) | collective-permute-done | bytes 131104 | tf_op jit(solution)/shard_map/ppermute | solution.py:348
  39.7 0.4 collective-permute-done.8
  40.1 4.0 %collective-permute-start.9 = (f32[4,4,8,8,128]{4,3,2,1,0:T(8,128)S(1)}, f32[4,4,8,8,128]{4,3,2,1,0:T(8,128)S(1)}, u32[]{:S(2)}, u32[]{:S(2)}) collective-permute-start(f32[4,4,8,8,128]{4,3,2,1,0:T(8,128)S(1)} %pad_maximum_fusion.refs_0_), channel_id=1, source_target_pairs={{0,8},{8,0},{1,9},{9,1},{2,10},{10,2},{3,11},{11,3},{4,12},{12,4},... | collective-permute-start | bytes 1572872 | tf_op jit(solution)/shard_map/ppermute | solution.py:348
  44.1 0.6 stack.62.pos
  44.8 0.9 collective-permute-done.9.refs_1_
  45.7 0.8 copy-done.6
  46.5 11.6 %pair_transform.1 = (bf16[8,4,16,256]{3,2,1,0:T(8,128)(2,1)}, bf16[1664,256]{1,0:T(8,128)(2,1)}) custom-call(s32[5]{0:T(128)} %stack.62.pos, f32[4,4,8,8,128]{4,3,2,1,0:T(8,128)} %copy-done.3, f32[4,4,8,8,128]{4,3,2,1,0:T(8,128)} %copy-done.6, f32[256,128]{1,0:T(8,128)} %bitcast.35, f32[256,128]{1,0:T(8,128)} %copy-done.7, f32[256,128]{1,0:T(8,128)} %copy-done.8, ...), custom_call_target="tpu_custom_call" | custom-call | flops 8000000000 | bytes 6291456 | tf_op jit(solution)/shard_map/pair_transform/pallas_call | solution.py:213
  58.0 10.7 %all_to_all.15 = bf16[8,4,16,256]{3,2,1,0:T(8,128)(2,1)S(1)} all-to-all(bf16[8,4,16,256]{3,2,1,0:T(8,128)(2,1)} %get-tuple-element.29), channel_id=1, replica_groups=mesh['zh'=4,'y'=4,'co'=2,'zl'=2,'x'=4] {'y','co'}, dimensions={0} | all-to-all | bytes 524288 | tf_op jit(solution)/shard_map/all_to_all | solution.py:376
  68.8 10.1 %column_pairs.1 = bf16[8,4,16,640]{3,2,1,0:T(8,128)(2,1)} custom-call(s32[5]{0:T(128)} %stack.62.pos, bf16[1664,256]{1,0:T(8,128)(2,1)} %get-tuple-element.28.refs_0_, s32[256,1]{1,0:T(8,128)} %constant.40.clone.refs_10_.refs_1_, s32[8,1,640]{2,1,0:T(1,128)} %constant.41.clone.refs_2_, s32[8,1,640]{2,1,0:T(1,128)} %constant.42.clone.refs_3_), custom_call_target="tpu_custom_call" | custom-call | flops 8000000000 | bytes 2097152 | tf_op jit(solution)/shard_map/column_pairs/pallas_call | solution.py:235
  78.9 4.4 %all-to-all-start.2 = ((bf16[8,4,16,640]{3,2,1,0:T(8,128)(2,1)}), bf16[8,4,16,640]{3,2,1,0:T(8,128)(2,1)S(1)}, u32[]{:S(2)}, u32[]{:S(2)}) async-start(bf16[8,4,16,640]{3,2,1,0:T(8,128)(2,1)} %column_pairs.1), calls=%async_computation.2 | async-start | bytes 1310720 | tf_op jit(solution)/shard_map/all_to_all | solution.py:380
  83.4 2.7 %collective-permute-start.13 = (bf16[2,4,2,4,16,256]{5,4,3,2,1,0:T(8,128)(2,1)S(1)}, bf16[2,4,2,4,16,256]{5,4,3,2,1,0:T(8,128)(2,1)S(1)}, u32[]{:S(2)}, u32[]{:S(2)}) collective-permute-start(bf16[2,4,2,4,16,256]{5,4,3,2,1,0:T(8,128)(2,1)S(1)} %pad_maximum_fusion.1.r0), channel_id=1, source_target_pairs={{0,3},{1,0},{2,1},{3,2},{4,7},{5,4},{6,5},{7,6},{8,11},{9,8},{10,9... | collective-permute-start | bytes 1572872 | tf_op jit(solution)/shard_map/ppermute | solution.py:348
  86.1 5.6 %all-to-all-done.2.mine = bf16[8,4,16,640]{3,2,1,0:T(8,128)(2,1)S(1)} async-done(((bf16[8,4,16,640]{3,2,1,0:T(8,128)(2,1)}), bf16[8,4,16,640]{3,2,1,0:T(8,128)(2,1)S(1)}, u32[]{:S(2)}, u32[]{:S(2)}) %all-to-all-start.2) | async-done | bytes 655392 | tf_op jit(solution)/shard_map/all_to_all | solution.py:380
  91.6 4.3 %collective-permute-start.11 = (bf16[8,4,16,640]{3,2,1,0:T(8,128)(2,1)S(1)}, bf16[8,4,16,640]{3,2,1,0:T(8,128)(2,1)S(1)}, u32[]{:S(2)}, u32[]{:S(2)}) collective-permute-start(bf16[8,4,16,640]{3,2,1,0:T(8,128)(2,1)S(1)} %all-to-all-done.2.mine), channel_id=1, source_target_pairs={{0,8},{8,0},{1,9},{9,1},{2,10},{10,2},{3,11},{11,3},{4,12},{12,4},... | collective-permute-start | bytes 1966088 | tf_op jit(solution)/shard_map/ppermute | solution.py:348
  96.0 7.5 %collective-permute-done.13.r3 = bf16[2,4,2,4,16,256]{5,4,3,2,1,0:T(8,128)(2,1)S(1)} collective-permute-done((bf16[2,4,2,4,16,256]{5,4,3,2,1,0:T(8,128)(2,1)S(1)}, bf16[2,4,2,4,16,256]{5,4,3,2,1,0:T(8,128)(2,1)S(1)}, u32[]{:S(2)}, u32[]{:S(2)}) %collective-permute-start.13) | collective-permute-done | bytes 524320 | tf_op jit(solution)/shard_map/ppermute | solution.py:348
  103.5 2.1 %collective-permute-start.14 = (bf16[1,4,2,4,16,256]{5,4,3,2,1,0:T(8,128)(2,1)S(1)}, bf16[1,4,2,4,16,256]{5,4,3,2,1,0:T(8,128)(2,1)S(1)}, u32[]{:S(2)}, u32[]{:S(2)}) collective-permute-start(bf16[1,4,2,4,16,256]{5,4,3,2,1,0:T(8,128)(2,1)S(1)} %slice.16), channel_id=1, source_target_pairs={{0,3},{1,0},{2,1},{3,2},{4,7},{5,4},{6,5},{7,6},{8,11},{9,8},{10,9... | collective-permute-start | bytes 786440 | tf_op jit(solution)/shard_map/ppermute | solution.py:348
  105.7 0.4 collective-permute-start.16
  106.1 2.4 %collective-permute-start.17 = (bf16[8,4,16,640]{3,2,1,0:T(8,128)(2,1)S(1)}, bf16[8,4,16,640]{3,2,1,0:T(8,128)(2,1)S(1)}, u32[]{:S(2)}, u32[]{:S(2)}) collective-permute-start(bf16[8,4,16,640]{3,2,1,0:T(8,128)(2,1)S(1)} %all-to-all-done.2.mine), channel_id=1, source_target_pairs={{0,48},{16,0},{32,16},{48,32},{1,49},{17,1},{33,17},{49,33},{2,50}... | collective-permute-start | bytes 1966088 | tf_op jit(solution)/shard_map/ppermute | solution.py:348
  108.5 1.7 %collective-permute-done.14 = bf16[1,4,2,4,16,256]{5,4,3,2,1,0:T(8,128)(2,1)S(1)} collective-permute-done((bf16[1,4,2,4,16,256]{5,4,3,2,1,0:T(8,128)(2,1)S(1)}, bf16[1,4,2,4,16,256]{5,4,3,2,1,0:T(8,128)(2,1)S(1)}, u32[]{:S(2)}, u32[]{:S(2)}) %collective-permute-start.14) | collective-permute-done | bytes 262176 | tf_op jit(solution)/shard_map/ppermute | solution.py:348
  110.2 3.2 %collective-permute-done.15 = bf16[1,4,2,4,16,256]{5,4,3,2,1,0:T(8,128)(2,1)S(1)} collective-permute-done((bf16[1,4,2,4,16,256]{5,4,3,2,1,0:T(8,128)(2,1)S(1)}, bf16[1,4,2,4,16,256]{5,4,3,2,1,0:T(8,128)(2,1)S(1)}, u32[]{:S(2)}, u32[]{:S(2)}) %collective-permute-start.15) | collective-permute-done | bytes 262176 | tf_op jit(solution)/shard_map/ppermute | solution.py:348
  113.4 0.8 pad_maximum_fusion.2.r2
  114.3 5.1 %scaled_rows.1 = (bf16[4,1536,1024]{2,1,0:T(8,128)(2,1)S(1)}, bf16[640,1024]{1,0:T(8,128)(2,1)S(1)}, f32[16,1024]{1,0:T(8,128)S(1)}) custom-call(s32[5]{0:T(128)S(1)} %copy-done, f32[6]{0:T(128)S(1)} %copy-done.1, bf16[2,4,2,4,16,256]{5,4,3,2,1,0:T(8,128)(2,1)} %copy-done.2, bf16[2,4,2,4,16,256]{5,4,3,2,1,0:T(8,128)(2,1)} %copy-done.5, ...), custom_call_target="tpu_custom_call" | custom-call | flops 1000000000 | bytes 20971520 | tf_op jit(solution)/shard_map/scaled_rows/pallas_call | solution.py:285
  119.4 5.1 %response_product.4.refs_0_ = f32[6,256,1024]{2,1,0:T(8,128)S(1)} custom-call(bf16[8,4,16,640]{3,2,1,0:T(8,128)(2,1)S(1)} %all-to-all-done.2.mine, bf16[8,4,16,640]{3,2,1,0:T(8,128)(2,1)S(1)} %collective-permute-done.11.theirs, bf16[4,1536,1024]{2,1,0:T(8,128)(2,1)S(1)} %get-tuple-element.33.scaled, bf16[640,1024]{1,0:T(8,128)(2,1)S(1)} %get-tuple-element.34.hot, ...), custom_call_target="tpu_custom_call" | custom-call | flops 4600000000 | bytes 10485760 | tf_op jit(solution)/shard_map/response_product/pallas_call | solution.py:332
  124.5 2.3 %collective-permute-start.22 = (bf16[8,4,16,640]{3,2,1,0:T(8,128)(2,1)S(1)}, bf16[8,4,16,640]{3,2,1,0:T(8,128)(2,1)S(1)}, u32[]{:S(2)}, u32[]{:S(2)}) collective-permute-start(bf16[8,4,16,640]{3,2,1,0:T(8,128)(2,1)S(1)} %collective-permute-done.16.mine), channel_id=1, source_target_pairs={{0,8},{8,0},{1,9},{9,1},{2,10},{10,2},{3,11},{11,3},{4,12},{12,4},... | collective-permute-start | bytes 1966088 | tf_op jit(solution)/shard_map/ppermute | solution.py:348
  126.8 1.2 collective-permute-start.18
  128.0 0.7 collective-permute-start.19
  128.7 0.6 collective-permute-start.21
  129.3 7.2 %collective-permute-done.18 = bf16[4,4,16,640]{3,2,1,0:T(8,128)(2,1)S(1)} collective-permute-done((bf16[4,4,16,640]{3,2,1,0:T(8,128)(2,1)S(1)}, bf16[4,4,16,640]{3,2,1,0:T(8,128)(2,1)S(1)}, u32[]{:S(2)}, u32[]{:S(2)}) %collective-permute-start.18) | collective-permute-done | bytes 327712 | tf_op jit(solution)/shard_map/ppermute | solution.py:348
  136.5 1.9 %collective-permute-done.19 = bf16[4,4,16,640]{3,2,1,0:T(8,128)(2,1)S(1)} collective-permute-done((bf16[4,4,16,640]{3,2,1,0:T(8,128)(2,1)S(1)}, bf16[4,4,16,640]{3,2,1,0:T(8,128)(2,1)S(1)}, u32[]{:S(2)}, u32[]{:S(2)}) %collective-permute-start.19) | collective-permute-done | bytes 327712 | tf_op jit(solution)/shard_map/ppermute | solution.py:348
  138.4 1.2 collective-permute-start.20
  139.6 5.4 %response_product.5.refs_0_ = f32[6,256,1024]{2,1,0:T(8,128)S(1)} custom-call(bf16[8,4,16,640]{3,2,1,0:T(8,128)(2,1)S(1)} %collective-permute-done.16.mine, bf16[8,4,16,640]{3,2,1,0:T(8,128)(2,1)S(1)} %collective-permute-done.22.theirs, bf16[4,1536,1024]{2,1,0:T(8,128)(2,1)S(1)} %get-tuple-element.33.scaled, ...), custom_call_target="tpu_custom_call", output_to_operand_aliasing={{}: (5, {})} | custom-call | flops 4600000000 | bytes 10485760 | tf_op jit(solution)/shard_map/response_product/pallas_call | solution.py:332
  145.0 5.4 %response_product.6.refs_0_ = f32[6,256,1024]{2,1,0:T(8,128)S(1)} custom-call(bf16[8,4,16,640]{3,2,1,0:T(8,128)(2,1)S(1)} %collective-permute-done.17.mine, bf16[8,4,16,640]{3,2,1,0:T(8,128)(2,1)S(1)} %collective-permute-done.21.theirs, bf16[4,1536,1024]{2,1,0:T(8,128)(2,1)S(1)} %get-tuple-element.33.scaled, ...), custom_call_target="tpu_custom_call", output_to_operand_aliasing={{}: (5, {})} | custom-call | flops 4600000000 | bytes 10485760 | tf_op jit(solution)/shard_map/response_product/pallas_call | solution.py:332
  150.4 7.1 %response_product.7 = f32[6,256,1024]{2,1,0:T(8,128)} custom-call(bf16[8,4,16,640]{3,2,1,0:T(8,128)(2,1)S(1)} %constant_dynamic-update-slice_fusion.mine, bf16[8,4,16,640]{3,2,1,0:T(8,128)(2,1)S(1)} %collective-permute-done.20.theirs, bf16[4,1536,1024]{2,1,0:T(8,128)(2,1)S(1)} %get-tuple-element.33.scaled, bf16[640,1024]{1,0:T(8,128)(2,1)S(1)} %get-tuple-element.34.hot, ...), custom_call_target="tpu_custom_call" | custom-call | flops 4600000000 | bytes 10485760 | tf_op jit(solution)/shard_map/response_product/pallas_call | solution.py:332
  (49 shorter events, 0.9 us)
Async XLA Ops:
  0.0 24.4 %collective-permute-start = (f32[256,128]{1,0:T(8,128)}, f32[256,128]{1,0:T(8,128)S(1)}, u32[]{:S(2)}, u32[]{:S(2)}) collective-permute-start(f32[256,128]{1,0:T(8,128)} %bitcast.32), channel_id=1, source_target_pairs={{0,64},{64,128},{128,192},{192,0},{1,65},{65,129},{129,193},{193,1... | collective-permute-start | bytes 393224 | tf_op jit(solution)/shard_map/ppermute | solution.py:348
  3.8 20.6 %collective-permute-start.1 = (f32[256,128]{1,0:T(8,128)}, f32[256,128]{1,0:T(8,128)S(1)}, u32[]{:S(2)}, u32[]{:S(2)}) collective-permute-start(f32[256,128]{1,0:T(8,128)} %bitcast.33), channel_id=1, source_target_pairs={{0,128},{64,192},{128,0},{192,64},{1,129},{65,193},{129,1},{193,65... | collective-permute-start | bytes 393224 | tf_op jit(solution)/shard_map/ppermute | solution.py:348
  8.9 15.5 %collective-permute-start.2 = (f32[256,128]{1,0:T(8,128)}, f32[256,128]{1,0:T(8,128)S(1)}, u32[]{:S(2)}, u32[]{:S(2)}) collective-permute-start(f32[256,128]{1,0:T(8,128)} %bitcast.34), channel_id=1, source_target_pairs={{0,192},{64,0},{128,64},{192,128},{1,193},{65,1},{129,65},{193,129... | collective-permute-start | bytes 393224 | tf_op jit(solution)/shard_map/ppermute | solution.py:348
  12.6 11.8 %all-to-all-start = ((f32[8,8,128]{2,1,0:T(8,128)}), f32[8,8,128]{2,1,0:T(8,128)S(1)}, u32[]{:S(2)}, u32[]{:S(2)}) async-start(f32[8,8,128]{2,1,0:T(8,128)} %broadcast_in_dim.4), calls=%async_computation | async-start | bytes 65536 | tf_op jit(solution)/shard_map/all_to_all | solution.py:366
  24.4 21.2 %copy-start.7 = (f32[256,128]{1,0:T(8,128)}, f32[256,128]{1,0:T(8,128)S(1)}, u32[]{:S(2)}) copy-start(f32[256,128]{1,0:T(8,128)S(1)} %collective-permute-done.refs_3_) | copy-start | bytes 393220
  24.4 21.2 %copy-start.8 = (f32[256,128]{1,0:T(8,128)}, f32[256,128]{1,0:T(8,128)S(1)}, u32[]{:S(2)}) copy-start(f32[256,128]{1,0:T(8,128)S(1)} %collective-permute-done.1.refs_4_) | copy-start | bytes 393220
  24.5 21.2 %copy-start.9 = (f32[256,128]{1,0:T(8,128)}, f32[256,128]{1,0:T(8,128)S(1)}, u32[]{:S(2)}) copy-start(f32[256,128]{1,0:T(8,128)S(1)} %collective-permute-done.2.refs_5_) | copy-start | bytes 393220
  24.5 5.9 %collective-permute-start.3 = (f32[8,8,128]{2,1,0:T(8,128)S(1)}, f32[8,8,128]{2,1,0:T(8,128)S(1)}, u32[]{:S(2)}, u32[]{:S(2)}) collective-permute-start(f32[8,8,128]{2,1,0:T(8,128)S(1)} %all-to-all-done), channel_id=1, source_target_pairs={{0,64},{64,128},{128,192},{192,0},{1,65},{65,129},{129,193},{193,1... | collective-permute-start | bytes 98312 | tf_op jit(solution)/shard_map/ppermute | solution.py:348
  24.6 7.1 %collective-permute-start.4 = (f32[8,8,128]{2,1,0:T(8,128)S(1)}, f32[8,8,128]{2,1,0:T(8,128)S(1)}, u32[]{:S(2)}, u32[]{:S(2)}) collective-permute-start(f32[8,8,128]{2,1,0:T(8,128)S(1)} %all-to-all-done), channel_id=1, source_target_pairs={{0,128},{64,192},{128,0},{192,64},{1,129},{65,193},{129,1},{193,65... | collective-permute-start | bytes 98312 | tf_op jit(solution)/shard_map/ppermute | solution.py:348
  27.4 4.4 %collective-permute-start.5 = (f32[8,8,128]{2,1,0:T(8,128)S(1)}, f32[8,8,128]{2,1,0:T(8,128)S(1)}, u32[]{:S(2)}, u32[]{:S(2)}) collective-permute-start(f32[8,8,128]{2,1,0:T(8,128)S(1)} %all-to-all-done), channel_id=1, source_target_pairs={{0,192},{64,0},{128,64},{192,128},{1,193},{65,1},{129,65},{193,129... | collective-permute-start | bytes 98312 | tf_op jit(solution)/shard_map/ppermute | solution.py:348
  31.8 5.2 %collective-permute-start.6 = (f32[4,8,8,128]{3,2,1,0:T(8,128)S(1)}, f32[4,8,8,128]{3,2,1,0:T(8,128)S(1)}, u32[]{:S(2)}, u32[]{:S(2)}) collective-permute-start(f32[4,8,8,128]{3,2,1,0:T(8,128)S(1)} %pad_maximum_fusion.3), channel_id=1, source_target_pairs={{0,16},{16,32},{32,48},{48,0},{1,17},{17,33},{33,49},{49,1},{2,18}... | collective-permute-start | bytes 393224 | tf_op jit(solution)/shard_map/ppermute | solution.py:348
  33.2 6.5 %collective-permute-start.7 = (f32[4,8,8,128]{3,2,1,0:T(8,128)S(1)}, f32[4,8,8,128]{3,2,1,0:T(8,128)S(1)}, u32[]{:S(2)}, u32[]{:S(2)}) collective-permute-start(f32[4,8,8,128]{3,2,1,0:T(8,128)S(1)} %pad_maximum_fusion.3), channel_id=1, source_target_pairs={{0,32},{16,48},{32,0},{48,16},{1,33},{17,49},{33,1},{49,17},{2,34}... | collective-permute-start | bytes 393224 | tf_op jit(solution)/shard_map/ppermute | solution.py:348
  35.8 4.2 %collective-permute-start.8 = (f32[4,8,8,128]{3,2,1,0:T(8,128)S(1)}, f32[4,8,8,128]{3,2,1,0:T(8,128)S(1)}, u32[]{:S(2)}, u32[]{:S(2)}) collective-permute-start(f32[4,8,8,128]{3,2,1,0:T(8,128)S(1)} %pad_maximum_fusion.3), channel_id=1, source_target_pairs={{0,48},{16,0},{32,16},{48,32},{1,49},{17,1},{33,17},{49,33},{2,50}... | collective-permute-start | bytes 393224 | tf_op jit(solution)/shard_map/ppermute | solution.py:348
  40.1 5.6 %copy-start.3 = (f32[4,4,8,8,128]{4,3,2,1,0:T(8,128)}, f32[4,4,8,8,128]{4,3,2,1,0:T(8,128)S(1)}, u32[]{:S(2)}) copy-start(f32[4,4,8,8,128]{4,3,2,1,0:T(8,128)S(1)} %pad_maximum_fusion.refs_0_) | copy-start | bytes 1572868
  40.1 5.6 %collective-permute-start.9 = (f32[4,4,8,8,128]{4,3,2,1,0:T(8,128)S(1)}, f32[4,4,8,8,128]{4,3,2,1,0:T(8,128)S(1)}, u32[]{:S(2)}, u32[]{:S(2)}) collective-permute-start(f32[4,4,8,8,128]{4,3,2,1,0:T(8,128)S(1)} %pad_maximum_fusion.refs_0_), channel_id=1, source_target_pairs={{0,8},{8,0},{1,9},{9,1},{2,10},{10,2},{3,11},{11,3},{4,12},{12,4},... | collective-permute-start | bytes 1572872 | tf_op jit(solution)/shard_map/ppermute | solution.py:348
  45.7 0.8 copy-start.6
  68.8 10.1 %collective-permute-start.10 = (bf16[8,4,16,256]{3,2,1,0:T(8,128)(2,1)S(1)}, bf16[8,4,16,256]{3,2,1,0:T(8,128)(2,1)S(1)}, u32[]{:S(2)}, u32[]{:S(2)}) collective-permute-start(bf16[8,4,16,256]{3,2,1,0:T(8,128)(2,1)S(1)} %all_to_all.15), channel_id=1, source_target_pairs={{0,4},{4,0},{1,5},{5,1},{2,6},{6,2},{3,7},{7,3},{8,12},{12,8},{9,1... | collective-permute-start | bytes 786440 | tf_op jit(solution)/shard_map/ppermute | solution.py:348
  68.8 45.5 %copy-start = (s32[5]{0:T(128)S(1)}, s32[5]{0:T(128)}, u32[]{:S(2)}) copy-start(s32[5]{0:T(128)} %stack.62.pos) | copy-start | bytes 64
  68.8 45.5 %copy-start.1 = (f32[6]{0:T(128)S(1)}, f32[6]{0:T(128)}, u32[]{:S(2)}) copy-start(f32[6]{0:T(128)} %omega.1) | copy-start | bytes 76
  78.9 35.3 %copy-start.2 = (bf16[2,4,2,4,16,256]{5,4,3,2,1,0:T(8,128)(2,1)}, bf16[2,4,2,4,16,256]{5,4,3,2,1,0:T(8,128)(2,1)S(1)}, u32[]{:S(2)}) copy-start(bf16[2,4,2,4,16,256]{5,4,3,2,1,0:T(8,128)(2,1)S(1)} %pad_maximum_fusion.1.r0) | copy-start | bytes 1572868
  78.9 12.7 %all-to-all-start.2 = ((bf16[8,4,16,640]{3,2,1,0:T(8,128)(2,1)}), bf16[8,4,16,640]{3,2,1,0:T(8,128)(2,1)S(1)}, u32[]{:S(2)}, u32[]{:S(2)}) async-start(bf16[8,4,16,640]{3,2,1,0:T(8,128)(2,1)} %column_pairs.1), calls=%async_computation.2 | async-start | bytes 1310720 | tf_op jit(solution)/shard_map/all_to_all | solution.py:380
  83.4 20.1 %collective-permute-start.13 = (bf16[2,4,2,4,16,256]{5,4,3,2,1,0:T(8,128)(2,1)S(1)}, bf16[2,4,2,4,16,256]{5,4,3,2,1,0:T(8,128)(2,1)S(1)}, u32[]{:S(2)}, u32[]{:S(2)}) collective-permute-start(bf16[2,4,2,4,16,256]{5,4,3,2,1,0:T(8,128)(2,1)S(1)} %pad_maximum_fusion.1.r0), channel_id=1, source_target_pairs={{0,3},{1,0},{2,1},{3,2},{4,7},{5,4},{6,5},{7,6},{8,11},{9,8},{10,9... | collective-permute-start | bytes 1572872 | tf_op jit(solution)/shard_map/ppermute | solution.py:348
  86.1 19.5 %collective-permute-start.12 = (bf16[2,4,2,4,16,256]{5,4,3,2,1,0:T(8,128)(2,1)S(1)}, bf16[2,4,2,4,16,256]{5,4,3,2,1,0:T(8,128)(2,1)S(1)}, u32[]{:S(2)}, u32[]{:S(2)}) collective-permute-start(bf16[2,4,2,4,16,256]{5,4,3,2,1,0:T(8,128)(2,1)S(1)} %pad_maximum_fusion.1.r0), channel_id=1, source_target_pairs={{0,1},{1,2},{2,3},{3,0},{4,5},{5,6},{6,7},{7,4},{8,9},{9,10},{10,1... | collective-permute-start | bytes 1572872 | tf_op jit(solution)/shard_map/ppermute | solution.py:348
  91.6 27.7 %collective-permute-start.11 = (bf16[8,4,16,640]{3,2,1,0:T(8,128)(2,1)S(1)}, bf16[8,4,16,640]{3,2,1,0:T(8,128)(2,1)S(1)}, u32[]{:S(2)}, u32[]{:S(2)}) collective-permute-start(bf16[8,4,16,640]{3,2,1,0:T(8,128)(2,1)S(1)} %all-to-all-done.2.mine), channel_id=1, source_target_pairs={{0,8},{8,0},{1,9},{9,1},{2,10},{10,2},{3,11},{11,3},{4,12},{12,4},... | collective-permute-start | bytes 1966088 | tf_op jit(solution)/shard_map/ppermute | solution.py:348
  103.5 10.8 %copy-start.4 = (bf16[2,4,2,4,16,256]{5,4,3,2,1,0:T(8,128)(2,1)}, bf16[2,4,2,4,16,256]{5,4,3,2,1,0:T(8,128)(2,1)S(1)}, u32[]{:S(2)}) copy-start(bf16[2,4,2,4,16,256]{5,4,3,2,1,0:T(8,128)(2,1)S(1)} %collective-permute-done.13.r3) | copy-start | bytes 1572868
  103.5 6.7 %collective-permute-start.14 = (bf16[1,4,2,4,16,256]{5,4,3,2,1,0:T(8,128)(2,1)S(1)}, bf16[1,4,2,4,16,256]{5,4,3,2,1,0:T(8,128)(2,1)S(1)}, u32[]{:S(2)}, u32[]{:S(2)}) collective-permute-start(bf16[1,4,2,4,16,256]{5,4,3,2,1,0:T(8,128)(2,1)S(1)} %slice.16), channel_id=1, source_target_pairs={{0,3},{1,0},{2,1},{3,2},{4,7},{5,4},{6,5},{7,6},{8,11},{9,8},{10,9... | collective-permute-start | bytes 786440 | tf_op jit(solution)/shard_map/ppermute | solution.py:348
  105.6 8.7 %copy-start.5 = (bf16[2,4,2,4,16,256]{5,4,3,2,1,0:T(8,128)(2,1)}, bf16[2,4,2,4,16,256]{5,4,3,2,1,0:T(8,128)(2,1)S(1)}, u32[]{:S(2)}) copy-start(bf16[2,4,2,4,16,256]{5,4,3,2,1,0:T(8,128)(2,1)S(1)} %collective-permute-done.12.r1) | copy-start | bytes 1572868
  105.6 7.8 %collective-permute-start.15 = (bf16[1,4,2,4,16,256]{5,4,3,2,1,0:T(8,128)(2,1)S(1)}, bf16[1,4,2,4,16,256]{5,4,3,2,1,0:T(8,128)(2,1)S(1)}, u32[]{:S(2)}, u32[]{:S(2)}) collective-permute-start(bf16[1,4,2,4,16,256]{5,4,3,2,1,0:T(8,128)(2,1)S(1)} %slice.17), channel_id=1, source_target_pairs={{0,1},{1,2},{2,3},{3,0},{4,5},{5,6},{6,7},{7,4},{8,9},{9,10},{10,1... | collective-permute-start | bytes 786440 | tf_op jit(solution)/shard_map/ppermute | solution.py:348
  105.7 18.8 %collective-permute-start.16 = (bf16[8,4,16,640]{3,2,1,0:T(8,128)(2,1)S(1)}, bf16[8,4,16,640]{3,2,1,0:T(8,128)(2,1)S(1)}, u32[]{:S(2)}, u32[]{:S(2)}) collective-permute-start(bf16[8,4,16,640]{3,2,1,0:T(8,128)(2,1)S(1)} %all-to-all-done.2.mine), channel_id=1, source_target_pairs={{0,16},{16,32},{32,48},{48,0},{1,17},{17,33},{33,49},{49,1},{2,18}... | collective-permute-start | bytes 1966088 | tf_op jit(solution)/shard_map/ppermute | solution.py:348
  106.1 18.4 %collective-permute-start.17 = (bf16[8,4,16,640]{3,2,1,0:T(8,128)(2,1)S(1)}, bf16[8,4,16,640]{3,2,1,0:T(8,128)(2,1)S(1)}, u32[]{:S(2)}, u32[]{:S(2)}) collective-permute-start(bf16[8,4,16,640]{3,2,1,0:T(8,128)(2,1)S(1)} %all-to-all-done.2.mine), channel_id=1, source_target_pairs={{0,48},{16,0},{32,16},{48,32},{1,49},{17,1},{33,17},{49,33},{2,50}... | collective-permute-start | bytes 1966088 | tf_op jit(solution)/shard_map/ppermute | solution.py:348
  124.5 15.1 %collective-permute-start.22 = (bf16[8,4,16,640]{3,2,1,0:T(8,128)(2,1)S(1)}, bf16[8,4,16,640]{3,2,1,0:T(8,128)(2,1)S(1)}, u32[]{:S(2)}, u32[]{:S(2)}) collective-permute-start(bf16[8,4,16,640]{3,2,1,0:T(8,128)(2,1)S(1)} %collective-permute-done.16.mine), channel_id=1, source_target_pairs={{0,8},{8,0},{1,9},{9,1},{2,10},{10,2},{3,11},{11,3},{4,12},{12,4},... | collective-permute-start | bytes 1966088 | tf_op jit(solution)/shard_map/ppermute | solution.py:348
  126.8 9.6 %collective-permute-start.18 = (bf16[4,4,16,640]{3,2,1,0:T(8,128)(2,1)S(1)}, bf16[4,4,16,640]{3,2,1,0:T(8,128)(2,1)S(1)}, u32[]{:S(2)}, u32[]{:S(2)}) collective-permute-start(bf16[4,4,16,640]{3,2,1,0:T(8,128)(2,1)S(1)} %slice.14), channel_id=1, source_target_pairs={{0,48},{16,0},{32,16},{48,32},{1,49},{17,1},{33,17},{49,33},{2,50}... | collective-permute-start | bytes 983048 | tf_op jit(solution)/shard_map/ppermute | solution.py:348
  128.0 10.3 %collective-permute-start.19 = (bf16[4,4,16,640]{3,2,1,0:T(8,128)(2,1)S(1)}, bf16[4,4,16,640]{3,2,1,0:T(8,128)(2,1)S(1)}, u32[]{:S(2)}, u32[]{:S(2)}) collective-permute-start(bf16[4,4,16,640]{3,2,1,0:T(8,128)(2,1)S(1)} %slice.15), channel_id=1, source_target_pairs={{0,16},{16,32},{32,48},{48,0},{1,17},{17,33},{33,49},{49,1},{2,18}... | collective-permute-start | bytes 983048 | tf_op jit(solution)/shard_map/ppermute | solution.py:348
  128.7 16.3 %collective-permute-start.21 = (bf16[8,4,16,640]{3,2,1,0:T(8,128)(2,1)S(1)}, bf16[8,4,16,640]{3,2,1,0:T(8,128)(2,1)S(1)}, u32[]{:S(2)}, u32[]{:S(2)}) collective-permute-start(bf16[8,4,16,640]{3,2,1,0:T(8,128)(2,1)S(1)} %collective-permute-done.17.mine), channel_id=1, source_target_pairs={{0,8},{8,0},{1,9},{9,1},{2,10},{10,2},{3,11},{11,3},{4,12},{12,4},... | collective-permute-start | bytes 1966088 | tf_op jit(solution)/shard_map/ppermute | solution.py:348
  138.4 12.0 %collective-permute-start.20 = (bf16[8,4,16,640]{3,2,1,0:T(8,128)(2,1)S(1)}, bf16[8,4,16,640]{3,2,1,0:T(8,128)(2,1)S(1)}, u32[]{:S(2)}, u32[]{:S(2)}) collective-permute-start(bf16[8,4,16,640]{3,2,1,0:T(8,128)(2,1)S(1)} %constant_dynamic-update-slice_fusion.mine), channel_id=1, source_target_pairs={{0,8},{8,0},{1,9},{9,1},{2,10},{10,2},{3,11},{11,3},{4,12},{12,4},... | collective-permute-start | bytes 1966088 | tf_op jit(solution)/shard_map/ppermute | solution.py:348
